TPU v7x, 128 devices: a whole 4x4x4 slice. The times are simulated.
128 devices in a mesh: row: 16 (over y, x_lo, core), col: 8 (over z, x_hi).
Axes of the slice: x: 4 (x_hi: 2, x_lo: 2; x = x_hi * 2 + x_lo), y: 4, z: 4, core: 2. Of those that a mesh axis runs over, the one named last changes fastest.
Arguments:
- density: bfloat16 [16384, 16384], P('col', 'row'), may hold values from -0.0625 to 0.0625
- hamiltonian: bfloat16 [16384, 16384], P('row', 'col'), may hold values from -6 to 6
- pattern_p: int32 [128, 128], P('col', 'row'), may hold values 0 or 1
- pattern_h: int32 [128, 128], P('row', 'col'), may hold values 0 or 1
- pattern_s: int32 [16, 128], P('col', 'row'), may hold values 0 or 1
- owner: int32 [8, 16, 16, 1], P('col', 'row'), may hold values from 0 to 7; in each aligned block of 16 rows (0 to 15, 16 to 31, ..., all dimensions but the last counted through in order) at most 4 rows name the same one
- d_intersection: bfloat16 [16, 8, 3, 32, 128, 128], P('row', 'col'), may hold values from -6 to 6
- d_hamilton: bfloat16 [16, 8, 3, 32, 128, 128], P('row', 'col'), may hold values from -6 to 6
Outputs:
- weighted: bfloat16 [2048, 16384], P('col', 'row')
- forces: float32 [16, 8, 3, 32], P('row', 'col')
Inputs may be any that keep to these rules, and one draw needn't show every extreme that they name: Among the 16 blocks of one device no owner is named more than 4 times.
All inputs are finite; a program needn't handle non-finite values. No bound on the sum of `pattern_p` or of `pattern_h` or of `pattern_s` on one device may be relied on, other than what follows from the above.
Results may differ from a plain program's by a relative error of at most 0.0049.
Values may be sent and summed in bfloat16 or wider, within the bound.
No kernel may reach another device: no remote copies, remote signals or barrier semaphores. Data moves between devices by JAX's collectives and lax.ppermute only.
A program may use at most 128 MiB of HBM per device.

v0:
```python
import jax
import jax.numpy as jnp
from jax import lax
from jax.sharding import PartitionSpec as P

BLOCK = 128
CBLK = 8
SBLK = 2


def spread(matrix, pattern):
    rows, cols = matrix.shape
    rb, cb = pattern.shape
    tiles = matrix.reshape(rb, rows // rb, cb, cols // cb) * pattern[:, None, :, None].astype(
        matrix.dtype
    )
    return tiles.reshape(rows, cols)


def as_blocks(matrix):
    tiles = matrix.reshape(SBLK, BLOCK, CBLK, BLOCK).transpose(0, 2, 1, 3)
    return tiles.reshape(SBLK * CBLK, BLOCK * BLOCK)


def local(density, hamiltonian, pattern_p, pattern_h, pattern_s, owner, d_intersection, d_hamilton):
    masked_p = spread(density, pattern_p)
    masked_h = spread(hamiltonian, pattern_h)
    slab = masked_p[: SBLK * BLOCK]
    partial_value = jnp.dot(
        lax.all_gather(slab, "col", axis=0, tiled=True),
        masked_h,
        preferred_element_type=jnp.float32,
    )
    panel = lax.psum(partial_value, "row").astype(jnp.bfloat16)
    product = lax.psum_scatter(
        jnp.dot(panel, masked_p, preferred_element_type=jnp.float32),
        "col",
        scatter_dimension=0,
        tiled=True,
    )
    weighted = spread(product, pattern_s).astype(jnp.bfloat16)
    columns = lax.axis_size("col")
    slot_total = d_intersection.shape[3]
    capacity = slot_total // columns
    target = owner.reshape(SBLK * CBLK)
    onehot = (target[:, None] == jnp.arange(columns, dtype=jnp.int32)[None, :]).astype(jnp.int32)
    before = jnp.cumsum(onehot, axis=0) - onehot
    rank = jnp.sum(before * onehot, axis=1)
    slot_id = target * capacity + rank
    select = (jnp.arange(slot_total, dtype=jnp.int32)[:, None] == slot_id[None, :]).astype(
        jnp.bfloat16
    )
    blocks = jnp.concatenate((as_blocks(weighted), as_blocks(slab)), axis=1)
    outgoing = jnp.dot(select, blocks, preferred_element_type=jnp.float32).astype(jnp.bfloat16)
    width = BLOCK * BLOCK
    dov = d_intersection.reshape(3, slot_total, width)
    dham = d_hamilton.reshape(3, slot_total, width)
    sending = outgoing.reshape(columns, capacity, 2 * width)
    arrived = lax.all_to_all(sending, "col", split_axis=0, concat_axis=0, tiled=True).reshape(
        slot_total, 2, width
    )
    first = jnp.einsum("zsx,sx->zs", dham, arrived[:, 1], preferred_element_type=jnp.float32)
    second = jnp.einsum("zsx,sx->zs", dov, arrived[:, 0], preferred_element_type=jnp.float32)
    forces = (first - second) / BLOCK
    return (weighted, forces.reshape(1, 1, 3, slot_total))


def solution(mesh):
    in_specs = (
        P("col", "row"),
        P("row", "col"),
        P("col", "row"),
        P("row", "col"),
        P("col", "row"),
        P("col", "row", None, None),
        P("row", "col", None, None, None, None),
        P("row", "col", None, None, None, None),
    )
    out_specs = (P("col", "row"), P("row", "col", None, None))
    return jax.shard_map(local, mesh=mesh, in_specs=in_specs, out_specs=out_specs, check_vma=False)
```

profile of v0, /device:TPU:0, one launch (start us, length us, event | category | flops | bytes accessed | tf_op | source)
XLA Modules:
  0.0 645.9 jit_solution(15476653192588457829)
XLA Ops:
  7.2 0.0 all-gather.2.cloned.1.call-start
  7.2 0.7 convert_element_type.25
  7.9 0.1 copy.14
  8.0 0.0 copy-start.4
  8.0 3.3 copy.22
  11.3 0.0 copy-start
  11.3 1.9 copy-done
  13.2 0.1 slice_multiply_fusion
  13.3 0.9 copy.42
  14.2 0.0 all-gather.2.cloned.1.call-update
  14.3 0.0 reduce-scatter.2.cloned.1.call-start
  14.3 0.0 copy-done.4
  14.3 74.1 %all-gather.2.cloned.1.call-done = bf16[2048,1024]{1,0:T(8,128)(2,1)} async-done(((bf16[256,1024]{1,0:T(8,128)(2,1)}), bf16[2048,1024]{1,0:T(8,128)(2,1)}) %all-gather.2.cloned.1.call-update) | async-done | bytes 4194320 | tf_op jit(solution)/shard_map/all_gather | solution.py:30
  88.4 0.0 copy-start.7
  88.4 0.6 mul.47
  89.1 1.6 copy-done.7
  90.6 14.0 %fusion.3 = f32[2048,2048]{1,0:T(8,128)} fusion(bf16[2048,1024]{1,0:T(8,128)(2,1)} %all-gather.2.cloned.1.call-done, bf16[1024,2048]{1,0:T(8,128)(2,1)S(1)} %copy-done.7, bf16[128,8,16,128]{3,2,1,0:T(8,128)(2,1)S(1)} %bitcast.67), kind=kOutput, calls=%fused_computation.6 | convolution fusion | flops 8592031744 | bytes 29360128 | tf_op jit(solution)/shard_map/dot_general | solution.py:29
  104.6 349.1 %all-reduce.1 = bf16[2048,2048]{1,0:T(8,128)(2,1)} all-reduce(f32[2048,2048]{1,0:T(8,128)} %fusion.3), channel_id=1, replica_groups=mesh['row'=16,'col'=8] {'row'}, use_global_device_ids=true, to_apply=%region_0.0 | all-reduce | flops 4194304 | bytes 25165824 | tf_op jit(solution)/shard_map/psum | solution.py:34
  453.8 0.0 copy-start.1
  453.8 0.6 mul.45
  454.4 1.6 copy-done.1
  456.0 13.2 %fusion = f32[2048,1024]{1,0:T(8,128)} fusion(bf16[2048,2048]{1,0:T(8,128)(2,1)} %all-reduce.1, bf16[2048,1024]{1,0:T(8,128)(2,1)S(1)} %copy-done.1, bf16[256,8,8,128]{3,2,1,0:T(8,128)(2,1)S(1)} %bitcast.65), kind=kOutput, calls=%fused_computation.1 | convolution fusion | flops 8592031744 | bytes 25165824 | tf_op jit(solution)/shard_map/dot_general | solution.py:36
  469.1 0.0 copy-start.6
  469.1 0.0 reduce-scatter.2.cloned.1.call-update
  469.2 0.7 copy-done.6
  469.8 0.0 copy-done.5
  469.8 0.1 fusion.14
  469.9 0.2 select_reduce_fusion
  470.1 1.2 fusion.20
  471.3 110.5 %reduce-scatter.2.cloned.1.call-done = f32[256,1024]{1,0:T(8,128)} async-done(((f32[2048,1024]{1,0:T(8,128)}), f32[256,1024]{1,0:T(8,128)}) %reduce-scatter.2.cloned.1.call-update) | async-done | bytes 1048592 | tf_op jit(solution)/shard_map/reduce_scatter | solution.py:35
  581.8 0.1 mul.52
  581.9 1.4 fusion.9
  583.4 0.0 copy-start.3
  583.4 0.1 copy.27
  583.5 0.7 copy-done.3
  584.2 0.7 convolution_convert_fusion
  584.9 2.2 reshape.65
  587.1 3.8 all-to-all-start
  591.0 5.8 reshape.67
  596.8 5.8 reshape.68
  602.6 16.3 %all-to-all-done = bf16[8,4,32768]{2,1,0:T(4,128)(2,1)S(1)} async-done(((bf16[8,4,32768]{2,1,0:T(4,128)(2,1)}), bf16[8,4,32768]{2,1,0:T(4,128)(2,1)S(1)}, u32[]{:S(2)}, u32[]{:S(2)}) %all-to-all-start) | async-done | bytes 2097184 | tf_op jit(solution)/shard_map/all_to_all | solution.py:59
  618.9 3.3 reshape.66
  622.1 8.8 %fusion.7 = f32[32,1,3]{2,1,0:T(1,128)S(1)} fusion(bf16[3,32,16384]{2,1,0:T(8,128)(2,1)} %reshape.67, bf16[32,2,16384]{2,1,0:T(2,128)(2,1)} %reshape.66), kind=kOutput, calls=%fused_computation.10 | convolution fusion | flops 3145728 | bytes 5243264 | tf_op jit(solution)/shard_map/zsx,sx->zs/dot_general | solution.py:62
  631.0 0.1 copy.18
  631.0 0.0 copy-done.2
  631.1 7.3 %fusion.5 = f32[32,1,3]{2,1,0:T(1,128)S(1)} fusion(bf16[3,32,16384]{2,1,0:T(8,128)(2,1)S(1)} %copy-done.2, bf16[32,2,16384]{2,1,0:T(2,128)(2,1)} %reshape.66), kind=kOutput, calls=%fused_computation.8 | convolution fusion | flops 3145728 | bytes 5243264 | tf_op jit(solution)/shard_map/zsx,sx->zs/dot_general | solution.py:63
  638.4 0.1 copy.21
  638.5 0.6 copy.15
  (9 shorter events, 0.1 us)
Async XLA Ops:
  7.2 81.3 %all-gather.2.cloned.1.call-start = ((), (), s32[]{:S(2)}) async-start(), calls=%async_computation.2 | async-start | bytes 4718592 | tf_op jit(solution)/shard_map/all_gather | solution.py:30
  8.0 6.3 copy-start.4
  11.3 1.9 copy-start
  14.3 567.5 %reduce-scatter.2.cloned.1.call-start = ((), (), s32[]{:S(2)}) async-start(), calls=%async_computation.3 | async-start | bytes 9437184 | tf_op jit(solution)/shard_map/reduce_scatter | solution.py:35
  88.4 2.2 copy-start.7
  453.8 2.2 copy-start.1
  469.1 0.7 copy-start.6
  469.1 0.7 copy-start.5
  583.4 0.8 copy-start.3
  587.1 31.7 %all-to-all-start = ((bf16[8,4,32768]{2,1,0:T(4,128)(2,1)}), bf16[8,4,32768]{2,1,0:T(4,128)(2,1)S(1)}, u32[]{:S(2)}, u32[]{:S(2)}) async-start(bf16[8,4,32768]{2,1,0:T(4,128)(2,1)} %reshape.65), calls=%async_computation.1 | async-start | bytes 4194304 | tf_op jit(solution)/shard_map/all_to_all | solution.py:59
  622.1 8.9 %copy-start.2 = (bf16[3,32,16384]{2,1,0:T(8,128)(2,1)S(1)}, bf16[3,32,16384]{2,1,0:T(8,128)(2,1)}, u32[]{:S(2)}) copy-start(bf16[3,32,16384]{2,1,0:T(8,128)(2,1)} %reshape.68) | copy-start | bytes 9437188
Sparse Core Ops, SparseCore 0:
  14.4 74.0 all-gather.1
  469.3 112.4 reduce-scatter.1
where the time goes:
time: 647 us; the launch traced here: 646 us
  blocking collectives  349 us (54%)
  waiting for transfers between devices  201 us (31%)
  matrix products  44 us (7%)
  local copies, waits for them, and re-layouts  30.1 us (5%)
  between operations  14.1 us (2%)
    psum x1, blocking collectives, local(): panel = lax.psum(partial_value, 'row').astype(jnp.bfloat16)  349 us
    reduce_scatter x1, waiting for transfers between devices, local(): lax.psum_scatter(jnp.dot(panel, masked_p, preferred_element_type=jnp.floa...  111 us
    all_gather x1, waiting for transfers between devices, local(): lax.all_gather(slab, 'col', axis=0, tiled=True)  74.1 us
    all_to_all x1, waiting for transfers between devices, local(): lax.all_to_all(sending, 'col', split_axis=0, concat_axis=0, tiled=True)  16.3 us
    dot_general x1, matrix products, local(): jnp.dot(lax.all_gather(slab, 'col', axis=0, tiled=True), masked_h, prefer...  14 us
    dot_general x1, matrix products, local(): jnp.dot(panel, masked_p, preferred_element_type=jnp.float32)  13.2 us
  transfers between devices with their start and end apart: 3, of which 3 were waited for; matrix products, arithmetic and copies ran while one was open for 2% of the time, Pallas kernels for 0%

commit v1 on v0

v1 whole, which is shorter than its diff:
```python
import functools

import jax
import jax.numpy as jnp
from jax import lax
from jax.experimental import pallas as pl
from jax.experimental.pallas import tpu as pltpu
from jax.sharding import Mesh, PartitionSpec as P

BLOCK = 128
CBLK = 8
SBLK = 2
BF = jnp.bfloat16
F32 = jnp.float32
WIRE = jnp.float16
ROW = ("y", "xlo", "core")
COL = ("z", "xhi")
ROW_PAIR = ("y", "xlo")
EARLY = (0, 1, 2, 6)
LATE = (3, 7, 4, 5)
PAD = 16
TOP = 115.0


def exchange(pieces, axes):
    return lax.all_to_all(pieces, axes, split_axis=0, concat_axis=0, tiled=True)


def flip(v, axis):
    return lax.ppermute(v, axis, [(0, 1), (1, 0)])


def gather_direct(piece, axes):
    return exchange(jnp.broadcast_to(piece[None], (CBLK,) + piece.shape), axes)


def shifted(v, k):
    dz, dx = k // 2, k % 2
    nz, nx = lax.axis_size("z"), lax.axis_size("xhi")
    pairs = [
        (z * nx + x, (z + dz) % nz * nx + (x ^ dx)) for z in range(nz) for x in range(nx)
    ]
    return lax.ppermute(v, COL, pairs)


def level_of(peak):
    return jnp.ceil(jnp.log2(jnp.maximum(jnp.max(peak), 2.0**-100))) + 101.0


def encode(padded, peak):
    level = level_of(peak)
    row = lax.broadcasted_iota(jnp.int32, padded.shape, 1)
    rows = padded.shape[1] - PAD
    return jnp.where(row < rows, padded * jnp.exp2(TOP - level), level).astype(WIRE)


def decode_sum(packed):
    rows = packed.shape[1] - PAD
    factor = jnp.exp2(packed[:, rows, 0].astype(F32) - TOP)[:, None, None]
    total = jnp.sum(packed[:, :rows].astype(F32) * factor, axis=0)
    return total, jnp.max(packed[:, rows, 0].astype(F32))


def other_core(v):
    return flip(v, "core")


def mask_body(corner, pattern, src, dst):
    rows, cols = (size // BLOCK for size in src.shape)
    for row in range(rows):
        for col in range(cols):
            at = (slice(row * BLOCK, (row + 1) * BLOCK), slice(col * BLOCK, (col + 1) * BLOCK))
            keep = pattern[corner[0] * rows + row, corner[1] * cols + col] != 0

            @pl.when(keep)
            def _():
                dst[at] = src[at]

            @pl.when(jnp.logical_not(keep))
            def _():
                dst[at] = jnp.zeros((BLOCK, BLOCK), BF)


def slab_body(target, pattern, src, dst):
    rows, cols = src.shape
    mask_body((0, 0), pattern, src, dst.at[:rows])
    lane = lax.broadcasted_iota(jnp.int32, (PAD, cols), 1)
    note = jnp.zeros((PAD, cols), F32)
    for k in range(SBLK * CBLK):
        note = jnp.where(lane == k, target[k].astype(F32), note)
    dst[rows:] = note.astype(BF)


def call_mask(body, scalars, matrix, shape, height, index):
    return pl.pallas_call(
        body,
        out_shape=jax.ShapeDtypeStruct((height, shape[1]), BF),
        grid_spec=pltpu.PrefetchScalarGridSpec(
            num_scalar_prefetch=2,
            grid=(1,),
            in_specs=[pl.BlockSpec(shape, index)],
            out_specs=pl.BlockSpec((height, shape[1]), lambda g, at, pat: (0, 0)),
        ),
        name=body.__name__,
    )(*scalars, matrix)


def mask(matrix, pattern, shape, row, col):
    corner = jnp.stack((jnp.asarray(row, jnp.int32), jnp.asarray(col, jnp.int32)))
    index = lambda g, at, pat: (at[0], at[1])
    return call_mask(mask_body, (corner, pattern), matrix, shape, shape[0], index)


def mask_slab(matrix, pattern, target, shape):
    index = lambda g, at, pat: (0, 0)
    return call_mask(slab_body, (target, pattern), matrix, shape, shape[0] + PAD, index)


def h_dot_body(*refs):
    count = (len(refs) - 4) // 2
    mine, other = refs[:count], refs[count : 2 * count]
    w_mine, w_other, out, peak = refs[2 * count :]
    height = mine[0].shape[0] - PAD
    tops = []
    for at in range(count):
        values = jnp.dot(mine[at][:height], w_mine[...], preferred_element_type=F32)
        values += jnp.dot(other[at][:height], w_other[...], preferred_element_type=F32)
        for g in range(out.shape[0]):
            out[g, at * height : (at + 1) * height] = values[:, g * BLOCK : (g + 1) * BLOCK]
        tops.append(jnp.max(jnp.abs(values), axis=0, keepdims=True))
    for g in range(out.shape[0]):
        out[g, count * height :] = jnp.zeros((PAD, BLOCK), F32)
    peak[0] = jnp.broadcast_to(functools.reduce(jnp.maximum, tops), peak.shape[1:])


def p_dot_body(mine, other, w_mine, w_other, out):
    def flat(tiles):
        return jnp.concatenate([tiles[g] for g in range(CBLK)], axis=1)

    values = jnp.dot(flat(mine), w_mine[...], preferred_element_type=F32)
    values += jnp.dot(flat(other), w_other[...], preferred_element_type=F32)
    out[...] = values


COST = pl.CostEstimate(flops=1 << 20, bytes_accessed=1 << 20, transcendentals=0)
ROOM = pltpu.CompilerParams(vmem_limit_bytes=58 << 20)


def dot_specs(operands, width):
    whole = [pl.BlockSpec(v.shape, lambda n, rank=v.ndim: (0,) * rank) for v in operands]
    return whole + [pl.BlockSpec((width, 2 * BLOCK), lambda n: (0, n))] * 2


def h_dot(mine, other, w_mine, w_other):
    width = w_mine.shape[0]
    tile = 2 * BLOCK
    steps = width // tile
    return pl.pallas_call(
        h_dot_body,
        out_shape=(
            jax.ShapeDtypeStruct((CBLK, width + PAD, BLOCK), F32),
            jax.ShapeDtypeStruct((steps, 8, tile), F32),
        ),
        grid=(steps,),
        in_specs=dot_specs(mine + other, width),
        out_specs=(
            pl.BlockSpec((2, width + PAD, BLOCK), lambda n: (n, 0, 0)),
            pl.BlockSpec((1, 8, tile), lambda n: (n, 0, 0)),
        ),
        cost_estimate=COST,
        compiler_params=ROOM,
        name="h_dot",
    )(*mine, *other, w_mine, w_other)


def p_dot(mine, other, w_mine, w_other):
    width = w_mine.shape[0]
    tile = 2 * BLOCK
    return pl.pallas_call(
        p_dot_body,
        out_shape=jax.ShapeDtypeStruct((width, width), F32),
        grid=(width // tile,),
        in_specs=dot_specs((mine, other), width),
        out_specs=pl.BlockSpec((width, tile), lambda n: (0, n)),
        cost_estimate=COST,
        compiler_params=ROOM,
        name="p_dot",
    )(mine, other, w_mine, w_other)


def collect_body(source, base, *refs):
    pieces, out = refs[:-1], refs[-1]
    room = source.shape[1]
    for k, blocks in enumerate(pieces):
        for q in range(room):
            b = source[k, q]
            safe = jnp.maximum(b, 0)
            rows = pl.ds(pl.multiple_of((safe // CBLK) * BLOCK, BLOCK), BLOCK)
            cols = pl.ds(pl.multiple_of((safe % CBLK) * BLOCK, BLOCK), BLOCK)
            value = blocks[rows, cols]
            out[base[k] * room + q] = jnp.where(b >= 0, value, jnp.zeros_like(value))


def collect(pieces, source, base):
    scalar = pl.BlockSpec(memory_space=pltpu.SMEM)
    whole = pl.BlockSpec(memory_space=pltpu.VMEM)
    slots = source.shape[0] * source.shape[1]
    return pl.pallas_call(
        collect_body,
        out_shape=jax.ShapeDtypeStruct((slots, BLOCK, BLOCK), BF),
        in_specs=[scalar, scalar] + [whole] * len(pieces),
        out_specs=whole,
        compiler_params=pltpu.CompilerParams(vmem_limit_bytes=24 << 20),
        name="collect",
    )(source, base, *pieces)


def pick_body(source, blocks, out):
    for slot in range(out.shape[0]):
        k = source[slot]
        safe = jnp.maximum(k, 0)
        rows = pl.ds(pl.multiple_of((safe // CBLK) * BLOCK, BLOCK), BLOCK)
        cols = pl.ds(pl.multiple_of((safe % CBLK) * BLOCK, BLOCK), BLOCK)
        value = blocks[rows, cols]
        out[slot] = jnp.where(k >= 0, value, jnp.zeros_like(value))


def pick(blocks, source):
    slots = source.shape[0]
    return pl.pallas_call(
        pick_body,
        out_shape=jax.ShapeDtypeStruct((slots, BLOCK, BLOCK), BF),
        in_specs=[
            pl.BlockSpec(memory_space=pltpu.SMEM),
            pl.BlockSpec(memory_space=pltpu.VMEM),
        ],
        out_specs=pl.BlockSpec(memory_space=pltpu.VMEM),
        name="pick",
    )(source, blocks)


def routing(target, columns, capacity):
    count = target.shape[0]
    onehot = (target[:, None] == jnp.arange(columns, dtype=jnp.int32)[None, :]).astype(jnp.int32)
    place = jnp.arange(count, dtype=jnp.int32)
    earlier = (place[None, :] < place[:, None]).astype(jnp.int32)
    rank = jnp.sum(earlier * (target[None, :] == target[:, None]), axis=1)
    hit = (rank[:, None, None] == jnp.arange(capacity, dtype=jnp.int32)) & (onehot[:, :, None] > 0)
    return jnp.sum(jnp.where(hit, place[:, None, None] + 1, 0), axis=0) - 1


def pair_sums(derivative, blocks):
    return jnp.sum(derivative.astype(F32) * blocks.astype(F32)[None], axis=(2, 3))


def local(density, hamiltonian, pattern_p, pattern_h, pattern_s, owner, d_intersection, d_hamilton):
    core = lax.axis_index("core")
    columns = lax.axis_size(COL)
    slot_total = d_intersection.shape[3]
    width = CBLK * BLOCK

    capacity = slot_total // columns
    target = owner.reshape(SBLK * CBLK)
    source = routing(target, columns, capacity).reshape(slot_total)
    d_over = d_intersection.reshape(d_intersection.shape[2:])
    d_ham = d_hamilton.reshape(d_hamilton.shape[2:])

    def route(blocks):
        return exchange(pick(blocks, source), COL)

    slab = mask_slab(density, pattern_p[:SBLK], target, (SBLK * BLOCK, width))
    up, down = ([(i, (i + d) % 4) for i in range(4)] for d in (1, -1))
    barrier = lax.optimization_barrier
    height = SBLK * BLOCK
    side = flip(slab, "xhi")
    up_own = lax.ppermute(slab, "z", up)
    down_own = lax.ppermute(slab, "z", down)
    h_mine = mask(hamiltonian, pattern_h, (width, width), 0, core)
    h_sent = mask(hamiltonian, pattern_h, (width, width), 0, 1 - core)
    side, up_own, down_own, h_mine, h_sent = barrier((side, up_own, down_own, h_mine, h_sent))
    h_other = other_core(h_sent)
    down_side = lax.ppermute(side, "z", down)
    up_two = lax.ppermute(up_own, "z", up)
    up_side = lax.ppermute(side, "z", up)
    pieces = [slab, side, down_own, down_side, up_two, None, up_own, up_side]

    def partial_w(tiles, p_mine, p_other):
        part = p_dot(tiles, other_core(tiles), p_mine, p_other)
        blocks = [part[at * height : (at + 1) * height] for at in range(len(EARLY))]
        return blocks[0], [(v * scale).astype(WIRE) for v in blocks]

    mine = [pieces[k] for k in EARLY]
    others, down_side = barrier(([other_core(v) for v in mine], down_side))
    pieces[3] = down_side
    pieces[5] = lax.ppermute(down_side, "z", down)
    partial, peak = h_dot(mine, others, h_mine, h_other)
    packed, late, density = barrier(
        (encode(partial, peak), [pieces[k] for k in LATE], density)
    )
    for k, piece in zip(LATE, late):
        pieces[k] = piece
    mine = [pieces[k] for k in LATE]
    packed_late = encode(*h_dot(mine, [other_core(v) for v in mine], h_mine, h_other))
    arrived, packed_late = barrier((exchange(packed, ROW_PAIR), packed_late))
    arrived_late = exchange(packed_late, ROW_PAIR)
    panel, level = decode_sum(arrived)
    panel = panel.astype(BF)
    copies = jnp.broadcast_to(panel[None], (CBLK,) + panel.shape)
    keep = jnp.repeat(jnp.repeat(pattern_s, BLOCK, axis=0), BLOCK, axis=1).astype(F32)
    p_mine = mask(density, pattern_p, (width, width), core, 0)
    p_other = mask(density, pattern_p, (width, width), 1 - core, 0)
    most_p = jnp.max(jnp.abs(density)).astype(F32)
    copies, arrived_late, p_mine, p_other, keep, most_p = barrier(
        (copies, arrived_late, p_mine, p_other, keep, most_p)
    )
    panel_late, level_late = decode_sum(arrived_late)
    panel_late = panel_late.astype(BF)
    copies_late = jnp.broadcast_to(panel_late[None], (CBLK,) + panel_late.shape)
    room = jnp.ceil(jnp.log2(jnp.maximum(most_p, 2.0**-100))) + 14.0
    room = jnp.full((8, BLOCK), room + jnp.maximum(level, level_late), F32)
    two = [(i, (i + 2) % 4) for i in range(4)]
    room = jnp.maximum(room, other_core(room))
    room = jnp.maximum(room, lax.ppermute(room, "z", two))
    room = jnp.maximum(room, lax.ppermute(room, "z", up))
    room = jnp.max(jnp.maximum(room, flip(room, "xhi"))) - 101.0
    tiles, copies_late, room = barrier((exchange(copies, ROW_PAIR), copies_late, room))
    tiles_late = exchange(copies_late, ROW_PAIR)
    scale, unscale = jnp.exp2(14.0 - room), jnp.exp2(room - 14.0)

    early, wire = partial_w(tiles, p_mine, p_other)
    wire, tiles_late = barrier((wire, tiles_late))
    _, wire_late = partial_w(tiles_late, p_mine, p_other)
    total = early
    for part, chosen in ((wire, EARLY), (wire_late, LATE)):
        for v, k in zip(part, chosen):
            if k:
                total = total + shifted(v, k).astype(F32) * unscale
        if k == EARLY[-1]:
            total = barrier(total)
    weighted = (total * keep).astype(BF)

    z, xhi = lax.axis_index("z"), lax.axis_index("xhi")
    step = jnp.arange(CBLK, dtype=jnp.int32)
    base = ((z + step // 2) % 4) * 2 + (xhi ^ (step % 2))
    owners = jnp.stack([p[height, : SBLK * CBLK] for p in pieces]).astype(jnp.int32)
    me = z * 2 + xhi
    found = jax.vmap(lambda t: routing(t, columns, capacity))(owners)
    mine = jnp.sum(jnp.where(jnp.arange(columns)[None, :, None] == me, found, 0), axis=1)
    routed_slab = collect(pieces, mine, base)

    first = pair_sums(d_ham, routed_slab)
    second = pair_sums(d_over, route(weighted))
    forces = (first - second) / BLOCK
    return weighted, forces.reshape((1, 1) + forces.shape)


def solution(mesh):
    fine = Mesh(mesh.devices.reshape(4, 2, 2, 4, 2), ROW + COL)
    in_specs = (
        P(COL, ROW),
        P(ROW, COL),
        P(COL, ROW),
        P(ROW, COL),
        P(COL, ROW),
        P(COL, ROW, None, None),
        P(ROW, COL, None, None, None, None),
        P(ROW, COL, None, None, None, None),
    )
    out_specs = (P(COL, ROW), P(ROW, COL, None, None))
    return jax.shard_map(local, mesh=fine, in_specs=in_specs, out_specs=out_specs, check_vma=False)
```

time: 647 us -> 279 us (0.43)
  blocking collectives: 349 us -> 0 us
  waiting for transfers between devices: 201 us -> 98.7 us
  Pallas kernels: 0 us -> 63.2 us
  starting transfers between devices: 3.9 us -> 58.1 us
  matrix products: 44 us -> 0 us
  other arithmetic: 3.7 us -> 38.7 us
  local copies, waits for them, and re-layouts: 30.1 us -> 13.2 us
  between operations: 14.1 us -> 5.4 us
    psum x1 -> x0, blocking collectives: 349 us -> none  [local(): panel = lax.psum(partial_value, 'row').astype(jnp.bfloat16)]
    reduce_scatter x1 -> x0, waiting for transfers between devices: 111 us -> none  [local(): lax.psum_scatter(jnp.dot(panel, masked_p, preferred_element_type=jnp.floa...]
    all_gather x1 -> x0, waiting for transfers between devices: 74.1 us -> none  [local(): lax.all_gather(slab, 'col', axis=0, tiled=True)]
    pallas_call x0 -> x11, Pallas kernels: none -> 63.2 us  [the longest x5 23.1 us: call_mask(): pl.pallas_call(body, out_shape=jax.ShapeDtypeStruct((height, shape[1]), B...]
    ppermute x0 -> x29, waiting for transfers between devices: none -> 60.1 us  [the longest x7 27 us: shifted(): return lax.ppermute(v, COL, pairs)]
    dot_general x5 -> x0, matrix products: 44 us -> none  [the longest x1 14 us: local(): jnp.dot(lax.all_gather(slab, 'col', axis=0, tiled=True), masked_h, prefer...]
    ppermute x0 -> x29, starting transfers between devices: none -> 37 us  [the longest x7 15.5 us: shifted(): return lax.ppermute(v, COL, pairs)]
    all_to_all x1 -> x5, waiting for transfers between devices: 16.3 us -> 38.6 us  [exchange(): return lax.all_to_all(pieces, axes, split_axis=0, concat_axis=0, tiled=True)]
  transfers between devices with their start and end apart: 3 -> 34, of which waited for: 3 -> 21; matrix products, arithmetic and copies ran while one was open for 2% -> 13% of each run, Pallas kernels for 0% -> 21%
where the time goes in v1:
time: 279 us; the launch traced here: 277 us
  waiting for transfers between devices  98.7 us (35%)
  Pallas kernels  63.2 us (23%)
  starting transfers between devices  58.1 us (21%)
  other arithmetic  38.7 us (14%)
  local copies, waits for them, and re-layouts  13.2 us (5%)
  between operations  5.4 us (2%)
    all_to_all x5, waiting for transfers between devices, exchange(): return lax.all_to_all(pieces, axes, split_axis=0, concat_axis=0, tiled=True)  38.6 us
    ppermute x7, waiting for transfers between devices, shifted(): return lax.ppermute(v, COL, pairs)  27 us
    pallas_call x5, Pallas kernels, call_mask(): pl.pallas_call(body, out_shape=jax.ShapeDtypeStruct((height, shape[1]), B...  23.1 us
    all_to_all x5, starting transfers between devices, exchange(): return lax.all_to_all(pieces, axes, split_axis=0, concat_axis=0, tiled=True)  21 us
    pallas_call x2, Pallas kernels, p_dot(): pl.pallas_call(p_dot_body, out_shape=jax.ShapeDtypeStruct((width, width),...  18.2 us
    pallas_call x2, Pallas kernels, h_dot(): pl.pallas_call(h_dot_body, out_shape=(jax.ShapeDtypeStruct((CBLK, width +...  18.1 us
    ppermute x7, starting transfers between devices, shifted(): return lax.ppermute(v, COL, pairs)  15.5 us
    ppermute x14, waiting for transfers between devices, flip(): return lax.ppermute(v, axis, [(0, 1), (1, 0)])  14.3 us
  transfers between devices with their start and end apart: 34, of which 21 were waited for; matrix products, arithmetic and copies ran while one was open for 13% of the time, Pallas kernels for 21%

profile of v1, /device:TPU:0, one launch (start us, length us, event | category | flops | bytes accessed | tf_op | source)
XLA Modules:
  0.0 277.2 jit_solution(10815634448001322166)
XLA Ops:
  2.0 2.8 %slab_body.1.refs_0_ = bf16[272,1024]{1,0:T(8,128)(2,1)} custom-call(s32[16]{0:T(128)} %bitcast.19, s32[2,8]{1,0:T(2,128)} %slice.86.pattern, bf16[2048,1024]{1,0:T(8,128)(2,1)} %src.7), custom_call_target="tpu_custom_call" | custom-call | tf_op jit(solution)/shard_map/slab_body/pallas_call | solution.py:95
  4.7 3.1 %collective-permute-start = (bf16[272,1024]{1,0:T(8,128)(2,1)}, bf16[272,1024]{1,0:T(8,128)(2,1)S(1)}, u32[]{:S(2)}, u32[]{:S(2)}) collective-permute-start(bf16[272,1024]{1,0:T(8,128)(2,1)} %slab_body.1.refs_0_), channel_id=1, source_target_pairs={{0,1},{1,0},{2,3},{3,2},{4,5},{5,4},{6,7},{7,6},{8,9},{9,8},{10,11... | collective-permute-start | bytes 1671176 | tf_op jit(solution)/shard_map/ppermute | solution.py:30
  7.9 1.9 collective-permute-start.1
  9.8 2.1 collective-permute-start.2
  12.5 5.0 %mask_body.4.refs_8_ = bf16[1024,1024]{1,0:T(8,128)(2,1)} custom-call(s32[2]{0:T(128)} %get-tuple-element.90.corner, s32[8,16]{1,0:T(8,128)} %pattern.5, bf16[1024,2048]{1,0:T(8,128)(2,1)} %src.5), custom_call_target="tpu_custom_call" | custom-call | tf_op jit(solution)/shard_map/mask_body/pallas_call | solution.py:95
  17.5 5.2 %mask_body.5 = bf16[1024,1024]{1,0:T(8,128)(2,1)} custom-call(s32[2]{0:T(128)} %get-tuple-element.89.corner, s32[8,16]{1,0:T(8,128)} %pattern.5, bf16[1024,2048]{1,0:T(8,128)(2,1)} %src.5), custom_call_target="tpu_custom_call" | custom-call | tf_op jit(solution)/shard_map/mask_body/pallas_call | solution.py:95
  22.6 1.8 collective-permute-done.1.refs_3_.refs_6_
  25.2 2.8 %collective-permute-start.7 = (bf16[272,1024]{1,0:T(8,128)(2,1)S(1)}, bf16[272,1024]{1,0:T(8,128)(2,1)S(1)}, u32[]{:S(2)}, u32[]{:S(2)}) collective-permute-start(bf16[272,1024]{1,0:T(8,128)(2,1)S(1)} %collective-permute-done.refs_1_), channel_id=1, source_target_pairs={{0,6},{2,0},{4,2},{6,4},{1,7},{3,1},{5,3},{7,5},{8,14},{10,8},{12,... | collective-permute-start | bytes 1671176 | tf_op jit(solution)/shard_map/ppermute | solution.py:282
  31.1 9.4 %collective-permute-done.7.refs_0_.refs_3_ = bf16[272,1024]{1,0:T(8,128)(2,1)S(1)} collective-permute-done((bf16[272,1024]{1,0:T(8,128)(2,1)S(1)}, bf16[272,1024]{1,0:T(8,128)(2,1)S(1)}, u32[]{:S(2)}, u32[]{:S(2)}) %collective-permute-start.7) | collective-permute-done | bytes 557088 | tf_op jit(solution)/shard_map/ppermute | solution.py:282
  41.3 3.0 %collective-permute-start.11 = (bf16[272,1024]{1,0:T(8,128)(2,1)S(1)}, bf16[272,1024]{1,0:T(8,128)(2,1)}, u32[]{:S(2)}, u32[]{:S(2)}) collective-permute-start(bf16[272,1024]{1,0:T(8,128)(2,1)S(1)} %collective-permute-done.7.refs_0_.refs_3_), channel_id=1, source_target_pairs={{0,6},{2,0},{4,2},{6,4},{1,7},{3,1},{5,3},{7,5},{8,14},{10,8},{12,... | collective-permute-start | bytes 1671176 | tf_op jit(solution)/shard_map/ppermute | solution.py:295
  45.7 9.1 %h_dot.2 = (f32[8,1040,128]{2,1,0:T(8,128)}, f32[4,8,256]{2,1,0:T(8,128)}) custom-call(bf16[272,1024]{1,0:T(8,128)(2,1)} %slab_body.1.refs_0_, bf16[272,1024]{1,0:T(8,128)(2,1)} %copy-done.2, bf16[272,1024]{1,0:T(8,128)(2,1)} %copy-done.6, bf16[272,1024]{1,0:T(8,128)(2,1)} %copy-done.4, bf16[272,1024]{1,0:T(8,128)(2,1)} %copy-done.19, ...), custom_call_target="tpu_custom_call" | custom-call | flops 1048576 | bytes 1048576 | tf_op jit(solution)/shard_map/h_dot/pallas_call | solution.py:158
  57.0 4.1 %select_convert_fusion.1 = f16[8,1040,128]{2,1,0:T(8,128)(2,1)} fusion(f32[8,1040,128]{2,1,0:T(8,128)} %get-tuple-element.46, f32[]{:T(128)S(6)} %add.78, f32[]{:T(128)S(6)} %exp2.41, pred[1040]{0:T(1024)(128)(4,1)S(1)} %iota_compare_fusion.3), kind=kLoop, calls=%fused_computation.5 | loop fusion | flops 3194880 | bytes 6390808 | tf_op jit(solution)/shard_map/convert_element_type | solution.py:54
  61.2 4.5 %all-to-all-start = ((f16[8,1040,128]{2,1,0:T(8,128)(2,1)}), f16[8,1040,128]{2,1,0:T(8,128)(2,1)}, u32[]{:S(2)}, u32[]{:S(2)}) async-start(f16[8,1040,128]{2,1,0:T(8,128)(2,1)} %select_convert_fusion.1), calls=%async_computation | async-start | bytes 4259840 | tf_op jit(solution)/shard_map/all_to_all | solution.py:26
  67.7 1.6 collective-permute-done.13.refs_5_
  71.7 9.0 %h_dot.3 = (f32[8,1040,128]{2,1,0:T(8,128)}, f32[4,8,256]{2,1,0:T(8,128)}) custom-call(bf16[272,1024]{1,0:T(8,128)(2,1)} %copy-done.8, bf16[272,1024]{1,0:T(8,128)(2,1)} %copy-done.10, bf16[272,1024]{1,0:T(8,128)(2,1)} %copy-done.12, bf16[272,1024]{1,0:T(8,128)(2,1)} %collective-permute-done.11.refs_3_.refs_5_, bf16[272,1024]{1,0:T(8,128)(2,1)} %copy-done.23, ...), custom_call_target="tpu_custom_call" | custom-call | flops 1048576 | bytes 1048576 | tf_op jit(solution)/shard_map/h_dot/pallas_call | solution.py:158
  83.0 4.1 %select_convert_fusion = f16[8,1040,128]{2,1,0:T(8,128)(2,1)} fusion(f32[8,1040,128]{2,1,0:T(8,128)} %get-tuple-element.54, f32[]{:T(128)S(6)} %add.79, f32[]{:T(128)S(6)} %exp2.43, pred[1040]{0:T(1024)(128)(4,1)S(1)} %iota_compare_fusion.3), kind=kLoop, calls=%fused_computation.4 | loop fusion | flops 3194880 | bytes 6390808 | tf_op jit(solution)/shard_map/convert_element_type | solution.py:54
  87.1 5.6 %all-to-all-done = f16[8,1040,128]{2,1,0:T(8,128)(2,1)} async-done(((f16[8,1040,128]{2,1,0:T(8,128)(2,1)}), f16[8,1040,128]{2,1,0:T(8,128)(2,1)}, u32[]{:S(2)}, u32[]{:S(2)}) %all-to-all-start) | async-done | bytes 2129952 | tf_op jit(solution)/shard_map/all_to_all | solution.py:26
  92.7 3.8 %all-to-all-start.1 = ((f16[8,1040,128]{2,1,0:T(8,128)(2,1)}), f16[8,1040,128]{2,1,0:T(8,128)(2,1)S(1)}, u32[]{:S(2)}, u32[]{:S(2)}) async-start(f16[8,1040,128]{2,1,0:T(8,128)(2,1)} %select_convert_fusion), calls=%async_computation.1 | async-start | bytes 4259840 | tf_op jit(solution)/shard_map/all_to_all | solution.py:26
  98.7 5.1 %mask_body.6.w_mine = bf16[1024,1024]{1,0:T(8,128)(2,1)} custom-call(s32[2]{0:T(128)} %get-tuple-element.92.corner, s32[16,8]{1,0:T(8,128)} %copy-done.27, bf16[2048,1024]{1,0:T(8,128)(2,1)} %src.7), custom_call_target="tpu_custom_call" | custom-call | tf_op jit(solution)/shard_map/mask_body/pallas_call | solution.py:95
  103.8 5.0 %mask_body.7.w_other = bf16[1024,1024]{1,0:T(8,128)(2,1)} custom-call(s32[2]{0:T(128)} %get-tuple-element.91.corner, s32[16,8]{1,0:T(8,128)} %copy-done.27, bf16[2048,1024]{1,0:T(8,128)(2,1)} %src.7), custom_call_target="tpu_custom_call" | custom-call | tf_op jit(solution)/shard_map/mask_body/pallas_call | solution.py:95
  108.9 3.8 %abs_reduce_fusion = bf16[]{:T(256)} fusion(bf16[2048,1024]{1,0:T(8,128)(2,1)} %src.7), kind=kLoop, calls=%fused_computation.7 | loop fusion | flops 4194303 | bytes 4194306 | tf_op jit(solution)/shard_map/reduce_max | solution.py:312
  114.7 2.1 multiply_reduce_fusion.1
  116.8 6.1 %all-to-all-done.1 = f16[8,1040,128]{2,1,0:T(8,128)(2,1)S(1)} async-done(((f16[8,1040,128]{2,1,0:T(8,128)(2,1)}), f16[8,1040,128]{2,1,0:T(8,128)(2,1)S(1)}, u32[]{:S(2)}, u32[]{:S(2)}) %all-to-all-start.1) | async-done | bytes 2129952 | tf_op jit(solution)/shard_map/all_to_all | solution.py:26
  124.4 4.3 %all-to-all-start.2 = ((bf16[8,1024,128]{2,1,0:T(8,128)(2,1)}), bf16[8,1024,128]{2,1,0:T(8,128)(2,1)}, u32[]{:S(2)}, u32[]{:S(2)}) async-start(bf16[8,1024,128]{2,1,0:T(8,128)(2,1)} %broadcast_in_dim.51), calls=%async_computation.2 | async-start | bytes 4194304 | tf_op jit(solution)/shard_map/all_to_all | solution.py:26
  132.0 2.3 collective-permute-start.17
  134.4 2.8 %collective-permute-done.17 = f32[8,128]{1,0:T(8,128)S(1)} collective-permute-done((f32[8,128]{1,0:T(8,128)S(1)}, f32[8,128]{1,0:T(8,128)S(1)}, u32[]{:S(2)}, u32[]{:S(2)}) %collective-permute-start.17) | collective-permute-done | bytes 4128 | tf_op jit(solution)/shard_map/ppermute | solution.py:323
  137.1 4.8 %collective-permute-done.18 = f32[8,128]{1,0:T(8,128)S(1)} collective-permute-done((f32[8,128]{1,0:T(8,128)S(1)}, f32[8,128]{1,0:T(8,128)S(1)}, u32[]{:S(2)}, u32[]{:S(2)}) %collective-permute-start.18) | collective-permute-done | bytes 4128 | tf_op jit(solution)/shard_map/ppermute | solution.py:324
  142.0 2.0 collective-permute-start.19
  144.4 8.1 %collective-permute-done.19 = f32[8,128]{1,0:T(8,128)S(1)} collective-permute-done((f32[8,128]{1,0:T(8,128)S(1)}, f32[8,128]{1,0:T(8,128)S(1)}, u32[]{:S(2)}, u32[]{:S(2)}) %collective-permute-start.19) | collective-permute-done | bytes 4128 | tf_op jit(solution)/shard_map/ppermute | solution.py:30
  154.4 1.6 broadcast_in_dim.58
  156.0 4.1 %all-to-all-start.3 = ((bf16[8,1024,128]{2,1,0:T(8,128)(2,1)}), bf16[8,1024,128]{2,1,0:T(8,128)(2,1)S(1)}, u32[]{:S(2)}, u32[]{:S(2)}) async-start(bf16[8,1024,128]{2,1,0:T(8,128)(2,1)} %broadcast_in_dim.58), calls=%async_computation.3 | async-start | bytes 4194304 | tf_op jit(solution)/shard_map/all_to_all | solution.py:26
  160.5 9.1 %p_dot.2 = f32[1024,1024]{1,0:T(8,128)} custom-call(bf16[8,1024,128]{2,1,0:T(8,128)(2,1)} %all-to-all-done.2.mine, bf16[8,1024,128]{2,1,0:T(8,128)(2,1)} %collective-permute-done.20.other, bf16[1024,1024]{1,0:T(8,128)(2,1)} %mask_body.6.w_mine, bf16[1024,1024]{1,0:T(8,128)(2,1)} %mask_body.7.w_other), custom_call_target="tpu_custom_call" | custom-call | flops 1048576 | bytes 1048576 | tf_op jit(solution)/shard_map/p_dot/pallas_call | solution.py:179
  169.6 3.3 %fusion.6 = (f16[256,1024]{1,0:T(8,128)(2,1)}, f16[256,1024]{1,0:T(8,128)(2,1)}, f16[256,1024]{1,0:T(8,128)(2,1)}) fusion(f32[1024,1024]{1,0:T(8,128)} %p_dot.2, f32[]{:T(128)S(6)} %exp2.49), kind=kLoop, calls=%fused_computation.19 | loop fusion | flops 1572864 | bytes 4718596 | tf_op jit(solution)/shard_map/convert_element_type | solution.py:290
  172.9 14.9 %all-to-all-done.3.mine = bf16[8,1024,128]{2,1,0:T(8,128)(2,1)S(1)} async-done(((bf16[8,1024,128]{2,1,0:T(8,128)(2,1)}), bf16[8,1024,128]{2,1,0:T(8,128)(2,1)S(1)}, u32[]{:S(2)}, u32[]{:S(2)}) %all-to-all-start.3) | async-done | bytes 2097184 | tf_op jit(solution)/shard_map/all_to_all | solution.py:26
  189.0 2.8 %collective-permute-start.21 = (f16[256,1024]{1,0:T(8,128)(2,1)}, f16[256,1024]{1,0:T(8,128)(2,1)}, u32[]{:S(2)}, u32[]{:S(2)}) collective-permute-start(f16[256,1024]{1,0:T(8,128)(2,1)} %get-tuple-element.67), channel_id=1, source_target_pairs={{0,1},{1,0},{2,3},{3,2},{4,5},{5,4},{6,7},{7,6},{8,9},{9,8},{10,11... | collective-permute-start | bytes 1572872 | tf_op jit(solution)/shard_map/ppermute | solution.py:43
  191.8 3.3 %collective-permute-start.23 = (f16[256,1024]{1,0:T(8,128)(2,1)}, f16[256,1024]{1,0:T(8,128)(2,1)}, u32[]{:S(2)}, u32[]{:S(2)}) collective-permute-start(f16[256,1024]{1,0:T(8,128)(2,1)} %get-tuple-element.69), channel_id=1, source_target_pairs={{0,6},{1,7},{2,0},{3,1},{4,2},{5,3},{6,4},{7,5},{8,14},{9,15},{10,... | collective-permute-start | bytes 1572872 | tf_op jit(solution)/shard_map/ppermute | solution.py:43
  195.1 9.1 %p_dot.3 = f32[1024,1024]{1,0:T(8,128)} custom-call(bf16[8,1024,128]{2,1,0:T(8,128)(2,1)} %copy-done.14, bf16[8,1024,128]{2,1,0:T(8,128)(2,1)} %collective-permute-done.24.other, bf16[1024,1024]{1,0:T(8,128)(2,1)} %mask_body.6.w_mine, bf16[1024,1024]{1,0:T(8,128)(2,1)} %mask_body.7.w_other), custom_call_target="tpu_custom_call" | custom-call | flops 1048576 | bytes 1048576 | tf_op jit(solution)/shard_map/p_dot/pallas_call | solution.py:179
  204.2 4.0 %fusion.5 = (f16[256,1024]{1,0:T(8,128)(2,1)}, f16[256,1024]{1,0:T(8,128)(2,1)}, f16[256,1024]{1,0:T(8,128)(2,1)}, f16[256,1024]{1,0:T(8,128)(2,1)}) fusion(f32[1024,1024]{1,0:T(8,128)} %p_dot.3, f32[]{:T(128)S(6)} %exp2.49), kind=kLoop, calls=%fused_computation.17 | loop fusion | flops 2097152 | bytes 6291460 | tf_op jit(solution)/shard_map/convert_element_type | solution.py:290
  208.2 5.6 %collective-permute-start.26 = (f16[256,1024]{1,0:T(8,128)(2,1)}, f16[256,1024]{1,0:T(8,128)(2,1)}, u32[]{:S(2)}, u32[]{:S(2)}) collective-permute-start(f16[256,1024]{1,0:T(8,128)(2,1)} %get-tuple-element.85), channel_id=1, source_target_pairs={{0,7},{1,6},{2,1},{3,0},{4,3},{5,2},{6,5},{7,4},{8,15},{9,14},{10,... | collective-permute-start | bytes 1572872 | tf_op jit(solution)/shard_map/ppermute | solution.py:43
  213.9 3.7 %collective-permute-start.28 = (f16[256,1024]{1,0:T(8,128)(2,1)}, f16[256,1024]{1,0:T(8,128)(2,1)}, u32[]{:S(2)}, u32[]{:S(2)}) collective-permute-start(f16[256,1024]{1,0:T(8,128)(2,1)} %get-tuple-element.83), channel_id=1, source_target_pairs={{0,5},{1,4},{2,7},{3,6},{4,1},{5,0},{6,3},{7,2},{8,13},{9,12},{10,... | collective-permute-start | bytes 1572872 | tf_op jit(solution)/shard_map/ppermute | solution.py:43
  219.4 2.2 fusion.10
  221.6 6.3 %collective-permute-done.25 = f16[256,1024]{1,0:T(8,128)(2,1)} collective-permute-done((f16[256,1024]{1,0:T(8,128)(2,1)}, f16[256,1024]{1,0:T(8,128)(2,1)}, u32[]{:S(2)}, u32[]{:S(2)}) %collective-permute-start.25) | collective-permute-done | bytes 524320 | tf_op jit(solution)/shard_map/ppermute | solution.py:43
  227.9 8.4 %collective-permute-done.26 = f16[256,1024]{1,0:T(8,128)(2,1)} collective-permute-done((f16[256,1024]{1,0:T(8,128)(2,1)}, f16[256,1024]{1,0:T(8,128)(2,1)}, u32[]{:S(2)}, u32[]{:S(2)}) %collective-permute-start.26) | collective-permute-done | bytes 524320 | tf_op jit(solution)/shard_map/ppermute | solution.py:43
  237.6 11.0 %collective-permute-done.28 = f16[256,1024]{1,0:T(8,128)(2,1)} collective-permute-done((f16[256,1024]{1,0:T(8,128)(2,1)}, f16[256,1024]{1,0:T(8,128)(2,1)}, u32[]{:S(2)}, u32[]{:S(2)}) %collective-permute-start.28) | collective-permute-done | bytes 524320 | tf_op jit(solution)/shard_map/ppermute | solution.py:43
  248.6 3.0 %multiply_convert_fusion.blocks = bf16[256,1024]{1,0:T(8,128)(2,1)} fusion(f32[256,1024]{1,0:T(8,128)S(1)} %bitcast.16, f16[256,1024]{1,0:T(8,128)(2,1)} %collective-permute-done.28, f16[256,1024]{1,0:T(8,128)(2,1)} %collective-permute-done.27, f16[256,1024]{1,0:T(8,128)(2,1)} %collective-permute-done.26, f32[256,1024]{1,0:T(8,128)S(1)} %fusion.10, ...), kind=kLoop, calls=%fused_computation.27 | loop fusion | flops 3670016 | bytes 4718596 | tf_op jit(solution)/shard_map/convert_element_type | solution.py:340
  251.5 2.3 pick.1
  253.9 4.3 %all-to-all-start.4 = ((bf16[32,128,128]{2,1,0:T(8,128)(2,1)}), bf16[32,128,128]{2,1,0:T(8,128)(2,1)}, u32[]{:S(2)}, u32[]{:S(2)}) async-start(bf16[32,128,128]{2,1,0:T(8,128)(2,1)} %pick.1), calls=%async_computation.4 | async-start | bytes 2097152 | tf_op jit(solution)/shard_map/all_to_all | solution.py:26
  263.0 11.4 %all-to-all-done.4 = bf16[32,128,128]{2,1,0:T(8,128)(2,1)} async-done(((bf16[32,128,128]{2,1,0:T(8,128)(2,1)}), bf16[32,128,128]{2,1,0:T(8,128)(2,1)}, u32[]{:S(2)}, u32[]{:S(2)}) %all-to-all-start.4) | async-done | bytes 1048608 | tf_op jit(solution)/shard_map/all_to_all | solution.py:26
  (152 shorter events, 36.2 us)
Async XLA Ops:
  1.4 16.1 %copy-start.27 = (s32[16,8]{1,0:T(8,128)}, s32[16,8]{1,0:T(8,128)S(1)}, u32[]{:S(2)}) copy-start(s32[16,8]{1,0:T(8,128)S(1)} %copy.18.pattern) | copy-start | bytes 1540
  4.7 17.9 %collective-permute-start = (bf16[272,1024]{1,0:T(8,128)(2,1)}, bf16[272,1024]{1,0:T(8,128)(2,1)S(1)}, u32[]{:S(2)}, u32[]{:S(2)}) collective-permute-start(bf16[272,1024]{1,0:T(8,128)(2,1)} %slab_body.1.refs_0_), channel_id=1, source_target_pairs={{0,1},{1,0},{2,3},{3,2},{4,5},{5,4},{6,7},{7,6},{8,9},{9,8},{10,11... | collective-permute-start | bytes 1671176 | tf_op jit(solution)/shard_map/ppermute | solution.py:30
  7.9 16.6 %collective-permute-start.1 = (bf16[272,1024]{1,0:T(8,128)(2,1)}, bf16[272,1024]{1,0:T(8,128)(2,1)S(1)}, u32[]{:S(2)}, u32[]{:S(2)}) collective-permute-start(bf16[272,1024]{1,0:T(8,128)(2,1)} %slab_body.1.refs_0_), channel_id=1, source_target_pairs={{0,2},{2,4},{4,6},{6,0},{1,3},{3,5},{5,7},{7,1},{8,10},{10,12},{12... | collective-permute-start | bytes 1671176 | tf_op jit(solution)/shard_map/ppermute | solution.py:276
  9.8 14.7 %collective-permute-start.2 = (bf16[272,1024]{1,0:T(8,128)(2,1)}, bf16[272,1024]{1,0:T(8,128)(2,1)S(1)}, u32[]{:S(2)}, u32[]{:S(2)}) collective-permute-start(bf16[272,1024]{1,0:T(8,128)(2,1)} %slab_body.1.refs_0_), channel_id=1, source_target_pairs={{0,6},{2,0},{4,2},{6,4},{1,7},{3,1},{5,3},{7,5},{8,14},{10,8},{12,... | collective-permute-start | bytes 1671176 | tf_op jit(solution)/shard_map/ppermute | solution.py:277
  22.6 21.7 %copy-start.2 = (bf16[272,1024]{1,0:T(8,128)(2,1)}, bf16[272,1024]{1,0:T(8,128)(2,1)S(1)}, u32[]{:S(2)}) copy-start(bf16[272,1024]{1,0:T(8,128)(2,1)S(1)} %collective-permute-done.refs_1_) | copy-start | bytes 1671172
  24.5 19.9 %copy-start.4 = (bf16[272,1024]{1,0:T(8,128)(2,1)}, bf16[272,1024]{1,0:T(8,128)(2,1)S(1)}, u32[]{:S(2)}) copy-start(bf16[272,1024]{1,0:T(8,128)(2,1)S(1)} %collective-permute-done.1.refs_3_.refs_6_) | copy-start | bytes 1671172
  24.5 19.9 %copy-start.6 = (bf16[272,1024]{1,0:T(8,128)(2,1)}, bf16[272,1024]{1,0:T(8,128)(2,1)S(1)}, u32[]{:S(2)}) copy-start(bf16[272,1024]{1,0:T(8,128)(2,1)S(1)} %collective-permute-done.2.refs_2_) | copy-start | bytes 1671172
  24.5 19.8 %collective-permute-start.8 = (bf16[1024,1024]{1,0:T(8,128)(2,1)}, bf16[1024,1024]{1,0:T(8,128)(2,1)S(1)}, u32[]{:S(2)}, u32[]{:S(2)}) collective-permute-start(bf16[1024,1024]{1,0:T(8,128)(2,1)} %mask_body.5), channel_id=1, source_target_pairs={{0,8},{8,0},{1,9},{9,1},{2,10},{10,2},{3,11},{11,3},{4,12},{12,4},... | collective-permute-start | bytes 6291464 | tf_op jit(solution)/shard_map/ppermute | solution.py:30
  24.6 4.6 %collective-permute-start.3 = (bf16[272,1024]{1,0:T(8,128)(2,1)S(1)}, bf16[272,1024]{1,0:T(8,128)(2,1)S(1)}, u32[]{:S(2)}, u32[]{:S(2)}) collective-permute-start(bf16[272,1024]{1,0:T(8,128)(2,1)S(1)} %copy-done), channel_id=1, source_target_pairs={{0,8},{8,0},{1,9},{9,1},{2,10},{10,2},{3,11},{11,3},{4,12},{12,4},... | collective-permute-start | bytes 1671176 | tf_op jit(solution)/shard_map/ppermute | solution.py:30
  25.1 4.9 %collective-permute-start.4 = (bf16[272,1024]{1,0:T(8,128)(2,1)S(1)}, bf16[272,1024]{1,0:T(8,128)(2,1)S(1)}, u32[]{:S(2)}, u32[]{:S(2)}) collective-permute-start(bf16[272,1024]{1,0:T(8,128)(2,1)S(1)} %collective-permute-done.refs_1_), channel_id=1, source_target_pairs={{0,8},{8,0},{1,9},{9,1},{2,10},{10,2},{3,11},{11,3},{4,12},{12,4},... | collective-permute-start | bytes 1671176 | tf_op jit(solution)/shard_map/ppermute | solution.py:30
  25.2 15.3 %collective-permute-start.7 = (bf16[272,1024]{1,0:T(8,128)(2,1)S(1)}, bf16[272,1024]{1,0:T(8,128)(2,1)S(1)}, u32[]{:S(2)}, u32[]{:S(2)}) collective-permute-start(bf16[272,1024]{1,0:T(8,128)(2,1)S(1)} %collective-permute-done.refs_1_), channel_id=1, source_target_pairs={{0,6},{2,0},{4,2},{6,4},{1,7},{3,1},{5,3},{7,5},{8,14},{10,8},{12,... | collective-permute-start | bytes 1671176 | tf_op jit(solution)/shard_map/ppermute | solution.py:282
  28.0 13.3 %collective-permute-start.6 = (bf16[272,1024]{1,0:T(8,128)(2,1)S(1)}, bf16[272,1024]{1,0:T(8,128)(2,1)S(1)}, u32[]{:S(2)}, u32[]{:S(2)}) collective-permute-start(bf16[272,1024]{1,0:T(8,128)(2,1)S(1)} %collective-permute-done.1.refs_3_.refs_6_), channel_id=1, source_target_pairs={{0,8},{8,0},{1,9},{9,1},{2,10},{10,2},{3,11},{11,3},{4,12},{12,4},... | collective-permute-start | bytes 1671176 | tf_op jit(solution)/shard_map/ppermute | solution.py:30
  29.1 15.2 %copy-start.19 = (bf16[272,1024]{1,0:T(8,128)(2,1)}, bf16[272,1024]{1,0:T(8,128)(2,1)S(1)}, u32[]{:S(2)}) copy-start(bf16[272,1024]{1,0:T(8,128)(2,1)S(1)} %collective-permute-done.3.refs_4_) | copy-start | bytes 1671172
  29.1 12.1 %collective-permute-start.5 = (bf16[272,1024]{1,0:T(8,128)(2,1)S(1)}, bf16[272,1024]{1,0:T(8,128)(2,1)S(1)}, u32[]{:S(2)}, u32[]{:S(2)}) collective-permute-start(bf16[272,1024]{1,0:T(8,128)(2,1)S(1)} %collective-permute-done.2.refs_2_), channel_id=1, source_target_pairs={{0,8},{8,0},{1,9},{9,1},{2,10},{10,2},{3,11},{11,3},{4,12},{12,4},... | collective-permute-start | bytes 1671176 | tf_op jit(solution)/shard_map/ppermute | solution.py:30
  29.9 31.2 %collective-permute-start.9 = (bf16[272,1024]{1,0:T(8,128)(2,1)S(1)}, bf16[272,1024]{1,0:T(8,128)(2,1)S(1)}, u32[]{:S(2)}, u32[]{:S(2)}) collective-permute-start(bf16[272,1024]{1,0:T(8,128)(2,1)S(1)} %collective-permute-done.refs_1_), channel_id=1, source_target_pairs={{0,2},{2,4},{4,6},{6,0},{1,3},{3,5},{5,7},{7,1},{8,10},{10,12},{12... | collective-permute-start | bytes 1671176 | tf_op jit(solution)/shard_map/ppermute | solution.py:284
  40.5 25.2 %copy-start.8 = (bf16[272,1024]{1,0:T(8,128)(2,1)}, bf16[272,1024]{1,0:T(8,128)(2,1)S(1)}, u32[]{:S(2)}) copy-start(bf16[272,1024]{1,0:T(8,128)(2,1)S(1)} %collective-permute-done.7.refs_0_.refs_3_) | copy-start | bytes 1671172
  40.5 20.6 %collective-permute-start.10 = (bf16[272,1024]{1,0:T(8,128)(2,1)S(1)}, bf16[272,1024]{1,0:T(8,128)(2,1)S(1)}, u32[]{:S(2)}, u32[]{:S(2)}) collective-permute-start(bf16[272,1024]{1,0:T(8,128)(2,1)S(1)} %collective-permute-done.1.refs_3_.refs_6_), channel_id=1, source_target_pairs={{0,2},{2,4},{4,6},{6,0},{1,3},{3,5},{5,7},{7,1},{8,10},{10,12},{12... | collective-permute-start | bytes 1671176 | tf_op jit(solution)/shard_map/ppermute | solution.py:283
  41.3 19.8 %collective-permute-start.11 = (bf16[272,1024]{1,0:T(8,128)(2,1)S(1)}, bf16[272,1024]{1,0:T(8,128)(2,1)}, u32[]{:S(2)}, u32[]{:S(2)}) collective-permute-start(bf16[272,1024]{1,0:T(8,128)(2,1)S(1)} %collective-permute-done.7.refs_0_.refs_3_), channel_id=1, source_target_pairs={{0,6},{2,0},{4,2},{6,4},{1,7},{3,1},{5,3},{7,5},{8,14},{10,8},{12,... | collective-permute-start | bytes 1671176 | tf_op jit(solution)/shard_map/ppermute | solution.py:295
  61.2 31.5 %all-to-all-start = ((f16[8,1040,128]{2,1,0:T(8,128)(2,1)}), f16[8,1040,128]{2,1,0:T(8,128)(2,1)}, u32[]{:S(2)}, u32[]{:S(2)}) async-start(f16[8,1040,128]{2,1,0:T(8,128)(2,1)} %select_convert_fusion.1), calls=%async_computation | async-start | bytes 4259840 | tf_op jit(solution)/shard_map/all_to_all | solution.py:26
  65.7 2.0 collective-permute-start.12
  65.8 3.5 %collective-permute-start.13 = (bf16[272,1024]{1,0:T(8,128)(2,1)S(1)}, bf16[272,1024]{1,0:T(8,128)(2,1)S(1)}, u32[]{:S(2)}, u32[]{:S(2)}) collective-permute-start(bf16[272,1024]{1,0:T(8,128)(2,1)S(1)} %collective-permute-done.9.refs_1_.refs_7_), channel_id=1, source_target_pairs={{0,8},{8,0},{1,9},{9,1},{2,10},{10,2},{3,11},{11,3},{4,12},{12,4},... | collective-permute-start | bytes 1671176 | tf_op jit(solution)/shard_map/ppermute | solution.py:30
  66.3 3.8 %collective-permute-start.14 = (bf16[272,1024]{1,0:T(8,128)(2,1)S(1)}, bf16[272,1024]{1,0:T(8,128)(2,1)S(1)}, u32[]{:S(2)}, u32[]{:S(2)}) collective-permute-start(bf16[272,1024]{1,0:T(8,128)(2,1)S(1)} %collective-permute-done.10.refs_2_.refs_4_), channel_id=1, source_target_pairs={{0,8},{8,0},{1,9},{9,1},{2,10},{10,2},{3,11},{11,3},{4,12},{12,4},... | collective-permute-start | bytes 1671176 | tf_op jit(solution)/shard_map/ppermute | solution.py:30
  66.3 3.7 %collective-permute-start.15 = (bf16[272,1024]{1,0:T(8,128)(2,1)}, bf16[272,1024]{1,0:T(8,128)(2,1)S(1)}, u32[]{:S(2)}, u32[]{:S(2)}) collective-permute-start(bf16[272,1024]{1,0:T(8,128)(2,1)} %collective-permute-done.11.refs_3_.refs_5_), channel_id=1, source_target_pairs={{0,8},{8,0},{1,9},{9,1},{2,10},{10,2},{3,11},{11,3},{4,12},{12,4},... | collective-permute-start | bytes 1671176 | tf_op jit(solution)/shard_map/ppermute | solution.py:30
  83.0 13.5 %copy-start.28 = (s32[2,8]{1,0:T(2,128)S(1)}, s32[2,8]{1,0:T(2,128)}, u32[]{:S(2)}) copy-start(s32[2,8]{1,0:T(2,128)} %param.12) | copy-start | bytes 196
  92.7 30.2 %all-to-all-start.1 = ((f16[8,1040,128]{2,1,0:T(8,128)(2,1)}), f16[8,1040,128]{2,1,0:T(8,128)(2,1)S(1)}, u32[]{:S(2)}, u32[]{:S(2)}) async-start(f16[8,1040,128]{2,1,0:T(8,128)(2,1)} %select_convert_fusion), calls=%async_computation.1 | async-start | bytes 4259840 | tf_op jit(solution)/shard_map/all_to_all | solution.py:26
  124.4 30.0 %all-to-all-start.2 = ((bf16[8,1024,128]{2,1,0:T(8,128)(2,1)}), bf16[8,1024,128]{2,1,0:T(8,128)(2,1)}, u32[]{:S(2)}, u32[]{:S(2)}) async-start(bf16[8,1024,128]{2,1,0:T(8,128)(2,1)} %broadcast_in_dim.51), calls=%async_computation.2 | async-start | bytes 4194304 | tf_op jit(solution)/shard_map/all_to_all | solution.py:26
  130.8 1.2 collective-permute-start.16
  132.0 5.1 %collective-permute-start.17 = (f32[8,128]{1,0:T(8,128)S(1)}, f32[8,128]{1,0:T(8,128)S(1)}, u32[]{:S(2)}, u32[]{:S(2)}) collective-permute-start(f32[8,128]{1,0:T(8,128)S(1)} %broadcast_maximum_fusion), channel_id=1, source_target_pairs={{0,4},{2,6},{4,0},{6,2},{1,5},{3,7},{5,1},{7,3},{8,12},{10,14},{12... | collective-permute-start | bytes 12296 | tf_op jit(solution)/shard_map/ppermute | solution.py:323
  137.1 4.8 %collective-permute-start.18 = (f32[8,128]{1,0:T(8,128)S(1)}, f32[8,128]{1,0:T(8,128)S(1)}, u32[]{:S(2)}, u32[]{:S(2)}) collective-permute-start(f32[8,128]{1,0:T(8,128)S(1)} %fusion.17), channel_id=1, source_target_pairs={{0,2},{2,4},{4,6},{6,0},{1,3},{3,5},{5,7},{7,1},{8,10},{10,12},{12... | collective-permute-start | bytes 12296 | tf_op jit(solution)/shard_map/ppermute | solution.py:324
  142.0 10.6 %collective-permute-start.19 = (f32[8,128]{1,0:T(8,128)S(1)}, f32[8,128]{1,0:T(8,128)S(1)}, u32[]{:S(2)}, u32[]{:S(2)}) collective-permute-start(f32[8,128]{1,0:T(8,128)S(1)} %max.30), channel_id=1, source_target_pairs={{0,1},{1,0},{2,3},{3,2},{4,5},{5,4},{6,7},{7,6},{8,9},{9,8},{10,11... | collective-permute-start | bytes 12296 | tf_op jit(solution)/shard_map/ppermute | solution.py:30
  156.0 4.5 %collective-permute-start.20 = (bf16[8,1024,128]{2,1,0:T(8,128)(2,1)}, bf16[8,1024,128]{2,1,0:T(8,128)(2,1)}, u32[]{:S(2)}, u32[]{:S(2)}) collective-permute-start(bf16[8,1024,128]{2,1,0:T(8,128)(2,1)} %all-to-all-done.2.mine), channel_id=1, source_target_pairs={{0,8},{8,0},{1,9},{9,1},{2,10},{10,2},{3,11},{11,3},{4,12},{12,4},... | collective-permute-start | bytes 6291464 | tf_op jit(solution)/shard_map/ppermute | solution.py:30
  156.0 31.8 %all-to-all-start.3 = ((bf16[8,1024,128]{2,1,0:T(8,128)(2,1)}), bf16[8,1024,128]{2,1,0:T(8,128)(2,1)S(1)}, u32[]{:S(2)}, u32[]{:S(2)}) async-start(bf16[8,1024,128]{2,1,0:T(8,128)(2,1)} %broadcast_in_dim.58), calls=%async_computation.3 | async-start | bytes 4194304 | tf_op jit(solution)/shard_map/all_to_all | solution.py:26
  169.6 18.2 %copy-start.1 = (bf16[272,1024]{1,0:T(8,128)(2,1)S(1)}, bf16[272,1024]{1,0:T(8,128)(2,1)}, u32[]{:S(2)}) copy-start(bf16[272,1024]{1,0:T(8,128)(2,1)} %slab_body.1.refs_0_) | copy-start | bytes 1671172
  169.6 18.2 %copy-start.29 = (s32[1,1,16,1]{2,3,1,0:T(1,128)S(1)}, s32[1,1,16,1]{2,3,1,0:T(1,128)}, u32[]{:S(2)}) copy-start(s32[1,1,16,1]{2,3,1,0:T(1,128)} %param.13) | copy-start | bytes 196
  187.8 7.3 %collective-permute-start.24 = (bf16[8,1024,128]{2,1,0:T(8,128)(2,1)S(1)}, bf16[8,1024,128]{2,1,0:T(8,128)(2,1)}, u32[]{:S(2)}, u32[]{:S(2)}) collective-permute-start(bf16[8,1024,128]{2,1,0:T(8,128)(2,1)S(1)} %all-to-all-done.3.mine), channel_id=1, source_target_pairs={{0,8},{8,0},{1,9},{9,1},{2,10},{10,2},{3,11},{11,3},{4,12},{12,4},... | collective-permute-start | bytes 6291464 | tf_op jit(solution)/shard_map/ppermute | solution.py:30
  189.0 24.9 %collective-permute-start.21 = (f16[256,1024]{1,0:T(8,128)(2,1)}, f16[256,1024]{1,0:T(8,128)(2,1)}, u32[]{:S(2)}, u32[]{:S(2)}) collective-permute-start(f16[256,1024]{1,0:T(8,128)(2,1)} %get-tuple-element.67), channel_id=1, source_target_pairs={{0,1},{1,0},{2,3},{3,2},{4,5},{5,4},{6,7},{7,6},{8,9},{9,8},{10,11... | collective-permute-start | bytes 1572872 | tf_op jit(solution)/shard_map/ppermute | solution.py:43
  191.8 22.1 %collective-permute-start.22 = (f16[256,1024]{1,0:T(8,128)(2,1)}, f16[256,1024]{1,0:T(8,128)(2,1)}, u32[]{:S(2)}, u32[]{:S(2)}) collective-permute-start(f16[256,1024]{1,0:T(8,128)(2,1)} %get-tuple-element.68), channel_id=1, source_target_pairs={{0,2},{1,3},{2,4},{3,5},{4,6},{5,7},{6,0},{7,1},{8,10},{9,11},{10,... | collective-permute-start | bytes 1572872 | tf_op jit(solution)/shard_map/ppermute | solution.py:43
  191.8 27.6 %collective-permute-start.23 = (f16[256,1024]{1,0:T(8,128)(2,1)}, f16[256,1024]{1,0:T(8,128)(2,1)}, u32[]{:S(2)}, u32[]{:S(2)}) collective-permute-start(f16[256,1024]{1,0:T(8,128)(2,1)} %get-tuple-element.69), channel_id=1, source_target_pairs={{0,6},{1,7},{2,0},{3,1},{4,2},{5,3},{6,4},{7,5},{8,14},{9,15},{10,... | collective-permute-start | bytes 1572872 | tf_op jit(solution)/shard_map/ppermute | solution.py:43
  204.2 13.4 %copy-start.7 = (bf16[272,1024]{1,0:T(8,128)(2,1)S(1)}, bf16[272,1024]{1,0:T(8,128)(2,1)}, u32[]{:S(2)}) copy-start(bf16[272,1024]{1,0:T(8,128)(2,1)} %copy-done.6) | copy-start | bytes 1671172
  204.2 13.5 %copy-start.9 = (bf16[272,1024]{1,0:T(8,128)(2,1)S(1)}, bf16[272,1024]{1,0:T(8,128)(2,1)}, u32[]{:S(2)}) copy-start(bf16[272,1024]{1,0:T(8,128)(2,1)} %copy-done.8) | copy-start | bytes 1671172
  204.2 14.8 %copy-start.11 = (bf16[272,1024]{1,0:T(8,128)(2,1)S(1)}, bf16[272,1024]{1,0:T(8,128)(2,1)}, u32[]{:S(2)}) copy-start(bf16[272,1024]{1,0:T(8,128)(2,1)} %copy-done.10) | copy-start | bytes 1671172
  208.2 19.6 %collective-permute-start.25 = (f16[256,1024]{1,0:T(8,128)(2,1)}, f16[256,1024]{1,0:T(8,128)(2,1)}, u32[]{:S(2)}, u32[]{:S(2)}) collective-permute-start(f16[256,1024]{1,0:T(8,128)(2,1)} %get-tuple-element.82), channel_id=1, source_target_pairs={{0,3},{1,2},{2,5},{3,4},{4,7},{5,6},{6,1},{7,0},{8,11},{9,10},{10,... | collective-permute-start | bytes 1572872 | tf_op jit(solution)/shard_map/ppermute | solution.py:43
  208.2 28.0 %collective-permute-start.26 = (f16[256,1024]{1,0:T(8,128)(2,1)}, f16[256,1024]{1,0:T(8,128)(2,1)}, u32[]{:S(2)}, u32[]{:S(2)}) collective-permute-start(f16[256,1024]{1,0:T(8,128)(2,1)} %get-tuple-element.85), channel_id=1, source_target_pairs={{0,7},{1,6},{2,1},{3,0},{4,3},{5,2},{6,5},{7,4},{8,15},{9,14},{10,... | collective-permute-start | bytes 1572872 | tf_op jit(solution)/shard_map/ppermute | solution.py:43
  213.9 23.7 %collective-permute-start.27 = (f16[256,1024]{1,0:T(8,128)(2,1)}, f16[256,1024]{1,0:T(8,128)(2,1)}, u32[]{:S(2)}, u32[]{:S(2)}) collective-permute-start(f16[256,1024]{1,0:T(8,128)(2,1)} %get-tuple-element.84), channel_id=1, source_target_pairs={{0,4},{1,5},{2,6},{3,7},{4,0},{5,1},{6,2},{7,3},{8,12},{9,13},{10,... | collective-permute-start | bytes 1572872 | tf_op jit(solution)/shard_map/ppermute | solution.py:43
  213.9 34.7 %collective-permute-start.28 = (f16[256,1024]{1,0:T(8,128)(2,1)}, f16[256,1024]{1,0:T(8,128)(2,1)}, u32[]{:S(2)}, u32[]{:S(2)}) collective-permute-start(f16[256,1024]{1,0:T(8,128)(2,1)} %get-tuple-element.83), channel_id=1, source_target_pairs={{0,5},{1,4},{2,7},{3,6},{4,1},{5,0},{6,3},{7,2},{8,13},{9,12},{10,... | collective-permute-start | bytes 1572872 | tf_op jit(solution)/shard_map/ppermute | solution.py:43
  219.4 29.2 %copy-start.16 = (f32[32,8,8,128]{3,1,2,0:T(8,128)S(1)}, f32[32,8,8,128]{3,1,2,0:T(8,128)}, u32[]{:S(2)}) copy-start(f32[32,8,8,128]{3,1,2,0:T(8,128)} %copy.28) | copy-start | bytes 3145732
  253.9 20.5 %all-to-all-start.4 = ((bf16[32,128,128]{2,1,0:T(8,128)(2,1)}), bf16[32,128,128]{2,1,0:T(8,128)(2,1)}, u32[]{:S(2)}, u32[]{:S(2)}) async-start(bf16[32,128,128]{2,1,0:T(8,128)(2,1)} %pick.1), calls=%async_computation.4 | async-start | bytes 2097152 | tf_op jit(solution)/shard_map/all_to_all | solution.py:26
  262.1 13.7 %copy-start.18 = (bf16[1,1,3,32,128,128]{5,4,3,2,1,0:T(8,128)(2,1)S(1)}, bf16[1,1,3,32,128,128]{5,4,3,2,1,0:T(8,128)(2,1)}, u32[]{:S(2)}) copy-start(bf16[1,1,3,32,128,128]{5,4,3,2,1,0:T(8,128)(2,1)} %param.14) | copy-start | bytes 9437188
  (16 other events, 85.9 us)

commit v2 on v1

--- a/solution.py
+++ b/solution.py
@@ -284,21 +284,14 @@
     up_side = lax.ppermute(side, "z", up)
     pieces = [slab, side, down_own, down_side, up_two, None, up_own, up_side]
 
-    def partial_w(tiles, p_mine, p_other):
-        part = p_dot(tiles, other_core(tiles), p_mine, p_other)
-        blocks = [part[at * height : (at + 1) * height] for at in range(len(EARLY))]
-        return blocks[0], [(v * scale).astype(WIRE) for v in blocks]
-
     mine = [pieces[k] for k in EARLY]
-    others, down_side = barrier(([other_core(v) for v in mine], down_side))
-    pieces[3] = down_side
-    pieces[5] = lax.ppermute(down_side, "z", down)
-    partial, peak = h_dot(mine, others, h_mine, h_other)
-    packed, late, density = barrier(
-        (encode(partial, peak), [pieces[k] for k in LATE], density)
+    partial, peak = h_dot(mine, [other_core(v) for v in mine], h_mine, h_other)
+    peak, down_side_late = barrier((peak, down_side))
+    packed, down_side, up_two, up_side, density = barrier(
+        (encode(partial, peak), down_side, up_two, up_side, density)
     )
-    for k, piece in zip(LATE, late):
-        pieces[k] = piece
+    pieces[3], pieces[4], pieces[7] = down_side, up_two, up_side
+    pieces[5] = lax.ppermute(down_side_late, "z", down)
     mine = [pieces[k] for k in LATE]
     packed_late = encode(*h_dot(mine, [other_core(v) for v in mine], h_mine, h_other))
     arrived, packed_late = barrier((exchange(packed, ROW_PAIR), packed_late))
@@ -323,20 +316,29 @@
     room = jnp.maximum(room, lax.ppermute(room, "z", two))
     room = jnp.maximum(room, lax.ppermute(room, "z", up))
     room = jnp.max(jnp.maximum(room, flip(room, "xhi"))) - 101.0
-    tiles, copies_late, room = barrier((exchange(copies, ROW_PAIR), copies_late, room))
-    tiles_late = exchange(copies_late, ROW_PAIR)
+    room = jnp.maximum(room, -100.0)
+    tiles_late, copies, room = barrier((exchange(copies_late, ROW_PAIR), copies, room))
+    tiles = exchange(copies, ROW_PAIR)
     scale, unscale = jnp.exp2(14.0 - room), jnp.exp2(room - 14.0)
 
-    early, wire = partial_w(tiles, p_mine, p_other)
-    wire, tiles_late = barrier((wire, tiles_late))
-    _, wire_late = partial_w(tiles_late, p_mine, p_other)
-    total = early
-    for part, chosen in ((wire, EARLY), (wire_late, LATE)):
-        for v, k in zip(part, chosen):
-            if k:
-                total = total + shifted(v, k).astype(F32) * unscale
-        if k == EARLY[-1]:
-            total = barrier(total)
+    part_late = p_dot(tiles_late, other_core(tiles_late), p_mine, p_other)
+    blocks = {k: part_late[at * height : (at + 1) * height] * scale for at, k in enumerate(LATE)}
+    near, far = lax.ppermute(blocks[4].astype(WIRE), "z", down), lax.ppermute(
+        blocks[5].astype(WIRE), "z", up
+    )
+    tiles, near, far = barrier((tiles, near, far))
+    got = [
+        shifted(blocks[7].astype(WIRE), 7),
+        shifted((blocks[3] + far.astype(F32)).astype(WIRE), 3),
+    ]
+    part = p_dot(tiles, other_core(tiles), p_mine, p_other)
+    total, one, two, six = (part[at * height : (at + 1) * height] * scale for at in range(4))
+    wires = [v.astype(WIRE) for v in (one, two, six + near.astype(F32))]
+    total, wires = barrier((total, wires))
+    got = [shifted(v, k) for v, k in zip(wires, (1, 2, 6))] + got
+    for v in got:
+        total = total + v.astype(F32)
+    total = total * unscale
     weighted = (total * keep).astype(BF)
 
     z, xhi = lax.axis_index("z"), lax.axis_index("xhi")

time: 279 us -> 266 us (0.953)
  waiting for transfers between devices: 98.7 us -> 85.2 us
  local copies, waits for them, and re-layouts: 13.2 us -> 17 us
  starting transfers between devices: 58.1 us -> 54.9 us
    ppermute x7 -> x5, waiting for transfers between devices: 27 us -> 12.4 us  [shifted(): return lax.ppermute(v, COL, pairs)]
    ppermute x1, waiting for transfers between devices: 9.38 us -> 0.01 us  [local(): down_side = lax.ppermute(side, 'z', down)]
    ppermute x7 -> x5, starting transfers between devices: 15.5 us -> 9.69 us  [shifted(): return lax.ppermute(v, COL, pairs)]
    ppermute x1, waiting for transfers between devices: 0.01 us -> 5.29 us  [local(): up_side = lax.ppermute(side, 'z', up)]
    ppermute x1 -> x3, starting transfers between devices: 2.99 us -> 7.01 us  [the longest x1 3.71 us: local(): pieces[5] = lax.ppermute(down_side_late, 'z', down)]
    ppermute x14, waiting for transfers between devices: 14.3 us -> 18.2 us  [flip(): return lax.ppermute(v, axis, [(0, 1), (1, 0)])]
    unnamed x63 -> x69, local copies, waits for them, and re-layouts: 6.96 us -> 10.7 us
    convert_element_type x2 -> x3, other arithmetic: 7.26 us -> 9.01 us  [the longest x1 4.38 us: local(): wires = [v.astype(WIRE) for v in (one, two, six + near.astype(F32))]]
  transfers between devices with their start and end apart: 34 -> 34, of which waited for: 21 -> 18; matrix products, arithmetic and copies ran while one was open for 13% -> 13% of each run, Pallas kernels for 21% -> 22%
where the time goes in v2:
time: 266 us; the launch traced here: 264 us
  waiting for transfers between devices  85.2 us (32%)
  Pallas kernels  62.6 us (24%)
  starting transfers between devices  54.9 us (21%)
  other arithmetic  39.1 us (15%)
  local copies, waits for them, and re-layouts  17 us (6%)
  between operations  5.41 us (2%)
    all_to_all x5, waiting for transfers between devices, exchange(): return lax.all_to_all(pieces, axes, split_axis=0, concat_axis=0, tiled=True)  37.6 us
    pallas_call x5, Pallas kernels, call_mask(): pl.pallas_call(body, out_shape=jax.ShapeDtypeStruct((height, shape[1]), B...  23.1 us
    all_to_all x5, starting transfers between devices, exchange(): return lax.all_to_all(pieces, axes, split_axis=0, concat_axis=0, tiled=True)  22.8 us
    pallas_call x2, Pallas kernels, p_dot(): pl.pallas_call(p_dot_body, out_shape=jax.ShapeDtypeStruct((width, width),...  18.2 us
    ppermute x14, waiting for transfers between devices, flip(): return lax.ppermute(v, axis, [(0, 1), (1, 0)])  18.2 us
    pallas_call x2, Pallas kernels, h_dot(): pl.pallas_call(h_dot_body, out_shape=(jax.ShapeDtypeStruct((CBLK, width +...  18.1 us
    ppermute x5, waiting for transfers between devices, shifted(): return lax.ppermute(v, COL, pairs)  12.4 us
    unnamed x69, local copies, waits for them, and re-layouts  10.7 us
  transfers between devices with their start and end apart: 34, of which 18 were waited for; matrix products, arithmetic and copies ran while one was open for 13% of the time, Pallas kernels for 22%

profile of v2, /device:TPU:0, one launch (start us, length us, event | category | flops | bytes accessed | tf_op | source)
XLA Modules:
  0.0 264.2 jit_solution(16146751222173510668)
XLA Ops:
  2.0 2.8 %slab_body.1.refs_0_ = bf16[272,1024]{1,0:T(8,128)(2,1)} custom-call(s32[16]{0:T(128)} %bitcast.19, s32[2,8]{1,0:T(2,128)} %slice.86.pattern, bf16[2048,1024]{1,0:T(8,128)(2,1)} %src.7), custom_call_target="tpu_custom_call" | custom-call | tf_op jit(solution)/shard_map/slab_body/pallas_call | solution.py:95
  4.8 4.1 %collective-permute-start.2 = (bf16[272,1024]{1,0:T(8,128)(2,1)}, bf16[272,1024]{1,0:T(8,128)(2,1)S(1)}, u32[]{:S(2)}, u32[]{:S(2)}) collective-permute-start(bf16[272,1024]{1,0:T(8,128)(2,1)} %slab_body.1.refs_0_), channel_id=1, source_target_pairs={{0,6},{2,0},{4,2},{6,4},{1,7},{3,1},{5,3},{7,5},{8,14},{10,8},{12,... | collective-permute-start | bytes 1671176 | tf_op jit(solution)/shard_map/ppermute | solution.py:277
  8.9 3.0 %collective-permute-start = (bf16[272,1024]{1,0:T(8,128)(2,1)}, bf16[272,1024]{1,0:T(8,128)(2,1)S(1)}, u32[]{:S(2)}, u32[]{:S(2)}) collective-permute-start(bf16[272,1024]{1,0:T(8,128)(2,1)} %slab_body.1.refs_0_), channel_id=1, source_target_pairs={{0,1},{1,0},{2,3},{3,2},{4,5},{5,4},{6,7},{7,6},{8,9},{9,8},{10,11... | collective-permute-start | bytes 1671176 | tf_op jit(solution)/shard_map/ppermute | solution.py:30
  12.5 5.0 %mask_body.5 = bf16[1024,1024]{1,0:T(8,128)(2,1)} custom-call(s32[2]{0:T(128)} %get-tuple-element.88.corner, s32[8,16]{1,0:T(8,128)} %pattern.5, bf16[1024,2048]{1,0:T(8,128)(2,1)} %src.5), custom_call_target="tpu_custom_call" | custom-call | tf_op jit(solution)/shard_map/mask_body/pallas_call | solution.py:95
  17.5 5.1 %mask_body.4.refs_8_ = bf16[1024,1024]{1,0:T(8,128)(2,1)} custom-call(s32[2]{0:T(128)} %get-tuple-element.89.corner, s32[8,16]{1,0:T(8,128)} %pattern.5, bf16[1024,2048]{1,0:T(8,128)(2,1)} %src.5), custom_call_target="tpu_custom_call" | custom-call | tf_op jit(solution)/shard_map/mask_body/pallas_call | solution.py:95
  22.6 1.7 collective-permute-done.1.refs_3_.refs_6_
  25.8 3.5 %collective-permute-done.3.refs_4_ = bf16[272,1024]{1,0:T(8,128)(2,1)S(1)} collective-permute-done((bf16[272,1024]{1,0:T(8,128)(2,1)S(1)}, bf16[272,1024]{1,0:T(8,128)(2,1)S(1)}, u32[]{:S(2)}, u32[]{:S(2)}) %collective-permute-start.3) | collective-permute-done | bytes 557088 | tf_op jit(solution)/shard_map/ppermute | solution.py:30
  29.3 3.0 %collective-permute-start.8 = (bf16[272,1024]{1,0:T(8,128)(2,1)S(1)}, bf16[272,1024]{1,0:T(8,128)(2,1)S(1)}, u32[]{:S(2)}, u32[]{:S(2)}) collective-permute-start(bf16[272,1024]{1,0:T(8,128)(2,1)S(1)} %collective-permute-done.refs_1_), channel_id=1, source_target_pairs={{0,6},{2,0},{4,2},{6,4},{1,7},{3,1},{5,3},{7,5},{8,14},{10,8},{12,... | collective-permute-start | bytes 1671176 | tf_op jit(solution)/shard_map/ppermute | solution.py:282
  35.6 9.1 %h_dot.2 = (f32[8,1040,128]{2,1,0:T(8,128)}, f32[4,8,256]{2,1,0:T(8,128)}) custom-call(bf16[272,1024]{1,0:T(8,128)(2,1)} %slab_body.1.refs_0_, bf16[272,1024]{1,0:T(8,128)(2,1)} %copy-done.6, bf16[272,1024]{1,0:T(8,128)(2,1)} %copy-done.2, bf16[272,1024]{1,0:T(8,128)(2,1)} %copy-done.4, bf16[272,1024]{1,0:T(8,128)(2,1)} %copy-done.21, ...), custom_call_target="tpu_custom_call" | custom-call | flops 1048576 | bytes 1048576 | tf_op jit(solution)/shard_map/h_dot/pallas_call | solution.py:158
  44.7 1.5 reduce_max.54
  46.9 3.7 %collective-permute-start.11 = (bf16[272,1024]{1,0:T(8,128)(2,1)S(1)}, bf16[272,1024]{1,0:T(8,128)(2,1)S(1)}, u32[]{:S(2)}, u32[]{:S(2)}) collective-permute-start(bf16[272,1024]{1,0:T(8,128)(2,1)S(1)} %collective-permute-done.8.refs_0_.refs_3_), channel_id=1, source_target_pairs={{0,6},{2,0},{4,2},{6,4},{1,7},{3,1},{5,3},{7,5},{8,14},{10,8},{12,... | collective-permute-start | bytes 1671176 | tf_op jit(solution)/shard_map/ppermute | solution.py:294
  50.6 4.1 %select_convert_fusion.1 = f16[8,1040,128]{2,1,0:T(8,128)(2,1)} fusion(f32[8,1040,128]{2,1,0:T(8,128)} %get-tuple-element.41, f32[]{:T(128)S(6)} %add.78, f32[]{:T(128)S(6)} %exp2.41, pred[1040]{0:T(1024)(128)(4,1)S(1)} %iota_compare_fusion.3), kind=kLoop, calls=%fused_computation.5 | loop fusion | flops 3194880 | bytes 6390808 | tf_op jit(solution)/shard_map/convert_element_type | solution.py:54
  54.8 5.3 %collective-permute-done.10.refs_1_.refs_7_ = bf16[272,1024]{1,0:T(8,128)(2,1)S(1)} collective-permute-done((bf16[272,1024]{1,0:T(8,128)(2,1)S(1)}, bf16[272,1024]{1,0:T(8,128)(2,1)S(1)}, u32[]{:S(2)}, u32[]{:S(2)}) %collective-permute-start.10) | collective-permute-done | bytes 557088 | tf_op jit(solution)/shard_map/ppermute | solution.py:284
  60.1 5.4 %all-to-all-start = ((f16[8,1040,128]{2,1,0:T(8,128)(2,1)}), f16[8,1040,128]{2,1,0:T(8,128)(2,1)}, u32[]{:S(2)}, u32[]{:S(2)}) async-start(f16[8,1040,128]{2,1,0:T(8,128)(2,1)} %select_convert_fusion.1), calls=%async_computation | async-start | bytes 4259840 | tf_op jit(solution)/shard_map/all_to_all | solution.py:26
  70.8 9.0 %h_dot.3 = (f32[8,1040,128]{2,1,0:T(8,128)}, f32[4,8,256]{2,1,0:T(8,128)}) custom-call(bf16[272,1024]{1,0:T(8,128)(2,1)} %copy-done.8, bf16[272,1024]{1,0:T(8,128)(2,1)} %copy-done.12, bf16[272,1024]{1,0:T(8,128)(2,1)} %copy-done.10, bf16[272,1024]{1,0:T(8,128)(2,1)} %copy-done.14, bf16[272,1024]{1,0:T(8,128)(2,1)} %copy-done.25, ...), custom_call_target="tpu_custom_call" | custom-call | flops 1048576 | bytes 1048576 | tf_op jit(solution)/shard_map/h_dot/pallas_call | solution.py:158
  81.9 4.2 %select_convert_fusion = f16[8,1040,128]{2,1,0:T(8,128)(2,1)} fusion(f32[8,1040,128]{2,1,0:T(8,128)} %get-tuple-element.49, f32[]{:T(128)S(6)} %add.79, f32[]{:T(128)S(6)} %exp2.43, pred[1040]{0:T(1024)(128)(4,1)S(1)} %iota_compare_fusion.3), kind=kLoop, calls=%fused_computation.4 | loop fusion | flops 3194880 | bytes 6390808 | tf_op jit(solution)/shard_map/convert_element_type | solution.py:54
  86.1 6.2 %all-to-all-done = f16[8,1040,128]{2,1,0:T(8,128)(2,1)} async-done(((f16[8,1040,128]{2,1,0:T(8,128)(2,1)}), f16[8,1040,128]{2,1,0:T(8,128)(2,1)}, u32[]{:S(2)}, u32[]{:S(2)}) %all-to-all-start) | async-done | bytes 2129952 | tf_op jit(solution)/shard_map/all_to_all | solution.py:26
  92.3 3.8 %all-to-all-start.1 = ((f16[8,1040,128]{2,1,0:T(8,128)(2,1)}), f16[8,1040,128]{2,1,0:T(8,128)(2,1)S(1)}, u32[]{:S(2)}, u32[]{:S(2)}) async-start(f16[8,1040,128]{2,1,0:T(8,128)(2,1)} %select_convert_fusion), calls=%async_computation.1 | async-start | bytes 4259840 | tf_op jit(solution)/shard_map/all_to_all | solution.py:26
  98.3 3.8 %abs_reduce_fusion = bf16[]{:T(256)} fusion(bf16[2048,1024]{1,0:T(8,128)(2,1)} %src.7), kind=kLoop, calls=%fused_computation.7 | loop fusion | flops 4194303 | bytes 4194306 | tf_op jit(solution)/shard_map/reduce_max | solution.py:305
  102.7 5.1 %mask_body.7.w_other = bf16[1024,1024]{1,0:T(8,128)(2,1)} custom-call(s32[2]{0:T(128)} %get-tuple-element.90.corner, s32[16,8]{1,0:T(8,128)} %copy-done.30, bf16[2048,1024]{1,0:T(8,128)(2,1)} %src.7), custom_call_target="tpu_custom_call" | custom-call | tf_op jit(solution)/shard_map/mask_body/pallas_call | solution.py:95
  107.8 5.1 %mask_body.6.w_mine = bf16[1024,1024]{1,0:T(8,128)(2,1)} custom-call(s32[2]{0:T(128)} %get-tuple-element.91.corner, s32[16,8]{1,0:T(8,128)} %copy-done.30, bf16[2048,1024]{1,0:T(8,128)(2,1)} %src.7), custom_call_target="tpu_custom_call" | custom-call | tf_op jit(solution)/shard_map/mask_body/pallas_call | solution.py:95
  112.9 1.5 convert_reduce_fusion.1
  114.4 2.1 multiply_reduce_fusion.1
  116.4 6.1 %all-to-all-done.1 = f16[8,1040,128]{2,1,0:T(8,128)(2,1)S(1)} async-done(((f16[8,1040,128]{2,1,0:T(8,128)(2,1)}), f16[8,1040,128]{2,1,0:T(8,128)(2,1)S(1)}, u32[]{:S(2)}, u32[]{:S(2)}) %all-to-all-start.1) | async-done | bytes 2129952 | tf_op jit(solution)/shard_map/all_to_all | solution.py:26
  122.5 1.6 broadcast_in_dim.51
  125.2 1.7 broadcast_in_dim.58
  126.9 3.6 %all-to-all-start.2 = ((bf16[8,1024,128]{2,1,0:T(8,128)(2,1)}), bf16[8,1024,128]{2,1,0:T(8,128)(2,1)S(1)}, u32[]{:S(2)}, u32[]{:S(2)}) async-start(bf16[8,1024,128]{2,1,0:T(8,128)(2,1)} %broadcast_in_dim.58), calls=%async_computation.2 | async-start | bytes 4194304 | tf_op jit(solution)/shard_map/all_to_all | solution.py:26
  133.1 5.1 %collective-permute-done.17 = f32[8,128]{1,0:T(8,128)S(1)} collective-permute-done((f32[8,128]{1,0:T(8,128)S(1)}, f32[8,128]{1,0:T(8,128)S(1)}, u32[]{:S(2)}, u32[]{:S(2)}) %collective-permute-start.17) | collective-permute-done | bytes 4128 | tf_op jit(solution)/shard_map/ppermute | solution.py:316
  138.2 4.8 %collective-permute-done.18 = f32[8,128]{1,0:T(8,128)S(1)} collective-permute-done((f32[8,128]{1,0:T(8,128)S(1)}, f32[8,128]{1,0:T(8,128)S(1)}, u32[]{:S(2)}, u32[]{:S(2)}) %collective-permute-start.18) | collective-permute-done | bytes 4128 | tf_op jit(solution)/shard_map/ppermute | solution.py:317
  143.0 2.7 %collective-permute-start.19 = (f32[8,128]{1,0:T(8,128)S(1)}, f32[8,128]{1,0:T(8,128)S(1)}, u32[]{:S(2)}, u32[]{:S(2)}) collective-permute-start(f32[8,128]{1,0:T(8,128)S(1)} %max.33), channel_id=1, source_target_pairs={{0,1},{1,0},{2,3},{3,2},{4,5},{5,4},{6,7},{7,6},{8,9},{9,8},{10,11... | collective-permute-start | bytes 12296 | tf_op jit(solution)/shard_map/ppermute | solution.py:30
  145.7 10.0 %collective-permute-done.19 = f32[8,128]{1,0:T(8,128)S(1)} collective-permute-done((f32[8,128]{1,0:T(8,128)S(1)}, f32[8,128]{1,0:T(8,128)S(1)}, u32[]{:S(2)}, u32[]{:S(2)}) %collective-permute-start.19) | collective-permute-done | bytes 4128 | tf_op jit(solution)/shard_map/ppermute | solution.py:30
  157.1 5.3 %all-to-all-start.3 = ((bf16[8,1024,128]{2,1,0:T(8,128)(2,1)}), bf16[8,1024,128]{2,1,0:T(8,128)(2,1)}, u32[]{:S(2)}, u32[]{:S(2)}) async-start(bf16[8,1024,128]{2,1,0:T(8,128)(2,1)} %broadcast_in_dim.51), calls=%async_computation.3 | async-start | bytes 4194304 | tf_op jit(solution)/shard_map/all_to_all | solution.py:26
  162.4 9.1 %p_dot.2 = f32[1024,1024]{1,0:T(8,128)} custom-call(bf16[8,1024,128]{2,1,0:T(8,128)(2,1)} %copy-done.16, bf16[8,1024,128]{2,1,0:T(8,128)(2,1)} %collective-permute-done.20.other, bf16[1024,1024]{1,0:T(8,128)(2,1)} %mask_body.6.w_mine, bf16[1024,1024]{1,0:T(8,128)(2,1)} %mask_body.7.w_other), custom_call_target="tpu_custom_call" | custom-call | flops 1048576 | bytes 1048576 | tf_op jit(solution)/shard_map/p_dot/pallas_call | solution.py:179
  171.6 1.8 fusion.9
  173.5 3.2 %collective-permute-start.21 = (f16[256,1024]{1,0:T(8,128)(2,1)S(1)}, f16[256,1024]{1,0:T(8,128)(2,1)S(1)}, u32[]{:S(2)}, u32[]{:S(2)}) collective-permute-start(f16[256,1024]{1,0:T(8,128)(2,1)S(1)} %get-tuple-element.87), channel_id=1, source_target_pairs={{0,6},{2,0},{4,2},{6,4},{1,7},{3,1},{5,3},{7,5},{8,14},{10,8},{12,... | collective-permute-start | bytes 1572872 | tf_op jit(solution)/shard_map/ppermute | solution.py:326
  176.7 13.4 %all-to-all-done.3.mine = bf16[8,1024,128]{2,1,0:T(8,128)(2,1)} async-done(((bf16[8,1024,128]{2,1,0:T(8,128)(2,1)}), bf16[8,1024,128]{2,1,0:T(8,128)(2,1)}, u32[]{:S(2)}, u32[]{:S(2)}) %all-to-all-start.3) | async-done | bytes 2097184 | tf_op jit(solution)/shard_map/all_to_all | solution.py:26
  190.6 2.8 %fusion.4 = (f16[256,1024]{1,0:T(8,128)(2,1)}, f16[256,1024]{1,0:T(8,128)(2,1)}) fusion(f32[1024,1024]{1,0:T(8,128)} %p_dot.2, f32[]{:T(128)S(6)} %exp2.49, f16[256,1024]{1,0:T(8,128)(2,1)S(1)} %collective-permute-done.22), kind=kLoop, calls=%fused_computation.14 | loop fusion | flops 1572864 | bytes 3670020 | tf_op jit(solution)/shard_map/convert_element_type | solution.py:331
  193.4 2.9 %collective-permute-start.27 = (f16[256,1024]{1,0:T(8,128)(2,1)}, f16[256,1024]{1,0:T(8,128)(2,1)}, u32[]{:S(2)}, u32[]{:S(2)}) collective-permute-start(f16[256,1024]{1,0:T(8,128)(2,1)} %get-tuple-element.84), channel_id=1, source_target_pairs={{0,7},{1,6},{2,1},{3,0},{4,3},{5,2},{6,5},{7,4},{8,15},{9,14},{10,... | collective-permute-start | bytes 1572872 | tf_op jit(solution)/shard_map/ppermute | solution.py:43
  196.3 1.5 collective-permute-start.28
  199.2 9.1 %p_dot.3 = f32[1024,1024]{1,0:T(8,128)} custom-call(bf16[8,1024,128]{2,1,0:T(8,128)(2,1)} %all-to-all-done.3.mine, bf16[8,1024,128]{2,1,0:T(8,128)(2,1)} %copy-done.20, bf16[1024,1024]{1,0:T(8,128)(2,1)} %mask_body.6.w_mine, bf16[1024,1024]{1,0:T(8,128)(2,1)} %mask_body.7.w_other), custom_call_target="tpu_custom_call" | custom-call | flops 1048576 | bytes 1048576 | tf_op jit(solution)/shard_map/p_dot/pallas_call | solution.py:179
  208.3 4.4 %fusion.6 = (f16[256,1024]{1,0:T(8,128)(2,1)}, f16[256,1024]{1,0:T(8,128)(2,1)}, f16[256,1024]{1,0:T(8,128)(2,1)}, f32[256,1024]{1,0:T(8,128)}) fusion(f32[1024,1024]{1,0:T(8,128)} %p_dot.3, f16[256,1024]{1,0:T(8,128)(2,1)} %copy-done.29, f32[]{:T(128)S(6)} %exp2.49), kind=kLoop, calls=%fused_computation.17 | loop fusion | flops 2359296 | bytes 7340036 | tf_op jit(solution)/shard_map/convert_element_type | solution.py:336
  212.7 2.0 collective-permute-start.24
  214.7 3.2 %collective-permute-start.26 = (f16[256,1024]{1,0:T(8,128)(2,1)}, f16[256,1024]{1,0:T(8,128)(2,1)}, u32[]{:S(2)}, u32[]{:S(2)}) collective-permute-start(f16[256,1024]{1,0:T(8,128)(2,1)} %get-tuple-element.67), channel_id=1, source_target_pairs={{0,6},{1,7},{2,0},{3,1},{4,2},{5,3},{6,4},{7,5},{8,14},{9,15},{10,... | collective-permute-start | bytes 1572872 | tf_op jit(solution)/shard_map/ppermute | solution.py:43
  220.6 12.3 %collective-permute-done.24 = f16[256,1024]{1,0:T(8,128)(2,1)} collective-permute-done((f16[256,1024]{1,0:T(8,128)(2,1)}, f16[256,1024]{1,0:T(8,128)(2,1)}, u32[]{:S(2)}, u32[]{:S(2)}) %collective-permute-start.24) | collective-permute-done | bytes 524320 | tf_op jit(solution)/shard_map/ppermute | solution.py:43
  233.0 3.8 %multiply_convert_fusion.blocks = bf16[256,1024]{1,0:T(8,128)(2,1)} fusion(f32[256,1024]{1,0:T(8,128)} %bitcast.17, f16[256,1024]{1,0:T(8,128)(2,1)} %collective-permute-done.28, f16[256,1024]{1,0:T(8,128)(2,1)} %collective-permute-done.27, f16[256,1024]{1,0:T(8,128)(2,1)} %collective-permute-done.26, f16[256,1024]{1,0:T(8,128)(2,1)} %collective-permute-done.25, ...), kind=kLoop, calls=%fused_computation.27 | loop fusion | flops 3407872 | bytes 5242884 | tf_op jit(solution)/shard_map/convert_element_type | solution.py:342
  236.8 2.3 pick.1
  239.1 4.7 %all-to-all-start.4 = ((bf16[32,128,128]{2,1,0:T(8,128)(2,1)}), bf16[32,128,128]{2,1,0:T(8,128)(2,1)}, u32[]{:S(2)}, u32[]{:S(2)}) async-start(bf16[32,128,128]{2,1,0:T(8,128)(2,1)} %pick.1), calls=%async_computation.4 | async-start | bytes 2097152 | tf_op jit(solution)/shard_map/all_to_all | solution.py:26
  249.5 11.8 %all-to-all-done.4 = bf16[32,128,128]{2,1,0:T(8,128)(2,1)} async-done(((bf16[32,128,128]{2,1,0:T(8,128)(2,1)}), bf16[32,128,128]{2,1,0:T(8,128)(2,1)}, u32[]{:S(2)}, u32[]{:S(2)}) %all-to-all-start.4) | async-done | bytes 1048608 | tf_op jit(solution)/shard_map/all_to_all | solution.py:26
  (158 shorter events, 31.5 us)
Async XLA Ops:
  1.4 16.1 %copy-start.30 = (s32[16,8]{1,0:T(8,128)}, s32[16,8]{1,0:T(8,128)S(1)}, u32[]{:S(2)}) copy-start(s32[16,8]{1,0:T(8,128)S(1)} %copy.18.pattern) | copy-start | bytes 1540
  4.8 17.9 %collective-permute-start.2 = (bf16[272,1024]{1,0:T(8,128)(2,1)}, bf16[272,1024]{1,0:T(8,128)(2,1)S(1)}, u32[]{:S(2)}, u32[]{:S(2)}) collective-permute-start(bf16[272,1024]{1,0:T(8,128)(2,1)} %slab_body.1.refs_0_), channel_id=1, source_target_pairs={{0,6},{2,0},{4,2},{6,4},{1,7},{3,1},{5,3},{7,5},{8,14},{10,8},{12,... | collective-permute-start | bytes 1671176 | tf_op jit(solution)/shard_map/ppermute | solution.py:277
  8.9 15.5 %collective-permute-start.1 = (bf16[272,1024]{1,0:T(8,128)(2,1)}, bf16[272,1024]{1,0:T(8,128)(2,1)S(1)}, u32[]{:S(2)}, u32[]{:S(2)}) collective-permute-start(bf16[272,1024]{1,0:T(8,128)(2,1)} %slab_body.1.refs_0_), channel_id=1, source_target_pairs={{0,2},{2,4},{4,6},{6,0},{1,3},{3,5},{5,7},{7,1},{8,10},{10,12},{12... | collective-permute-start | bytes 1671176 | tf_op jit(solution)/shard_map/ppermute | solution.py:276
  8.9 15.8 %collective-permute-start = (bf16[272,1024]{1,0:T(8,128)(2,1)}, bf16[272,1024]{1,0:T(8,128)(2,1)S(1)}, u32[]{:S(2)}, u32[]{:S(2)}) collective-permute-start(bf16[272,1024]{1,0:T(8,128)(2,1)} %slab_body.1.refs_0_), channel_id=1, source_target_pairs={{0,1},{1,0},{2,3},{3,2},{4,5},{5,4},{6,7},{7,6},{8,9},{9,8},{10,11... | collective-permute-start | bytes 1671176 | tf_op jit(solution)/shard_map/ppermute | solution.py:30
  22.6 11.6 %copy-start.2 = (bf16[272,1024]{1,0:T(8,128)(2,1)}, bf16[272,1024]{1,0:T(8,128)(2,1)S(1)}, u32[]{:S(2)}) copy-start(bf16[272,1024]{1,0:T(8,128)(2,1)S(1)} %collective-permute-done.2.refs_2_) | copy-start | bytes 1671172
  24.4 9.8 %copy-start.4 = (bf16[272,1024]{1,0:T(8,128)(2,1)}, bf16[272,1024]{1,0:T(8,128)(2,1)S(1)}, u32[]{:S(2)}) copy-start(bf16[272,1024]{1,0:T(8,128)(2,1)S(1)} %collective-permute-done.1.refs_3_.refs_6_) | copy-start | bytes 1671172
  24.7 9.5 %collective-permute-start.7 = (bf16[1024,1024]{1,0:T(8,128)(2,1)}, bf16[1024,1024]{1,0:T(8,128)(2,1)S(1)}, u32[]{:S(2)}, u32[]{:S(2)}) collective-permute-start(bf16[1024,1024]{1,0:T(8,128)(2,1)} %mask_body.5), channel_id=1, source_target_pairs={{0,8},{8,0},{1,9},{9,1},{2,10},{10,2},{3,11},{11,3},{4,12},{12,4},... | collective-permute-start | bytes 6291464 | tf_op jit(solution)/shard_map/ppermute | solution.py:30
  24.7 4.6 %collective-permute-start.3 = (bf16[272,1024]{1,0:T(8,128)(2,1)S(1)}, bf16[272,1024]{1,0:T(8,128)(2,1)S(1)}, u32[]{:S(2)}, u32[]{:S(2)}) collective-permute-start(bf16[272,1024]{1,0:T(8,128)(2,1)S(1)} %copy-done), channel_id=1, source_target_pairs={{0,8},{8,0},{1,9},{9,1},{2,10},{10,2},{3,11},{11,3},{4,12},{12,4},... | collective-permute-start | bytes 1671176 | tf_op jit(solution)/shard_map/ppermute | solution.py:30
  25.2 7.1 %collective-permute-start.5 = (bf16[272,1024]{1,0:T(8,128)(2,1)S(1)}, bf16[272,1024]{1,0:T(8,128)(2,1)S(1)}, u32[]{:S(2)}, u32[]{:S(2)}) collective-permute-start(bf16[272,1024]{1,0:T(8,128)(2,1)S(1)} %collective-permute-done.2.refs_2_), channel_id=1, source_target_pairs={{0,8},{8,0},{1,9},{9,1},{2,10},{10,2},{3,11},{11,3},{4,12},{12,4},... | collective-permute-start | bytes 1671176 | tf_op jit(solution)/shard_map/ppermute | solution.py:30
  25.3 7.1 %collective-permute-start.6 = (bf16[272,1024]{1,0:T(8,128)(2,1)S(1)}, bf16[272,1024]{1,0:T(8,128)(2,1)S(1)}, u32[]{:S(2)}, u32[]{:S(2)}) collective-permute-start(bf16[272,1024]{1,0:T(8,128)(2,1)S(1)} %collective-permute-done.1.refs_3_.refs_6_), channel_id=1, source_target_pairs={{0,8},{8,0},{1,9},{9,1},{2,10},{10,2},{3,11},{11,3},{4,12},{12,4},... | collective-permute-start | bytes 1671176 | tf_op jit(solution)/shard_map/ppermute | solution.py:30
  25.7 6.7 %collective-permute-start.4 = (bf16[272,1024]{1,0:T(8,128)(2,1)S(1)}, bf16[272,1024]{1,0:T(8,128)(2,1)S(1)}, u32[]{:S(2)}, u32[]{:S(2)}) collective-permute-start(bf16[272,1024]{1,0:T(8,128)(2,1)S(1)} %collective-permute-done.refs_1_), channel_id=1, source_target_pairs={{0,8},{8,0},{1,9},{9,1},{2,10},{10,2},{3,11},{11,3},{4,12},{12,4},... | collective-permute-start | bytes 1671176 | tf_op jit(solution)/shard_map/ppermute | solution.py:30
  29.3 15.4 %collective-permute-start.8 = (bf16[272,1024]{1,0:T(8,128)(2,1)S(1)}, bf16[272,1024]{1,0:T(8,128)(2,1)S(1)}, u32[]{:S(2)}, u32[]{:S(2)}) collective-permute-start(bf16[272,1024]{1,0:T(8,128)(2,1)S(1)} %collective-permute-done.refs_1_), channel_id=1, source_target_pairs={{0,6},{2,0},{4,2},{6,4},{1,7},{3,1},{5,3},{7,5},{8,14},{10,8},{12,... | collective-permute-start | bytes 1671176 | tf_op jit(solution)/shard_map/ppermute | solution.py:282
  32.2 22.5 %collective-permute-start.9 = (bf16[272,1024]{1,0:T(8,128)(2,1)S(1)}, bf16[272,1024]{1,0:T(8,128)(2,1)S(1)}, u32[]{:S(2)}, u32[]{:S(2)}) collective-permute-start(bf16[272,1024]{1,0:T(8,128)(2,1)S(1)} %collective-permute-done.1.refs_3_.refs_6_), channel_id=1, source_target_pairs={{0,2},{2,4},{4,6},{6,0},{1,3},{3,5},{5,7},{7,1},{8,10},{10,12},{12... | collective-permute-start | bytes 1671176 | tf_op jit(solution)/shard_map/ppermute | solution.py:283
  32.4 27.7 %collective-permute-start.10 = (bf16[272,1024]{1,0:T(8,128)(2,1)S(1)}, bf16[272,1024]{1,0:T(8,128)(2,1)S(1)}, u32[]{:S(2)}, u32[]{:S(2)}) collective-permute-start(bf16[272,1024]{1,0:T(8,128)(2,1)S(1)} %collective-permute-done.refs_1_), channel_id=1, source_target_pairs={{0,2},{2,4},{4,6},{6,0},{1,3},{3,5},{5,7},{7,1},{8,10},{10,12},{12... | collective-permute-start | bytes 1671176 | tf_op jit(solution)/shard_map/ppermute | solution.py:284
  44.7 20.8 %copy-start.8 = (bf16[272,1024]{1,0:T(8,128)(2,1)}, bf16[272,1024]{1,0:T(8,128)(2,1)S(1)}, u32[]{:S(2)}) copy-start(bf16[272,1024]{1,0:T(8,128)(2,1)S(1)} %collective-permute-done.8.refs_0_.refs_3_) | copy-start | bytes 1671172
  46.9 19.2 %collective-permute-start.11 = (bf16[272,1024]{1,0:T(8,128)(2,1)S(1)}, bf16[272,1024]{1,0:T(8,128)(2,1)S(1)}, u32[]{:S(2)}, u32[]{:S(2)}) collective-permute-start(bf16[272,1024]{1,0:T(8,128)(2,1)S(1)} %collective-permute-done.8.refs_0_.refs_3_), channel_id=1, source_target_pairs={{0,6},{2,0},{4,2},{6,4},{1,7},{3,1},{5,3},{7,5},{8,14},{10,8},{12,... | collective-permute-start | bytes 1671176 | tf_op jit(solution)/shard_map/ppermute | solution.py:294
  54.8 15.1 %copy-start.10 = (bf16[272,1024]{1,0:T(8,128)(2,1)}, bf16[272,1024]{1,0:T(8,128)(2,1)S(1)}, u32[]{:S(2)}) copy-start(bf16[272,1024]{1,0:T(8,128)(2,1)S(1)} %collective-permute-done.9.refs_2_.refs_4_) | copy-start | bytes 1671172
  60.1 9.8 %copy-start.12 = (bf16[272,1024]{1,0:T(8,128)(2,1)}, bf16[272,1024]{1,0:T(8,128)(2,1)S(1)}, u32[]{:S(2)}) copy-start(bf16[272,1024]{1,0:T(8,128)(2,1)S(1)} %collective-permute-done.10.refs_1_.refs_7_) | copy-start | bytes 1671172
  60.1 32.2 %all-to-all-start = ((f16[8,1040,128]{2,1,0:T(8,128)(2,1)}), f16[8,1040,128]{2,1,0:T(8,128)(2,1)}, u32[]{:S(2)}, u32[]{:S(2)}) async-start(f16[8,1040,128]{2,1,0:T(8,128)(2,1)} %select_convert_fusion.1), calls=%async_computation | async-start | bytes 4259840 | tf_op jit(solution)/shard_map/all_to_all | solution.py:26
  65.5 2.0 collective-permute-start.12
  65.6 2.7 %collective-permute-start.13 = (bf16[272,1024]{1,0:T(8,128)(2,1)S(1)}, bf16[272,1024]{1,0:T(8,128)(2,1)S(1)}, u32[]{:S(2)}, u32[]{:S(2)}) collective-permute-start(bf16[272,1024]{1,0:T(8,128)(2,1)S(1)} %collective-permute-done.10.refs_1_.refs_7_), channel_id=1, source_target_pairs={{0,8},{8,0},{1,9},{9,1},{2,10},{10,2},{3,11},{11,3},{4,12},{12,4},... | collective-permute-start | bytes 1671176 | tf_op jit(solution)/shard_map/ppermute | solution.py:30
  66.1 3.0 %collective-permute-start.14 = (bf16[272,1024]{1,0:T(8,128)(2,1)S(1)}, bf16[272,1024]{1,0:T(8,128)(2,1)S(1)}, u32[]{:S(2)}, u32[]{:S(2)}) collective-permute-start(bf16[272,1024]{1,0:T(8,128)(2,1)S(1)} %collective-permute-done.9.refs_2_.refs_4_), channel_id=1, source_target_pairs={{0,8},{8,0},{1,9},{9,1},{2,10},{10,2},{3,11},{11,3},{4,12},{12,4},... | collective-permute-start | bytes 1671176 | tf_op jit(solution)/shard_map/ppermute | solution.py:30
  66.2 3.7 %collective-permute-start.15 = (bf16[272,1024]{1,0:T(8,128)(2,1)S(1)}, bf16[272,1024]{1,0:T(8,128)(2,1)S(1)}, u32[]{:S(2)}, u32[]{:S(2)}) collective-permute-start(bf16[272,1024]{1,0:T(8,128)(2,1)S(1)} %collective-permute-done.11.refs_3_.refs_5_), channel_id=1, source_target_pairs={{0,8},{8,0},{1,9},{9,1},{2,10},{10,2},{3,11},{11,3},{4,12},{12,4},... | collective-permute-start | bytes 1671176 | tf_op jit(solution)/shard_map/ppermute | solution.py:30
  81.9 14.2 %copy-start.31 = (s32[2,8]{1,0:T(2,128)S(1)}, s32[2,8]{1,0:T(2,128)}, u32[]{:S(2)}) copy-start(s32[2,8]{1,0:T(2,128)} %param.12) | copy-start | bytes 196
  92.3 30.2 %all-to-all-start.1 = ((f16[8,1040,128]{2,1,0:T(8,128)(2,1)}), f16[8,1040,128]{2,1,0:T(8,128)(2,1)S(1)}, u32[]{:S(2)}, u32[]{:S(2)}) async-start(f16[8,1040,128]{2,1,0:T(8,128)(2,1)} %select_convert_fusion), calls=%async_computation.1 | async-start | bytes 4259840 | tf_op jit(solution)/shard_map/all_to_all | solution.py:26
  126.9 30.1 %all-to-all-start.2 = ((bf16[8,1024,128]{2,1,0:T(8,128)(2,1)}), bf16[8,1024,128]{2,1,0:T(8,128)(2,1)S(1)}, u32[]{:S(2)}, u32[]{:S(2)}) async-start(bf16[8,1024,128]{2,1,0:T(8,128)(2,1)} %broadcast_in_dim.58), calls=%async_computation.2 | async-start | bytes 4194304 | tf_op jit(solution)/shard_map/all_to_all | solution.py:26
  131.8 1.2 collective-permute-start.16
  133.1 5.1 %collective-permute-start.17 = (f32[8,128]{1,0:T(8,128)S(1)}, f32[8,128]{1,0:T(8,128)S(1)}, u32[]{:S(2)}, u32[]{:S(2)}) collective-permute-start(f32[8,128]{1,0:T(8,128)S(1)} %broadcast_maximum_fusion), channel_id=1, source_target_pairs={{0,4},{2,6},{4,0},{6,2},{1,5},{3,7},{5,1},{7,3},{8,12},{10,14},{12... | collective-permute-start | bytes 12296 | tf_op jit(solution)/shard_map/ppermute | solution.py:316
  138.2 4.8 %collective-permute-start.18 = (f32[8,128]{1,0:T(8,128)S(1)}, f32[8,128]{1,0:T(8,128)S(1)}, u32[]{:S(2)}, u32[]{:S(2)}) collective-permute-start(f32[8,128]{1,0:T(8,128)S(1)} %fusion.17), channel_id=1, source_target_pairs={{0,2},{2,4},{4,6},{6,0},{1,3},{3,5},{5,7},{7,1},{8,10},{10,12},{12... | collective-permute-start | bytes 12296 | tf_op jit(solution)/shard_map/ppermute | solution.py:317
  143.0 12.7 %collective-permute-start.19 = (f32[8,128]{1,0:T(8,128)S(1)}, f32[8,128]{1,0:T(8,128)S(1)}, u32[]{:S(2)}, u32[]{:S(2)}) collective-permute-start(f32[8,128]{1,0:T(8,128)S(1)} %max.33), channel_id=1, source_target_pairs={{0,1},{1,0},{2,3},{3,2},{4,5},{5,4},{6,7},{7,6},{8,9},{9,8},{10,11... | collective-permute-start | bytes 12296 | tf_op jit(solution)/shard_map/ppermute | solution.py:30
  157.0 5.4 %collective-permute-start.20 = (bf16[8,1024,128]{2,1,0:T(8,128)(2,1)S(1)}, bf16[8,1024,128]{2,1,0:T(8,128)(2,1)}, u32[]{:S(2)}, u32[]{:S(2)}) collective-permute-start(bf16[8,1024,128]{2,1,0:T(8,128)(2,1)S(1)} %all-to-all-done.2.mine), channel_id=1, source_target_pairs={{0,8},{8,0},{1,9},{9,1},{2,10},{10,2},{3,11},{11,3},{4,12},{12,4},... | collective-permute-start | bytes 6291464 | tf_op jit(solution)/shard_map/ppermute | solution.py:30
  157.1 33.0 %all-to-all-start.3 = ((bf16[8,1024,128]{2,1,0:T(8,128)(2,1)}), bf16[8,1024,128]{2,1,0:T(8,128)(2,1)}, u32[]{:S(2)}, u32[]{:S(2)}) async-start(bf16[8,1024,128]{2,1,0:T(8,128)(2,1)} %broadcast_in_dim.51), calls=%async_computation.3 | async-start | bytes 4194304 | tf_op jit(solution)/shard_map/all_to_all | solution.py:26
  162.4 27.8 %copy-start.32 = (s32[1,1,16,1]{2,3,1,0:T(1,128)S(1)}, s32[1,1,16,1]{2,3,1,0:T(1,128)}, u32[]{:S(2)}) copy-start(s32[1,1,16,1]{2,3,1,0:T(1,128)} %param.13) | copy-start | bytes 196
  173.4 16.7 %collective-permute-start.22 = (f16[256,1024]{1,0:T(8,128)(2,1)S(1)}, f16[256,1024]{1,0:T(8,128)(2,1)S(1)}, u32[]{:S(2)}, u32[]{:S(2)}) collective-permute-start(f16[256,1024]{1,0:T(8,128)(2,1)S(1)} %get-tuple-element.86), channel_id=1, source_target_pairs={{0,2},{2,4},{4,6},{6,0},{1,3},{3,5},{5,7},{7,1},{8,10},{10,12},{12... | collective-permute-start | bytes 1572872 | tf_op jit(solution)/shard_map/ppermute | solution.py:326
  173.5 16.6 %collective-permute-start.21 = (f16[256,1024]{1,0:T(8,128)(2,1)S(1)}, f16[256,1024]{1,0:T(8,128)(2,1)S(1)}, u32[]{:S(2)}, u32[]{:S(2)}) collective-permute-start(f16[256,1024]{1,0:T(8,128)(2,1)S(1)} %get-tuple-element.87), channel_id=1, source_target_pairs={{0,6},{2,0},{4,2},{6,4},{1,7},{3,1},{5,3},{7,5},{8,14},{10,8},{12,... | collective-permute-start | bytes 1572872 | tf_op jit(solution)/shard_map/ppermute | solution.py:326
  190.1 7.7 %collective-permute-start.23 = (bf16[8,1024,128]{2,1,0:T(8,128)(2,1)}, bf16[8,1024,128]{2,1,0:T(8,128)(2,1)S(1)}, u32[]{:S(2)}, u32[]{:S(2)}) collective-permute-start(bf16[8,1024,128]{2,1,0:T(8,128)(2,1)} %all-to-all-done.3.mine), channel_id=1, source_target_pairs={{0,8},{8,0},{1,9},{9,1},{2,10},{10,2},{3,11},{11,3},{4,12},{12,4},... | collective-permute-start | bytes 6291464 | tf_op jit(solution)/shard_map/ppermute | solution.py:30
  193.4 27.1 %collective-permute-start.27 = (f16[256,1024]{1,0:T(8,128)(2,1)}, f16[256,1024]{1,0:T(8,128)(2,1)}, u32[]{:S(2)}, u32[]{:S(2)}) collective-permute-start(f16[256,1024]{1,0:T(8,128)(2,1)} %get-tuple-element.84), channel_id=1, source_target_pairs={{0,7},{1,6},{2,1},{3,0},{4,3},{5,2},{6,5},{7,4},{8,15},{9,14},{10,... | collective-permute-start | bytes 1572872 | tf_op jit(solution)/shard_map/ppermute | solution.py:43
  196.3 24.3 %collective-permute-start.28 = (f16[256,1024]{1,0:T(8,128)(2,1)}, f16[256,1024]{1,0:T(8,128)(2,1)}, u32[]{:S(2)}, u32[]{:S(2)}) collective-permute-start(f16[256,1024]{1,0:T(8,128)(2,1)} %get-tuple-element.85), channel_id=1, source_target_pairs={{0,3},{1,2},{2,5},{3,4},{4,7},{5,6},{6,1},{7,0},{8,11},{9,10},{10,... | collective-permute-start | bytes 1572872 | tf_op jit(solution)/shard_map/ppermute | solution.py:43
  208.3 10.4 %copy-start.3 = (bf16[272,1024]{1,0:T(8,128)(2,1)S(1)}, bf16[272,1024]{1,0:T(8,128)(2,1)}, u32[]{:S(2)}) copy-start(bf16[272,1024]{1,0:T(8,128)(2,1)} %copy-done.2) | copy-start | bytes 1671172
  208.3 10.4 %copy-start.5 = (bf16[272,1024]{1,0:T(8,128)(2,1)S(1)}, bf16[272,1024]{1,0:T(8,128)(2,1)}, u32[]{:S(2)}) copy-start(bf16[272,1024]{1,0:T(8,128)(2,1)} %copy-done.4) | copy-start | bytes 1671172
  208.3 10.4 %copy-start.7 = (bf16[272,1024]{1,0:T(8,128)(2,1)S(1)}, bf16[272,1024]{1,0:T(8,128)(2,1)}, u32[]{:S(2)}) copy-start(bf16[272,1024]{1,0:T(8,128)(2,1)} %copy-done.6) | copy-start | bytes 1671172
  208.3 10.4 %copy-start.9 = (bf16[272,1024]{1,0:T(8,128)(2,1)S(1)}, bf16[272,1024]{1,0:T(8,128)(2,1)}, u32[]{:S(2)}) copy-start(bf16[272,1024]{1,0:T(8,128)(2,1)} %copy-done.8) | copy-start | bytes 1671172
  208.3 11.1 %copy-start.11 = (bf16[272,1024]{1,0:T(8,128)(2,1)S(1)}, bf16[272,1024]{1,0:T(8,128)(2,1)}, u32[]{:S(2)}) copy-start(bf16[272,1024]{1,0:T(8,128)(2,1)} %copy-done.10) | copy-start | bytes 1671172
  212.7 20.2 %collective-permute-start.24 = (f16[256,1024]{1,0:T(8,128)(2,1)}, f16[256,1024]{1,0:T(8,128)(2,1)}, u32[]{:S(2)}, u32[]{:S(2)}) collective-permute-start(f16[256,1024]{1,0:T(8,128)(2,1)} %get-tuple-element.65), channel_id=1, source_target_pairs={{0,1},{1,0},{2,3},{3,2},{4,5},{5,4},{6,7},{7,6},{8,9},{9,8},{10,11... | collective-permute-start | bytes 1572872 | tf_op jit(solution)/shard_map/ppermute | solution.py:43
  214.7 18.2 %collective-permute-start.25 = (f16[256,1024]{1,0:T(8,128)(2,1)}, f16[256,1024]{1,0:T(8,128)(2,1)}, u32[]{:S(2)}, u32[]{:S(2)}) collective-permute-start(f16[256,1024]{1,0:T(8,128)(2,1)} %get-tuple-element.66), channel_id=1, source_target_pairs={{0,2},{1,3},{2,4},{3,5},{4,6},{5,7},{6,0},{7,1},{8,10},{9,11},{10,... | collective-permute-start | bytes 1572872 | tf_op jit(solution)/shard_map/ppermute | solution.py:43
  214.7 18.2 %collective-permute-start.26 = (f16[256,1024]{1,0:T(8,128)(2,1)}, f16[256,1024]{1,0:T(8,128)(2,1)}, u32[]{:S(2)}, u32[]{:S(2)}) collective-permute-start(f16[256,1024]{1,0:T(8,128)(2,1)} %get-tuple-element.67), channel_id=1, source_target_pairs={{0,6},{1,7},{2,0},{3,1},{4,2},{5,3},{6,4},{7,5},{8,14},{9,15},{10,... | collective-permute-start | bytes 1572872 | tf_op jit(solution)/shard_map/ppermute | solution.py:43
  239.1 22.3 %all-to-all-start.4 = ((bf16[32,128,128]{2,1,0:T(8,128)(2,1)}), bf16[32,128,128]{2,1,0:T(8,128)(2,1)}, u32[]{:S(2)}, u32[]{:S(2)}) async-start(bf16[32,128,128]{2,1,0:T(8,128)(2,1)} %pick.1), calls=%async_computation.4 | async-start | bytes 2097152 | tf_op jit(solution)/shard_map/all_to_all | solution.py:26
  248.7 14.1 %copy-start.19 = (bf16[1,1,3,32,128,128]{5,4,3,2,1,0:T(8,128)(2,1)S(1)}, bf16[1,1,3,32,128,128]{5,4,3,2,1,0:T(8,128)(2,1)}, u32[]{:S(2)}) copy-start(bf16[1,1,3,32,128,128]{5,4,3,2,1,0:T(8,128)(2,1)} %param.14) | copy-start | bytes 9437188
  (19 other events, 63.3 us)

commit v3 on v2

--- a/solution.py
+++ b/solution.py
@@ -65,25 +65,32 @@
     return flip(v, "core")
 
 
+def keep_rows(pattern, row, col, src, dst):
+    rows, cols = (size // BLOCK for size in src.shape)
+    at_col = lax.broadcasted_iota(jnp.int32, (1, src.shape[1]), 1) // BLOCK
+    for r in range(rows):
+        keep = jnp.zeros((1, src.shape[1]), F32)
+        for c in range(cols):
+            keep = jnp.where(at_col == c, pattern(row + r, col + c).astype(F32), keep)
+        at = slice(r * BLOCK, (r + 1) * BLOCK)
+        dst[at] = src[at] * keep.astype(BF)
+
+
 def mask_body(corner, pattern, src, dst):
     rows, cols = (size // BLOCK for size in src.shape)
-    for row in range(rows):
-        for col in range(cols):
-            at = (slice(row * BLOCK, (row + 1) * BLOCK), slice(col * BLOCK, (col + 1) * BLOCK))
-            keep = pattern[corner[0] * rows + row, corner[1] * cols + col] != 0
-
-            @pl.when(keep)
-            def _():
-                dst[at] = src[at]
-
-            @pl.when(jnp.logical_not(keep))
-            def _():
-                dst[at] = jnp.zeros((BLOCK, BLOCK), BF)
+    read = lambda r, c: pattern[r, c]
+    keep_rows(read, corner[0] * rows, corner[1] * cols, src, dst)
+
+
+def turned_body(corner, pattern, src, dst):
+    rows, cols = (size // BLOCK for size in src.shape)
+    read = lambda r, c: pattern[c, r]
+    keep_rows(read, corner[0] * rows, corner[1] * cols, src, dst)
 
 
 def slab_body(target, pattern, src, dst):
     rows, cols = src.shape
-    mask_body((0, 0), pattern, src, dst.at[:rows])
+    keep_rows(lambda r, c: pattern[c, r], 0, 0, src, dst.at[:rows])
     lane = lax.broadcasted_iota(jnp.int32, (PAD, cols), 1)
     note = jnp.zeros((PAD, cols), F32)
     for k in range(SBLK * CBLK):
@@ -105,10 +112,10 @@
     )(*scalars, matrix)
 
 
-def mask(matrix, pattern, shape, row, col):
+def mask(body, matrix, pattern, shape, row, col):
     corner = jnp.stack((jnp.asarray(row, jnp.int32), jnp.asarray(col, jnp.int32)))
     index = lambda g, at, pat: (at[0], at[1])
-    return call_mask(mask_body, (corner, pattern), matrix, shape, shape[0], index)
+    return call_mask(body, (corner, pattern), matrix, shape, shape[0], index)
 
 
 def mask_slab(matrix, pattern, target, shape):
@@ -250,7 +257,12 @@
 
 
 def pair_sums(derivative, blocks):
-    return jnp.sum(derivative.astype(F32) * blocks.astype(F32)[None], axis=(2, 3))
+    return jnp.stack(
+        [
+            jnp.sum(derivative[z].astype(F32) * blocks.astype(F32), axis=(1, 2))
+            for z in range(derivative.shape[0])
+        ]
+    )
 
 
 def local(density, hamiltonian, pattern_p, pattern_h, pattern_s, owner, d_intersection, d_hamilton):
@@ -268,15 +280,15 @@
     def route(blocks):
         return exchange(pick(blocks, source), COL)
 
-    slab = mask_slab(density, pattern_p[:SBLK], target, (SBLK * BLOCK, width))
+    slab = mask_slab(density, pattern_p.T, target, (SBLK * BLOCK, width))
     up, down = ([(i, (i + d) % 4) for i in range(4)] for d in (1, -1))
     barrier = lax.optimization_barrier
     height = SBLK * BLOCK
     side = flip(slab, "xhi")
     up_own = lax.ppermute(slab, "z", up)
     down_own = lax.ppermute(slab, "z", down)
-    h_mine = mask(hamiltonian, pattern_h, (width, width), 0, core)
-    h_sent = mask(hamiltonian, pattern_h, (width, width), 0, 1 - core)
+    h_mine = mask(mask_body, hamiltonian, pattern_h, (width, width), 0, core)
+    h_sent = mask(mask_body, hamiltonian, pattern_h, (width, width), 0, 1 - core)
     side, up_own, down_own, h_mine, h_sent = barrier((side, up_own, down_own, h_mine, h_sent))
     h_other = other_core(h_sent)
     down_side = lax.ppermute(side, "z", down)
@@ -287,8 +299,8 @@
     mine = [pieces[k] for k in EARLY]
     partial, peak = h_dot(mine, [other_core(v) for v in mine], h_mine, h_other)
     peak, down_side_late = barrier((peak, down_side))
-    packed, down_side, up_two, up_side, density = barrier(
-        (encode(partial, peak), down_side, up_two, up_side, density)
+    packed, down_side, up_two, density = barrier(
+        (encode(partial, peak), down_side, up_two, density)
     )
     pieces[3], pieces[4], pieces[7] = down_side, up_two, up_side
     pieces[5] = lax.ppermute(down_side_late, "z", down)
@@ -300,8 +312,8 @@
     panel = panel.astype(BF)
     copies = jnp.broadcast_to(panel[None], (CBLK,) + panel.shape)
     keep = jnp.repeat(jnp.repeat(pattern_s, BLOCK, axis=0), BLOCK, axis=1).astype(F32)
-    p_mine = mask(density, pattern_p, (width, width), core, 0)
-    p_other = mask(density, pattern_p, (width, width), 1 - core, 0)
+    p_mine = mask(turned_body, density, pattern_p.T, (width, width), core, 0)
+    p_other = mask(turned_body, density, pattern_p.T, (width, width), 1 - core, 0)
     most_p = jnp.max(jnp.abs(density)).astype(F32)
     copies, arrived_late, p_mine, p_other, keep, most_p = barrier(
         (copies, arrived_late, p_mine, p_other, keep, most_p)
@@ -335,8 +347,9 @@
     total, one, two, six = (part[at * height : (at + 1) * height] * scale for at in range(4))
     wires = [v.astype(WIRE) for v in (one, two, six + near.astype(F32))]
     total, wires = barrier((total, wires))
-    got = [shifted(v, k) for v, k in zip(wires, (1, 2, 6))] + got
-    for v in got:
+    last = [shifted(v, k) for v, k in zip(wires, (1, 2, 6))]
+    total = barrier(total + got[0].astype(F32) + got[1].astype(F32))
+    for v in last:
         total = total + v.astype(F32)
     total = total * unscale
     weighted = (total * keep).astype(BF)

time: 266 us -> 258 us (0.970)
  Pallas kernels: 62.6 us -> 57.6 us
  local copies, waits for them, and re-layouts: 17 us -> 13.6 us
    pallas_call x5, Pallas kernels: 23.1 us -> 18.1 us  [call_mask(): pl.pallas_call(body, out_shape=jax.ShapeDtypeStruct((height, shape[1]), B...]
    ppermute x1, waiting for transfers between devices: 5.29 us -> 0.86 us  [local(): up_side = lax.ppermute(side, 'z', up)]
    ppermute x1, starting transfers between devices: 3.22 us -> 0.43 us  [local(): lax.ppermute(blocks[4].astype(WIRE), 'z', down)]
    unnamed x69 -> x60, local copies, waits for them, and re-layouts: 10.7 us -> 7.95 us
  transfers between devices with their start and end apart: 34 -> 34, of which waited for: 18 -> 23; matrix products, arithmetic and copies ran while one was open for 13% -> 15% of each run, Pallas kernels for 22% -> 21%
where the time goes in v3:
time: 258 us; the launch traced here: 256 us
  waiting for transfers between devices  85.1 us (33%)
  Pallas kernels  57.6 us (22%)
  starting transfers between devices  54 us (21%)
  other arithmetic  40.5 us (16%)
  local copies, waits for them, and re-layouts  13.6 us (5%)
  between operations  5.07 us (2%)
    all_to_all x5, waiting for transfers between devices, exchange(): return lax.all_to_all(pieces, axes, split_axis=0, concat_axis=0, tiled=True)  39.9 us
    all_to_all x5, starting transfers between devices, exchange(): return lax.all_to_all(pieces, axes, split_axis=0, concat_axis=0, tiled=True)  23.1 us
    pallas_call x2, Pallas kernels, p_dot(): pl.pallas_call(p_dot_body, out_shape=jax.ShapeDtypeStruct((width, width),...  18.2 us
    pallas_call x2, Pallas kernels, h_dot(): pl.pallas_call(h_dot_body, out_shape=(jax.ShapeDtypeStruct((CBLK, width +...  18.1 us
    pallas_call x5, Pallas kernels, call_mask(): pl.pallas_call(body, out_shape=jax.ShapeDtypeStruct((height, shape[1]), B...  18.1 us
    ppermute x14, waiting for transfers between devices, flip(): return lax.ppermute(v, axis, [(0, 1), (1, 0)])  17.6 us
    ppermute x5, waiting for transfers between devices, shifted(): return lax.ppermute(v, COL, pairs)  11.2 us
    ppermute x5, starting transfers between devices, shifted(): return lax.ppermute(v, COL, pairs)  10.4 us
  transfers between devices with their start and end apart: 34, of which 23 were waited for; matrix products, arithmetic and copies ran while one was open for 15% of the time, Pallas kernels for 21%

profile of v3, /device:TPU:0, one launch (start us, length us, event | category | flops | bytes accessed | tf_op | source)
XLA Modules:
  0.0 255.9 jit_solution(11084848536568341009)
XLA Ops:
  0.6 2.6 %slab_body.1.refs_0_ = bf16[272,1024]{1,0:T(8,128)(2,1)} custom-call(s32[16]{0:T(128)} %bitcast.45, s32[8,16]{1,0:T(8,128)} %bitcast.36, bf16[2048,1024]{1,0:T(8,128)(2,1)} %src.7), custom_call_target="tpu_custom_call" | custom-call | tf_op jit(solution)/shard_map/slab_body/pallas_call | solution.py:102
  3.3 3.1 %collective-permute-start = (bf16[272,1024]{1,0:T(8,128)(2,1)}, bf16[272,1024]{1,0:T(8,128)(2,1)S(1)}, u32[]{:S(2)}, u32[]{:S(2)}) collective-permute-start(bf16[272,1024]{1,0:T(8,128)(2,1)} %slab_body.1.refs_0_), channel_id=1, source_target_pairs={{0,1},{1,0},{2,3},{3,2},{4,5},{5,4},{6,7},{7,6},{8,9},{9,8},{10,11... | collective-permute-start | bytes 1671176 | tf_op jit(solution)/shard_map/ppermute | solution.py:30
  6.4 1.9 collective-permute-start.1
  8.3 2.1 collective-permute-start.2
  11.0 3.9 %mask_body.2.refs_8_ = bf16[1024,1024]{1,0:T(8,128)(2,1)} custom-call(s32[2]{0:T(128)} %get-tuple-element.93.corner, s32[8,16]{1,0:T(8,128)} %pattern.3, bf16[1024,2048]{1,0:T(8,128)(2,1)} %src.5), custom_call_target="tpu_custom_call" | custom-call | tf_op jit(solution)/shard_map/mask_body/pallas_call | solution.py:102
  14.9 3.9 %mask_body.3 = bf16[1024,1024]{1,0:T(8,128)(2,1)} custom-call(s32[2]{0:T(128)} %get-tuple-element.92.corner, s32[8,16]{1,0:T(8,128)} %pattern.3, bf16[1024,2048]{1,0:T(8,128)(2,1)} %src.5), custom_call_target="tpu_custom_call" | custom-call | tf_op jit(solution)/shard_map/mask_body/pallas_call | solution.py:102
  19.2 3.8 %collective-permute-done.1.refs_3_.refs_6_ = bf16[272,1024]{1,0:T(8,128)(2,1)S(1)} collective-permute-done((bf16[272,1024]{1,0:T(8,128)(2,1)}, bf16[272,1024]{1,0:T(8,128)(2,1)S(1)}, u32[]{:S(2)}, u32[]{:S(2)}) %collective-permute-start.1) | collective-permute-done | bytes 557088 | tf_op jit(solution)/shard_map/ppermute | solution.py:288
  24.2 4.3 %collective-permute-done.3.refs_4_ = bf16[272,1024]{1,0:T(8,128)(2,1)S(1)} collective-permute-done((bf16[272,1024]{1,0:T(8,128)(2,1)S(1)}, bf16[272,1024]{1,0:T(8,128)(2,1)S(1)}, u32[]{:S(2)}, u32[]{:S(2)}) %collective-permute-start.3) | collective-permute-done | bytes 557088 | tf_op jit(solution)/shard_map/ppermute | solution.py:30
  28.5 2.9 %collective-permute-start.8 = (bf16[272,1024]{1,0:T(8,128)(2,1)S(1)}, bf16[272,1024]{1,0:T(8,128)(2,1)S(1)}, u32[]{:S(2)}, u32[]{:S(2)}) collective-permute-start(bf16[272,1024]{1,0:T(8,128)(2,1)S(1)} %collective-permute-done.refs_1_), channel_id=1, source_target_pairs={{0,6},{2,0},{4,2},{6,4},{1,7},{3,1},{5,3},{7,5},{8,14},{10,8},{12,... | collective-permute-start | bytes 1671176 | tf_op jit(solution)/shard_map/ppermute | solution.py:294
  34.2 9.0 %h_dot.2 = (f32[8,1040,128]{2,1,0:T(8,128)}, f32[4,8,256]{2,1,0:T(8,128)}) custom-call(bf16[272,1024]{1,0:T(8,128)(2,1)} %slab_body.1.refs_0_, bf16[272,1024]{1,0:T(8,128)(2,1)} %copy-done.2, bf16[272,1024]{1,0:T(8,128)(2,1)} %copy-done.6, bf16[272,1024]{1,0:T(8,128)(2,1)} %copy-done.4, bf16[272,1024]{1,0:T(8,128)(2,1)} %copy-done.21, ...), custom_call_target="tpu_custom_call" | custom-call | flops 1048576 | bytes 1048576 | tf_op jit(solution)/shard_map/h_dot/pallas_call | solution.py:165
  45.7 3.8 %collective-permute-start.11 = (bf16[272,1024]{1,0:T(8,128)(2,1)S(1)}, bf16[272,1024]{1,0:T(8,128)(2,1)S(1)}, u32[]{:S(2)}, u32[]{:S(2)}) collective-permute-start(bf16[272,1024]{1,0:T(8,128)(2,1)S(1)} %collective-permute-done.8.refs_0_.refs_3_), channel_id=1, source_target_pairs={{0,6},{2,0},{4,2},{6,4},{1,7},{3,1},{5,3},{7,5},{8,14},{10,8},{12,... | collective-permute-start | bytes 1671176 | tf_op jit(solution)/shard_map/ppermute | solution.py:306
  49.5 4.2 %select_convert_fusion.1 = f16[8,1040,128]{2,1,0:T(8,128)(2,1)} fusion(f32[8,1040,128]{2,1,0:T(8,128)} %get-tuple-element.40, f32[]{:T(128)S(6)} %add.78, f32[]{:T(128)S(6)} %exp2.41, pred[1040]{0:T(1024)(128)(4,1)S(1)} %iota_compare_fusion.3), kind=kLoop, calls=%fused_computation.1 | loop fusion | flops 3194880 | bytes 6390808 | tf_op jit(solution)/shard_map/convert_element_type | solution.py:54
  53.7 4.5 %all-to-all-start = ((f16[8,1040,128]{2,1,0:T(8,128)(2,1)}), f16[8,1040,128]{2,1,0:T(8,128)(2,1)}, u32[]{:S(2)}, u32[]{:S(2)}) async-start(f16[8,1040,128]{2,1,0:T(8,128)(2,1)} %select_convert_fusion.1), calls=%async_computation | async-start | bytes 4259840 | tf_op jit(solution)/shard_map/all_to_all | solution.py:26
  64.3 9.1 %h_dot.3 = (f32[8,1040,128]{2,1,0:T(8,128)}, f32[4,8,256]{2,1,0:T(8,128)}) custom-call(bf16[272,1024]{1,0:T(8,128)(2,1)} %copy-done.8, bf16[272,1024]{1,0:T(8,128)(2,1)} %copy-done.12, bf16[272,1024]{1,0:T(8,128)(2,1)} %copy-done.10, bf16[272,1024]{1,0:T(8,128)(2,1)} %copy-done.14, bf16[272,1024]{1,0:T(8,128)(2,1)} %copy-done.24, ...), custom_call_target="tpu_custom_call" | custom-call | flops 1048576 | bytes 1048576 | tf_op jit(solution)/shard_map/h_dot/pallas_call | solution.py:165
  75.4 4.2 %select_convert_fusion = f16[8,1040,128]{2,1,0:T(8,128)(2,1)} fusion(f32[8,1040,128]{2,1,0:T(8,128)} %get-tuple-element.47, f32[]{:T(128)S(6)} %add.79, f32[]{:T(128)S(6)} %exp2.43, pred[1040]{0:T(1024)(128)(4,1)S(1)} %iota_compare_fusion.3), kind=kLoop, calls=%fused_computation | loop fusion | flops 3194880 | bytes 6390808 | tf_op jit(solution)/shard_map/convert_element_type | solution.py:54
  79.6 5.6 %all-to-all-done = f16[8,1040,128]{2,1,0:T(8,128)(2,1)} async-done(((f16[8,1040,128]{2,1,0:T(8,128)(2,1)}), f16[8,1040,128]{2,1,0:T(8,128)(2,1)}, u32[]{:S(2)}, u32[]{:S(2)}) %all-to-all-start) | async-done | bytes 2129952 | tf_op jit(solution)/shard_map/all_to_all | solution.py:26
  85.2 3.8 %all-to-all-start.1 = ((f16[8,1040,128]{2,1,0:T(8,128)(2,1)}), f16[8,1040,128]{2,1,0:T(8,128)(2,1)S(1)}, u32[]{:S(2)}, u32[]{:S(2)}) async-start(f16[8,1040,128]{2,1,0:T(8,128)(2,1)} %select_convert_fusion), calls=%async_computation.1 | async-start | bytes 4259840 | tf_op jit(solution)/shard_map/all_to_all | solution.py:26
  91.1 3.8 %turned_body.2.w_mine = bf16[1024,1024]{1,0:T(8,128)(2,1)} custom-call(s32[2]{0:T(128)} %get-tuple-element.95.corner, s32[8,16]{1,0:T(8,128)} %bitcast.37, bf16[2048,1024]{1,0:T(8,128)(2,1)} %src.7), custom_call_target="tpu_custom_call" | custom-call | tf_op jit(solution)/shard_map/turned_body/pallas_call | solution.py:102
  95.0 3.8 %turned_body.3.w_other = bf16[1024,1024]{1,0:T(8,128)(2,1)} custom-call(s32[2]{0:T(128)} %get-tuple-element.94.corner, s32[8,16]{1,0:T(8,128)} %bitcast.38, bf16[2048,1024]{1,0:T(8,128)(2,1)} %src.7), custom_call_target="tpu_custom_call" | custom-call | tf_op jit(solution)/shard_map/turned_body/pallas_call | solution.py:102
  98.8 3.8 %abs_reduce_fusion = bf16[]{:T(256)} fusion(bf16[2048,1024]{1,0:T(8,128)(2,1)} %src.7), kind=kLoop, calls=%fused_computation.3 | loop fusion | flops 4194303 | bytes 4194306 | tf_op jit(solution)/shard_map/reduce_max | solution.py:317
  104.7 2.1 multiply_reduce_fusion.1
  106.8 8.6 %all-to-all-done.1 = f16[8,1040,128]{2,1,0:T(8,128)(2,1)S(1)} async-done(((f16[8,1040,128]{2,1,0:T(8,128)(2,1)}), f16[8,1040,128]{2,1,0:T(8,128)(2,1)S(1)}, u32[]{:S(2)}, u32[]{:S(2)}) %all-to-all-start.1) | async-done | bytes 2129952 | tf_op jit(solution)/shard_map/all_to_all | solution.py:26
  115.3 1.7 broadcast_in_dim.51
  119.7 4.3 %all-to-all-start.2 = ((bf16[8,1024,128]{2,1,0:T(8,128)(2,1)}), bf16[8,1024,128]{2,1,0:T(8,128)(2,1)}, u32[]{:S(2)}, u32[]{:S(2)}) async-start(bf16[8,1024,128]{2,1,0:T(8,128)(2,1)} %broadcast_in_dim.90), calls=%async_computation.2 | async-start | bytes 4194304 | tf_op jit(solution)/shard_map/all_to_all | solution.py:26
  126.8 5.0 %collective-permute-done.17 = f32[8,128]{1,0:T(8,128)S(1)} collective-permute-done((f32[8,128]{1,0:T(8,128)S(1)}, f32[8,128]{1,0:T(8,128)S(1)}, u32[]{:S(2)}, u32[]{:S(2)}) %collective-permute-start.17) | collective-permute-done | bytes 4128 | tf_op jit(solution)/shard_map/ppermute | solution.py:328
  131.8 4.8 %collective-permute-done.18 = f32[8,128]{1,0:T(8,128)S(1)} collective-permute-done((f32[8,128]{1,0:T(8,128)S(1)}, f32[8,128]{1,0:T(8,128)S(1)}, u32[]{:S(2)}, u32[]{:S(2)}) %collective-permute-start.18) | collective-permute-done | bytes 4128 | tf_op jit(solution)/shard_map/ppermute | solution.py:329
  136.6 2.0 collective-permute-start.19
  138.6 9.2 %collective-permute-done.19 = f32[8,128]{1,0:T(8,128)S(1)} collective-permute-done((f32[8,128]{1,0:T(8,128)S(1)}, f32[8,128]{1,0:T(8,128)S(1)}, u32[]{:S(2)}, u32[]{:S(2)}) %collective-permute-start.19) | collective-permute-done | bytes 4128 | tf_op jit(solution)/shard_map/ppermute | solution.py:30
  149.7 4.2 %all-to-all-start.3 = ((bf16[8,1024,128]{2,1,0:T(8,128)(2,1)}), bf16[8,1024,128]{2,1,0:T(8,128)(2,1)S(1)}, u32[]{:S(2)}, u32[]{:S(2)}) async-start(bf16[8,1024,128]{2,1,0:T(8,128)(2,1)} %broadcast_in_dim.51), calls=%async_computation.3 | async-start | bytes 4194304 | tf_op jit(solution)/shard_map/all_to_all | solution.py:26
  154.2 9.1 %p_dot.2 = f32[1024,1024]{1,0:T(8,128)} custom-call(bf16[8,1024,128]{2,1,0:T(8,128)(2,1)} %all-to-all-done.2.mine, bf16[8,1024,128]{2,1,0:T(8,128)(2,1)} %collective-permute-done.20.other, bf16[1024,1024]{1,0:T(8,128)(2,1)} %turned_body.2.w_mine, bf16[1024,1024]{1,0:T(8,128)(2,1)} %turned_body.3.w_other), custom_call_target="tpu_custom_call" | custom-call | flops 1048576 | bytes 1048576 | tf_op jit(solution)/shard_map/p_dot/pallas_call | solution.py:186
  163.3 2.9 %fusion.13 = (f16[256,1024]{1,0:T(8,128)(2,1)}, f16[256,1024]{1,0:T(8,128)(2,1)}) fusion(f32[1024,1024]{1,0:T(8,128)} %p_dot.2, f32[]{:T(128)S(6)} %exp2.49), kind=kLoop, calls=%fused_computation.32 | loop fusion | flops 1048576 | bytes 3145732 | tf_op jit(solution)/shard_map/convert_element_type | solution.py:339
  166.6 1.6 collective-permute-start.22
  168.2 13.4 %all-to-all-done.3.mine = bf16[8,1024,128]{2,1,0:T(8,128)(2,1)S(1)} async-done(((bf16[8,1024,128]{2,1,0:T(8,128)(2,1)}), bf16[8,1024,128]{2,1,0:T(8,128)(2,1)S(1)}, u32[]{:S(2)}, u32[]{:S(2)}) %all-to-all-start.3) | async-done | bytes 2097184 | tf_op jit(solution)/shard_map/all_to_all | solution.py:26
  182.8 2.9 %fusion.8 = (f16[256,1024]{1,0:T(8,128)(2,1)}, f16[256,1024]{1,0:T(8,128)(2,1)}) fusion(f32[1024,1024]{1,0:T(8,128)} %p_dot.2, f32[]{:T(128)S(6)} %exp2.49, f16[256,1024]{1,0:T(8,128)(2,1)S(1)} %collective-permute-done.22), kind=kLoop, calls=%fused_computation.22 | loop fusion | flops 1572864 | bytes 3670020 | tf_op jit(solution)/shard_map/convert_element_type | solution.py:343
  185.7 2.6 %collective-permute-start.24 = (f16[256,1024]{1,0:T(8,128)(2,1)}, f16[256,1024]{1,0:T(8,128)(2,1)}, u32[]{:S(2)}, u32[]{:S(2)}) collective-permute-start(f16[256,1024]{1,0:T(8,128)(2,1)} %get-tuple-element.84), channel_id=1, source_target_pairs={{0,7},{1,6},{2,1},{3,0},{4,3},{5,2},{6,5},{7,4},{8,15},{9,14},{10,... | collective-permute-start | bytes 1572872 | tf_op jit(solution)/shard_map/ppermute | solution.py:43
  188.3 1.8 collective-permute-start.25
  190.1 9.1 %p_dot.3 = f32[1024,1024]{1,0:T(8,128)} custom-call(bf16[8,1024,128]{2,1,0:T(8,128)(2,1)} %copy-done.16, bf16[8,1024,128]{2,1,0:T(8,128)(2,1)} %collective-permute-done.23.other, bf16[1024,1024]{1,0:T(8,128)(2,1)} %turned_body.2.w_mine, bf16[1024,1024]{1,0:T(8,128)(2,1)} %turned_body.3.w_other), custom_call_target="tpu_custom_call" | custom-call | flops 1048576 | bytes 1048576 | tf_op jit(solution)/shard_map/p_dot/pallas_call | solution.py:186
  199.3 4.4 %fusion.10 = (f16[256,1024]{1,0:T(8,128)(2,1)}, f16[256,1024]{1,0:T(8,128)(2,1)}, f16[256,1024]{1,0:T(8,128)(2,1)}, f32[256,1024]{1,0:T(8,128)}) fusion(f32[1024,1024]{1,0:T(8,128)} %p_dot.3, f16[256,1024]{1,0:T(8,128)(2,1)} %collective-permute-done.21, f32[]{:T(128)S(6)} %exp2.49), kind=kLoop, calls=%fused_computation.25 | loop fusion | flops 2359296 | bytes 7340036 | tf_op jit(solution)/shard_map/convert_element_type | solution.py:348
  203.7 2.8 %collective-permute-start.26 = (f16[256,1024]{1,0:T(8,128)(2,1)}, f16[256,1024]{1,0:T(8,128)(2,1)}, u32[]{:S(2)}, u32[]{:S(2)}) collective-permute-start(f16[256,1024]{1,0:T(8,128)(2,1)} %get-tuple-element.64), channel_id=1, source_target_pairs={{0,1},{1,0},{2,3},{3,2},{4,5},{5,4},{6,7},{7,6},{8,9},{9,8},{10,11... | collective-permute-start | bytes 1572872 | tf_op jit(solution)/shard_map/ppermute | solution.py:43
  206.7 2.9 %collective-permute-start.28 = (f16[256,1024]{1,0:T(8,128)(2,1)}, f16[256,1024]{1,0:T(8,128)(2,1)}, u32[]{:S(2)}, u32[]{:S(2)}) collective-permute-start(f16[256,1024]{1,0:T(8,128)(2,1)} %get-tuple-element.66), channel_id=1, source_target_pairs={{0,6},{1,7},{2,0},{3,1},{4,2},{5,3},{6,4},{7,5},{8,14},{9,15},{10,... | collective-permute-start | bytes 1572872 | tf_op jit(solution)/shard_map/ppermute | solution.py:43
  211.5 2.2 collective-permute-done.25
  213.6 1.8 convert_add_fusion
  215.4 8.8 %collective-permute-done.26 = f16[256,1024]{1,0:T(8,128)(2,1)} collective-permute-done((f16[256,1024]{1,0:T(8,128)(2,1)}, f16[256,1024]{1,0:T(8,128)(2,1)}, u32[]{:S(2)}, u32[]{:S(2)}) %collective-permute-start.26) | collective-permute-done | bytes 524320 | tf_op jit(solution)/shard_map/ppermute | solution.py:43
  224.5 2.7 %multiply_convert_fusion.blocks = bf16[256,1024]{1,0:T(8,128)(2,1)} fusion(f32[256,1024]{1,0:T(8,128)S(1)} %bitcast.33, f16[256,1024]{1,0:T(8,128)(2,1)} %collective-permute-done.28, f16[256,1024]{1,0:T(8,128)(2,1)} %collective-permute-done.27, f32[256,1024]{1,0:T(8,128)S(1)} %convert_add_fusion, f16[256,1024]{1,0:T(8,128)(2,1)} %collective-permute-done.26, ...), kind=kLoop, calls=%fused_computation.35 | loop fusion | flops 2359296 | bytes 4194308 | tf_op jit(solution)/shard_map/convert_element_type | solution.py:355
  227.1 2.3 pick.1
  229.5 6.3 %all-to-all-start.4 = ((bf16[32,128,128]{2,1,0:T(8,128)(2,1)}), bf16[32,128,128]{2,1,0:T(8,128)(2,1)}, u32[]{:S(2)}, u32[]{:S(2)}) async-start(bf16[32,128,128]{2,1,0:T(8,128)(2,1)} %pick.1), calls=%async_computation.4 | async-start | bytes 2097152 | tf_op jit(solution)/shard_map/all_to_all | solution.py:26
  241.5 11.8 %all-to-all-done.4 = bf16[32,128,128]{2,1,0:T(8,128)(2,1)} async-done(((bf16[32,128,128]{2,1,0:T(8,128)(2,1)}), bf16[32,128,128]{2,1,0:T(8,128)(2,1)}, u32[]{:S(2)}, u32[]{:S(2)}) %all-to-all-start.4) | async-done | bytes 1048608 | tf_op jit(solution)/shard_map/all_to_all | solution.py:26
  253.3 2.1 fusion.3
  (147 shorter events, 33.6 us)
Async XLA Ops:
  3.3 15.9 %collective-permute-start = (bf16[272,1024]{1,0:T(8,128)(2,1)}, bf16[272,1024]{1,0:T(8,128)(2,1)S(1)}, u32[]{:S(2)}, u32[]{:S(2)}) collective-permute-start(bf16[272,1024]{1,0:T(8,128)(2,1)} %slab_body.1.refs_0_), channel_id=1, source_target_pairs={{0,1},{1,0},{2,3},{3,2},{4,5},{5,4},{6,7},{7,6},{8,9},{9,8},{10,11... | collective-permute-start | bytes 1671176 | tf_op jit(solution)/shard_map/ppermute | solution.py:30
  6.4 16.6 %collective-permute-start.1 = (bf16[272,1024]{1,0:T(8,128)(2,1)}, bf16[272,1024]{1,0:T(8,128)(2,1)S(1)}, u32[]{:S(2)}, u32[]{:S(2)}) collective-permute-start(bf16[272,1024]{1,0:T(8,128)(2,1)} %slab_body.1.refs_0_), channel_id=1, source_target_pairs={{0,2},{2,4},{4,6},{6,0},{1,3},{3,5},{5,7},{7,1},{8,10},{10,12},{12... | collective-permute-start | bytes 1671176 | tf_op jit(solution)/shard_map/ppermute | solution.py:288
  8.3 14.7 %collective-permute-start.2 = (bf16[272,1024]{1,0:T(8,128)(2,1)}, bf16[272,1024]{1,0:T(8,128)(2,1)S(1)}, u32[]{:S(2)}, u32[]{:S(2)}) collective-permute-start(bf16[272,1024]{1,0:T(8,128)(2,1)} %slab_body.1.refs_0_), channel_id=1, source_target_pairs={{0,6},{2,0},{4,2},{6,4},{1,7},{3,1},{5,3},{7,5},{8,14},{10,8},{12,... | collective-permute-start | bytes 1671176 | tf_op jit(solution)/shard_map/ppermute | solution.py:289
  19.2 13.6 %copy-start.2 = (bf16[272,1024]{1,0:T(8,128)(2,1)}, bf16[272,1024]{1,0:T(8,128)(2,1)S(1)}, u32[]{:S(2)}) copy-start(bf16[272,1024]{1,0:T(8,128)(2,1)S(1)} %collective-permute-done.refs_1_) | copy-start | bytes 1671172
  23.0 9.8 %copy-start.4 = (bf16[272,1024]{1,0:T(8,128)(2,1)}, bf16[272,1024]{1,0:T(8,128)(2,1)S(1)}, u32[]{:S(2)}) copy-start(bf16[272,1024]{1,0:T(8,128)(2,1)S(1)} %collective-permute-done.1.refs_3_.refs_6_) | copy-start | bytes 1671172
  23.0 9.8 %copy-start.6 = (bf16[272,1024]{1,0:T(8,128)(2,1)}, bf16[272,1024]{1,0:T(8,128)(2,1)S(1)}, u32[]{:S(2)}) copy-start(bf16[272,1024]{1,0:T(8,128)(2,1)S(1)} %collective-permute-done.2.refs_2_) | copy-start | bytes 1671172
  23.0 9.8 %collective-permute-start.7 = (bf16[1024,1024]{1,0:T(8,128)(2,1)}, bf16[1024,1024]{1,0:T(8,128)(2,1)S(1)}, u32[]{:S(2)}, u32[]{:S(2)}) collective-permute-start(bf16[1024,1024]{1,0:T(8,128)(2,1)} %mask_body.3), channel_id=1, source_target_pairs={{0,8},{8,0},{1,9},{9,1},{2,10},{10,2},{3,11},{11,3},{4,12},{12,4},... | collective-permute-start | bytes 6291464 | tf_op jit(solution)/shard_map/ppermute | solution.py:30
  23.1 5.4 %collective-permute-start.3 = (bf16[272,1024]{1,0:T(8,128)(2,1)S(1)}, bf16[272,1024]{1,0:T(8,128)(2,1)S(1)}, u32[]{:S(2)}, u32[]{:S(2)}) collective-permute-start(bf16[272,1024]{1,0:T(8,128)(2,1)S(1)} %copy-done), channel_id=1, source_target_pairs={{0,8},{8,0},{1,9},{9,1},{2,10},{10,2},{3,11},{11,3},{4,12},{12,4},... | collective-permute-start | bytes 1671176 | tf_op jit(solution)/shard_map/ppermute | solution.py:30
  23.6 7.7 %collective-permute-start.4 = (bf16[272,1024]{1,0:T(8,128)(2,1)S(1)}, bf16[272,1024]{1,0:T(8,128)(2,1)}, u32[]{:S(2)}, u32[]{:S(2)}) collective-permute-start(bf16[272,1024]{1,0:T(8,128)(2,1)S(1)} %collective-permute-done.refs_1_), channel_id=1, source_target_pairs={{0,8},{8,0},{1,9},{9,1},{2,10},{10,2},{3,11},{11,3},{4,12},{12,4},... | collective-permute-start | bytes 1671176 | tf_op jit(solution)/shard_map/ppermute | solution.py:30
  23.7 7.6 %collective-permute-start.6 = (bf16[272,1024]{1,0:T(8,128)(2,1)S(1)}, bf16[272,1024]{1,0:T(8,128)(2,1)}, u32[]{:S(2)}, u32[]{:S(2)}) collective-permute-start(bf16[272,1024]{1,0:T(8,128)(2,1)S(1)} %collective-permute-done.1.refs_3_.refs_6_), channel_id=1, source_target_pairs={{0,8},{8,0},{1,9},{9,1},{2,10},{10,2},{3,11},{11,3},{4,12},{12,4},... | collective-permute-start | bytes 1671176 | tf_op jit(solution)/shard_map/ppermute | solution.py:30
  24.1 7.9 %collective-permute-start.5 = (bf16[272,1024]{1,0:T(8,128)(2,1)S(1)}, bf16[272,1024]{1,0:T(8,128)(2,1)S(1)}, u32[]{:S(2)}, u32[]{:S(2)}) collective-permute-start(bf16[272,1024]{1,0:T(8,128)(2,1)S(1)} %collective-permute-done.2.refs_2_), channel_id=1, source_target_pairs={{0,8},{8,0},{1,9},{9,1},{2,10},{10,2},{3,11},{11,3},{4,12},{12,4},... | collective-permute-start | bytes 1671176 | tf_op jit(solution)/shard_map/ppermute | solution.py:30
  28.5 15.3 %collective-permute-start.8 = (bf16[272,1024]{1,0:T(8,128)(2,1)S(1)}, bf16[272,1024]{1,0:T(8,128)(2,1)S(1)}, u32[]{:S(2)}, u32[]{:S(2)}) collective-permute-start(bf16[272,1024]{1,0:T(8,128)(2,1)S(1)} %collective-permute-done.refs_1_), channel_id=1, source_target_pairs={{0,6},{2,0},{4,2},{6,4},{1,7},{3,1},{5,3},{7,5},{8,14},{10,8},{12,... | collective-permute-start | bytes 1671176 | tf_op jit(solution)/shard_map/ppermute | solution.py:294
  31.3 22.4 %collective-permute-start.9 = (bf16[272,1024]{1,0:T(8,128)(2,1)S(1)}, bf16[272,1024]{1,0:T(8,128)(2,1)S(1)}, u32[]{:S(2)}, u32[]{:S(2)}) collective-permute-start(bf16[272,1024]{1,0:T(8,128)(2,1)S(1)} %collective-permute-done.1.refs_3_.refs_6_), channel_id=1, source_target_pairs={{0,2},{2,4},{4,6},{6,0},{1,3},{3,5},{5,7},{7,1},{8,10},{10,12},{12... | collective-permute-start | bytes 1671176 | tf_op jit(solution)/shard_map/ppermute | solution.py:295
  31.3 27.7 %collective-permute-start.10 = (bf16[272,1024]{1,0:T(8,128)(2,1)S(1)}, bf16[272,1024]{1,0:T(8,128)(2,1)S(1)}, u32[]{:S(2)}, u32[]{:S(2)}) collective-permute-start(bf16[272,1024]{1,0:T(8,128)(2,1)S(1)} %collective-permute-done.refs_1_), channel_id=1, source_target_pairs={{0,2},{2,4},{4,6},{6,0},{1,3},{3,5},{5,7},{7,1},{8,10},{10,12},{12... | collective-permute-start | bytes 1671176 | tf_op jit(solution)/shard_map/ppermute | solution.py:296
  43.7 15.4 %copy-start.8 = (bf16[272,1024]{1,0:T(8,128)(2,1)}, bf16[272,1024]{1,0:T(8,128)(2,1)S(1)}, u32[]{:S(2)}) copy-start(bf16[272,1024]{1,0:T(8,128)(2,1)S(1)} %collective-permute-done.8.refs_0_.refs_3_) | copy-start | bytes 1671172
  45.7 15.4 %collective-permute-start.11 = (bf16[272,1024]{1,0:T(8,128)(2,1)S(1)}, bf16[272,1024]{1,0:T(8,128)(2,1)S(1)}, u32[]{:S(2)}, u32[]{:S(2)}) collective-permute-start(bf16[272,1024]{1,0:T(8,128)(2,1)S(1)} %collective-permute-done.8.refs_0_.refs_3_), channel_id=1, source_target_pairs={{0,6},{2,0},{4,2},{6,4},{1,7},{3,1},{5,3},{7,5},{8,14},{10,8},{12,... | collective-permute-start | bytes 1671176 | tf_op jit(solution)/shard_map/ppermute | solution.py:306
  53.7 31.5 %all-to-all-start = ((f16[8,1040,128]{2,1,0:T(8,128)(2,1)}), f16[8,1040,128]{2,1,0:T(8,128)(2,1)}, u32[]{:S(2)}, u32[]{:S(2)}) async-start(f16[8,1040,128]{2,1,0:T(8,128)(2,1)} %select_convert_fusion.1), calls=%async_computation | async-start | bytes 4259840 | tf_op jit(solution)/shard_map/all_to_all | solution.py:26
  59.1 2.0 collective-permute-start.13
  59.1 2.7 %collective-permute-start.12 = (bf16[272,1024]{1,0:T(8,128)(2,1)S(1)}, bf16[272,1024]{1,0:T(8,128)(2,1)S(1)}, u32[]{:S(2)}, u32[]{:S(2)}) collective-permute-start(bf16[272,1024]{1,0:T(8,128)(2,1)S(1)} %collective-permute-done.8.refs_0_.refs_3_), channel_id=1, source_target_pairs={{0,8},{8,0},{1,9},{9,1},{2,10},{10,2},{3,11},{11,3},{4,12},{12,4},... | collective-permute-start | bytes 1671176 | tf_op jit(solution)/shard_map/ppermute | solution.py:30
  59.6 3.0 %collective-permute-start.14 = (bf16[272,1024]{1,0:T(8,128)(2,1)S(1)}, bf16[272,1024]{1,0:T(8,128)(2,1)S(1)}, u32[]{:S(2)}, u32[]{:S(2)}) collective-permute-start(bf16[272,1024]{1,0:T(8,128)(2,1)S(1)} %collective-permute-done.9.refs_2_.refs_4_), channel_id=1, source_target_pairs={{0,8},{8,0},{1,9},{9,1},{2,10},{10,2},{3,11},{11,3},{4,12},{12,4},... | collective-permute-start | bytes 1671176 | tf_op jit(solution)/shard_map/ppermute | solution.py:30
  61.1 2.3 collective-permute-start.15
  79.6 9.4 %copy-start.27 = (s32[2,8]{1,0:T(2,128)S(1)}, s32[2,8]{1,0:T(2,128)}, u32[]{:S(2)}) copy-start(s32[2,8]{1,0:T(2,128)} %param.12) | copy-start | bytes 196
  85.2 30.2 %all-to-all-start.1 = ((f16[8,1040,128]{2,1,0:T(8,128)(2,1)}), f16[8,1040,128]{2,1,0:T(8,128)(2,1)S(1)}, u32[]{:S(2)}, u32[]{:S(2)}) async-start(f16[8,1040,128]{2,1,0:T(8,128)(2,1)} %select_convert_fusion), calls=%async_computation.1 | async-start | bytes 4259840 | tf_op jit(solution)/shard_map/all_to_all | solution.py:26
  119.7 30.0 %all-to-all-start.2 = ((bf16[8,1024,128]{2,1,0:T(8,128)(2,1)}), bf16[8,1024,128]{2,1,0:T(8,128)(2,1)}, u32[]{:S(2)}, u32[]{:S(2)}) async-start(bf16[8,1024,128]{2,1,0:T(8,128)(2,1)} %broadcast_in_dim.90), calls=%async_computation.2 | async-start | bytes 4194304 | tf_op jit(solution)/shard_map/all_to_all | solution.py:26
  125.4 1.2 collective-permute-start.16
  126.7 5.1 %collective-permute-start.17 = (f32[8,128]{1,0:T(8,128)S(1)}, f32[8,128]{1,0:T(8,128)S(1)}, u32[]{:S(2)}, u32[]{:S(2)}) collective-permute-start(f32[8,128]{1,0:T(8,128)S(1)} %broadcast_maximum_fusion), channel_id=1, source_target_pairs={{0,4},{2,6},{4,0},{6,2},{1,5},{3,7},{5,1},{7,3},{8,12},{10,14},{12... | collective-permute-start | bytes 12296 | tf_op jit(solution)/shard_map/ppermute | solution.py:328
  131.8 4.8 %collective-permute-start.18 = (f32[8,128]{1,0:T(8,128)S(1)}, f32[8,128]{1,0:T(8,128)S(1)}, u32[]{:S(2)}, u32[]{:S(2)}) collective-permute-start(f32[8,128]{1,0:T(8,128)S(1)} %fusion.22), channel_id=1, source_target_pairs={{0,2},{2,4},{4,6},{6,0},{1,3},{3,5},{5,7},{7,1},{8,10},{10,12},{12... | collective-permute-start | bytes 12296 | tf_op jit(solution)/shard_map/ppermute | solution.py:329
  136.6 11.2 %collective-permute-start.19 = (f32[8,128]{1,0:T(8,128)S(1)}, f32[8,128]{1,0:T(8,128)S(1)}, u32[]{:S(2)}, u32[]{:S(2)}) collective-permute-start(f32[8,128]{1,0:T(8,128)S(1)} %max.33), channel_id=1, source_target_pairs={{0,1},{1,0},{2,3},{3,2},{4,5},{5,4},{6,7},{7,6},{8,9},{9,8},{10,11... | collective-permute-start | bytes 12296 | tf_op jit(solution)/shard_map/ppermute | solution.py:30
  149.7 4.5 %collective-permute-start.20 = (bf16[8,1024,128]{2,1,0:T(8,128)(2,1)}, bf16[8,1024,128]{2,1,0:T(8,128)(2,1)}, u32[]{:S(2)}, u32[]{:S(2)}) collective-permute-start(bf16[8,1024,128]{2,1,0:T(8,128)(2,1)} %all-to-all-done.2.mine), channel_id=1, source_target_pairs={{0,8},{8,0},{1,9},{9,1},{2,10},{10,2},{3,11},{11,3},{4,12},{12,4},... | collective-permute-start | bytes 6291464 | tf_op jit(solution)/shard_map/ppermute | solution.py:30
  149.7 31.9 %all-to-all-start.3 = ((bf16[8,1024,128]{2,1,0:T(8,128)(2,1)}), bf16[8,1024,128]{2,1,0:T(8,128)(2,1)S(1)}, u32[]{:S(2)}, u32[]{:S(2)}) async-start(bf16[8,1024,128]{2,1,0:T(8,128)(2,1)} %broadcast_in_dim.51), calls=%async_computation.3 | async-start | bytes 4194304 | tf_op jit(solution)/shard_map/all_to_all | solution.py:26
  163.3 18.4 %copy-start.1 = (bf16[272,1024]{1,0:T(8,128)(2,1)S(1)}, bf16[272,1024]{1,0:T(8,128)(2,1)}, u32[]{:S(2)}) copy-start(bf16[272,1024]{1,0:T(8,128)(2,1)} %slab_body.1.refs_0_) | copy-start | bytes 1671172
  163.3 18.5 %copy-start.28 = (s32[1,1,16,1]{2,3,1,0:T(1,128)S(1)}, s32[1,1,16,1]{2,3,1,0:T(1,128)}, u32[]{:S(2)}) copy-start(s32[1,1,16,1]{2,3,1,0:T(1,128)} %param.13) | copy-start | bytes 196
  166.1 15.4 %collective-permute-start.21 = (f16[256,1024]{1,0:T(8,128)(2,1)}, f16[256,1024]{1,0:T(8,128)(2,1)}, u32[]{:S(2)}, u32[]{:S(2)}) collective-permute-start(f16[256,1024]{1,0:T(8,128)(2,1)} %get-tuple-element.91), channel_id=1, source_target_pairs={{0,6},{2,0},{4,2},{6,4},{1,7},{3,1},{5,3},{7,5},{8,14},{10,8},{12,... | collective-permute-start | bytes 1572872 | tf_op jit(solution)/shard_map/ppermute | solution.py:338
  166.6 15.1 %collective-permute-start.22 = (f16[256,1024]{1,0:T(8,128)(2,1)}, f16[256,1024]{1,0:T(8,128)(2,1)S(1)}, u32[]{:S(2)}, u32[]{:S(2)}) collective-permute-start(f16[256,1024]{1,0:T(8,128)(2,1)} %get-tuple-element.90), channel_id=1, source_target_pairs={{0,2},{2,4},{4,6},{6,0},{1,3},{3,5},{5,7},{7,1},{8,10},{10,12},{12... | collective-permute-start | bytes 1572872 | tf_op jit(solution)/shard_map/ppermute | solution.py:338
  181.7 8.5 %collective-permute-start.23 = (bf16[8,1024,128]{2,1,0:T(8,128)(2,1)S(1)}, bf16[8,1024,128]{2,1,0:T(8,128)(2,1)}, u32[]{:S(2)}, u32[]{:S(2)}) collective-permute-start(bf16[8,1024,128]{2,1,0:T(8,128)(2,1)S(1)} %all-to-all-done.3.mine), channel_id=1, source_target_pairs={{0,8},{8,0},{1,9},{9,1},{2,10},{10,2},{3,11},{11,3},{4,12},{12,4},... | collective-permute-start | bytes 6291464 | tf_op jit(solution)/shard_map/ppermute | solution.py:30
  185.7 25.8 %collective-permute-start.24 = (f16[256,1024]{1,0:T(8,128)(2,1)}, f16[256,1024]{1,0:T(8,128)(2,1)}, u32[]{:S(2)}, u32[]{:S(2)}) collective-permute-start(f16[256,1024]{1,0:T(8,128)(2,1)} %get-tuple-element.84), channel_id=1, source_target_pairs={{0,7},{1,6},{2,1},{3,0},{4,3},{5,2},{6,5},{7,4},{8,15},{9,14},{10,... | collective-permute-start | bytes 1572872 | tf_op jit(solution)/shard_map/ppermute | solution.py:43
  188.3 25.3 %collective-permute-start.25 = (f16[256,1024]{1,0:T(8,128)(2,1)}, f16[256,1024]{1,0:T(8,128)(2,1)}, u32[]{:S(2)}, u32[]{:S(2)}) collective-permute-start(f16[256,1024]{1,0:T(8,128)(2,1)} %get-tuple-element.85), channel_id=1, source_target_pairs={{0,3},{1,2},{2,5},{3,4},{4,7},{5,6},{6,1},{7,0},{8,11},{9,10},{10,... | collective-permute-start | bytes 1572872 | tf_op jit(solution)/shard_map/ppermute | solution.py:43
  199.2 10.4 %copy-start.3 = (bf16[272,1024]{1,0:T(8,128)(2,1)S(1)}, bf16[272,1024]{1,0:T(8,128)(2,1)}, u32[]{:S(2)}) copy-start(bf16[272,1024]{1,0:T(8,128)(2,1)} %copy-done.2) | copy-start | bytes 1671172
  199.2 10.4 %copy-start.5 = (bf16[272,1024]{1,0:T(8,128)(2,1)S(1)}, bf16[272,1024]{1,0:T(8,128)(2,1)}, u32[]{:S(2)}) copy-start(bf16[272,1024]{1,0:T(8,128)(2,1)} %copy-done.4) | copy-start | bytes 1671172
  199.2 10.4 %copy-start.7 = (bf16[272,1024]{1,0:T(8,128)(2,1)S(1)}, bf16[272,1024]{1,0:T(8,128)(2,1)}, u32[]{:S(2)}) copy-start(bf16[272,1024]{1,0:T(8,128)(2,1)} %copy-done.6) | copy-start | bytes 1671172
  199.2 11.1 %copy-start.9 = (bf16[272,1024]{1,0:T(8,128)(2,1)S(1)}, bf16[272,1024]{1,0:T(8,128)(2,1)}, u32[]{:S(2)}) copy-start(bf16[272,1024]{1,0:T(8,128)(2,1)} %copy-done.8) | copy-start | bytes 1671172
  199.3 11.1 %copy-start.11 = (bf16[272,1024]{1,0:T(8,128)(2,1)S(1)}, bf16[272,1024]{1,0:T(8,128)(2,1)}, u32[]{:S(2)}) copy-start(bf16[272,1024]{1,0:T(8,128)(2,1)} %copy-done.10) | copy-start | bytes 1671172
  203.7 20.5 %collective-permute-start.26 = (f16[256,1024]{1,0:T(8,128)(2,1)}, f16[256,1024]{1,0:T(8,128)(2,1)}, u32[]{:S(2)}, u32[]{:S(2)}) collective-permute-start(f16[256,1024]{1,0:T(8,128)(2,1)} %get-tuple-element.64), channel_id=1, source_target_pairs={{0,1},{1,0},{2,3},{3,2},{4,5},{5,4},{6,7},{7,6},{8,9},{9,8},{10,11... | collective-permute-start | bytes 1572872 | tf_op jit(solution)/shard_map/ppermute | solution.py:43
  206.4 18.1 %collective-permute-start.27 = (f16[256,1024]{1,0:T(8,128)(2,1)}, f16[256,1024]{1,0:T(8,128)(2,1)}, u32[]{:S(2)}, u32[]{:S(2)}) collective-permute-start(f16[256,1024]{1,0:T(8,128)(2,1)} %get-tuple-element.65), channel_id=1, source_target_pairs={{0,2},{1,3},{2,4},{3,5},{4,6},{5,7},{6,0},{7,1},{8,10},{9,11},{10,... | collective-permute-start | bytes 1572872 | tf_op jit(solution)/shard_map/ppermute | solution.py:43
  206.7 17.8 %collective-permute-start.28 = (f16[256,1024]{1,0:T(8,128)(2,1)}, f16[256,1024]{1,0:T(8,128)(2,1)}, u32[]{:S(2)}, u32[]{:S(2)}) collective-permute-start(f16[256,1024]{1,0:T(8,128)(2,1)} %get-tuple-element.66), channel_id=1, source_target_pairs={{0,6},{1,7},{2,0},{3,1},{4,2},{5,3},{6,4},{7,5},{8,14},{9,15},{10,... | collective-permute-start | bytes 1572872 | tf_op jit(solution)/shard_map/ppermute | solution.py:43
  211.5 13.0 %copy-start.18 = (f32[32,8,8,128]{3,1,2,0:T(8,128)S(1)}, f32[32,8,8,128]{3,1,2,0:T(8,128)}, u32[]{:S(2)}) copy-start(f32[32,8,8,128]{3,1,2,0:T(8,128)} %copy.19) | copy-start | bytes 3145732
  229.5 23.8 %all-to-all-start.4 = ((bf16[32,128,128]{2,1,0:T(8,128)(2,1)}), bf16[32,128,128]{2,1,0:T(8,128)(2,1)}, u32[]{:S(2)}, u32[]{:S(2)}) async-start(bf16[32,128,128]{2,1,0:T(8,128)(2,1)} %pick.1), calls=%async_computation.4 | async-start | bytes 2097152 | tf_op jit(solution)/shard_map/all_to_all | solution.py:26
  240.6 12.6 %copy-start.20 = (bf16[1,1,3,32,128,128]{5,4,3,2,1,0:T(8,128)(2,1)S(1)}, bf16[1,1,3,32,128,128]{5,4,3,2,1,0:T(8,128)(2,1)}, u32[]{:S(2)}) copy-start(bf16[1,1,3,32,128,128]{5,4,3,2,1,0:T(8,128)(2,1)} %param.14) | copy-start | bytes 9437188
  (15 other events, 45.5 us)

commit v4 on v3

--- a/solution.py
+++ b/solution.py
@@ -155,12 +155,12 @@
 
 def dot_specs(operands, width):
     whole = [pl.BlockSpec(v.shape, lambda n, rank=v.ndim: (0,) * rank) for v in operands]
-    return whole + [pl.BlockSpec((width, 2 * BLOCK), lambda n: (0, n))] * 2
+    return whole + [pl.BlockSpec((width, 4 * BLOCK), lambda n: (0, n))] * 2
 
 
 def h_dot(mine, other, w_mine, w_other):
     width = w_mine.shape[0]
-    tile = 2 * BLOCK
+    tile = 4 * BLOCK
     steps = width // tile
     return pl.pallas_call(
         h_dot_body,
@@ -171,18 +171,18 @@
         grid=(steps,),
         in_specs=dot_specs(mine + other, width),
         out_specs=(
-            pl.BlockSpec((2, width + PAD, BLOCK), lambda n: (n, 0, 0)),
+            pl.BlockSpec((4, width + PAD, BLOCK), lambda n: (n, 0, 0)),
             pl.BlockSpec((1, 8, tile), lambda n: (n, 0, 0)),
         ),
         cost_estimate=COST,
         compiler_params=ROOM,
         name="h_dot",
-    )(*mine, *other, w_mine, w_other)
+    )(*[pltpu.with_memory_space_constraint(v, pltpu.HBM) for v in (*mine, *other, w_mine, w_other)])
 
 
 def p_dot(mine, other, w_mine, w_other):
     width = w_mine.shape[0]
-    tile = 2 * BLOCK
+    tile = 4 * BLOCK
     return pl.pallas_call(
         p_dot_body,
         out_shape=jax.ShapeDtypeStruct((width, width), F32),

time: 258 us -> 257 us (level)
  transfers between devices with their start and end apart: 34 -> 34, of which waited for: 23 -> 22; matrix products, arithmetic and copies ran while one was open for 15% -> 15% of each run, Pallas kernels for 21% -> 20%
where the time goes in v4:
time: 257 us; the launch traced here: 256 us
  waiting for transfers between devices  85.7 us (33%)
  Pallas kernels  56.9 us (22%)
  starting transfers between devices  54.1 us (21%)
  other arithmetic  40.5 us (16%)
  local copies, waits for them, and re-layouts  13.6 us (5%)
  between operations  5.1 us (2%)
    all_to_all x5, waiting for transfers between devices, exchange(): return lax.all_to_all(pieces, axes, split_axis=0, concat_axis=0, tiled=True)  40.2 us
    all_to_all x5, starting transfers between devices, exchange(): return lax.all_to_all(pieces, axes, split_axis=0, concat_axis=0, tiled=True)  23.3 us
    pallas_call x5, Pallas kernels, call_mask(): pl.pallas_call(body, out_shape=jax.ShapeDtypeStruct((height, shape[1]), B...  18.1 us
    pallas_call x2, Pallas kernels, p_dot(): pl.pallas_call(p_dot_body, out_shape=jax.ShapeDtypeStruct((width, width),...  17.8 us
    pallas_call x2, Pallas kernels, h_dot(): pl.pallas_call(h_dot_body, out_shape=(jax.ShapeDtypeStruct((CBLK, width +...  17.8 us
    ppermute x14, waiting for transfers between devices, flip(): return lax.ppermute(v, axis, [(0, 1), (1, 0)])  17.6 us
    ppermute x5, waiting for transfers between devices, shifted(): return lax.ppermute(v, COL, pairs)  11.2 us
    ppermute x5, starting transfers between devices, shifted(): return lax.ppermute(v, COL, pairs)  10.4 us
  transfers between devices with their start and end apart: 34, of which 22 were waited for; matrix products, arithmetic and copies ran while one was open for 15% of the time, Pallas kernels for 20%

profile of v4, /device:TPU:0, one launch (start us, length us, event | category | flops | bytes accessed | tf_op | source)
XLA Modules:
  0.0 255.9 jit_solution(10176393461315857748)
XLA Ops:
  0.6 2.6 %slab_body.1.refs_0_ = bf16[272,1024]{1,0:T(8,128)(2,1)} custom-call(s32[16]{0:T(128)} %bitcast.45, s32[8,16]{1,0:T(8,128)} %bitcast.36, bf16[2048,1024]{1,0:T(8,128)(2,1)} %src.7), custom_call_target="tpu_custom_call" | custom-call | tf_op jit(solution)/shard_map/slab_body/pallas_call | solution.py:102
  3.3 3.1 %collective-permute-start = (bf16[272,1024]{1,0:T(8,128)(2,1)}, bf16[272,1024]{1,0:T(8,128)(2,1)S(1)}, u32[]{:S(2)}, u32[]{:S(2)}) collective-permute-start(bf16[272,1024]{1,0:T(8,128)(2,1)} %slab_body.1.refs_0_), channel_id=1, source_target_pairs={{0,1},{1,0},{2,3},{3,2},{4,5},{5,4},{6,7},{7,6},{8,9},{9,8},{10,11... | collective-permute-start | bytes 1671176 | tf_op jit(solution)/shard_map/ppermute | solution.py:30
  6.4 1.9 collective-permute-start.1
  8.3 2.1 collective-permute-start.2
  11.0 3.9 %mask_body.2.refs_8_ = bf16[1024,1024]{1,0:T(8,128)(2,1)} custom-call(s32[2]{0:T(128)} %get-tuple-element.93.corner, s32[8,16]{1,0:T(8,128)} %pattern.3, bf16[1024,2048]{1,0:T(8,128)(2,1)} %src.5), custom_call_target="tpu_custom_call" | custom-call | tf_op jit(solution)/shard_map/mask_body/pallas_call | solution.py:102
  14.9 3.9 %mask_body.3 = bf16[1024,1024]{1,0:T(8,128)(2,1)} custom-call(s32[2]{0:T(128)} %get-tuple-element.92.corner, s32[8,16]{1,0:T(8,128)} %pattern.3, bf16[1024,2048]{1,0:T(8,128)(2,1)} %src.5), custom_call_target="tpu_custom_call" | custom-call | tf_op jit(solution)/shard_map/mask_body/pallas_call | solution.py:102
  19.2 3.8 %collective-permute-done.1.refs_3_.refs_6_ = bf16[272,1024]{1,0:T(8,128)(2,1)S(1)} collective-permute-done((bf16[272,1024]{1,0:T(8,128)(2,1)}, bf16[272,1024]{1,0:T(8,128)(2,1)S(1)}, u32[]{:S(2)}, u32[]{:S(2)}) %collective-permute-start.1) | collective-permute-done | bytes 557088 | tf_op jit(solution)/shard_map/ppermute | solution.py:288
  24.2 4.3 %collective-permute-done.3.refs_4_ = bf16[272,1024]{1,0:T(8,128)(2,1)S(1)} collective-permute-done((bf16[272,1024]{1,0:T(8,128)(2,1)S(1)}, bf16[272,1024]{1,0:T(8,128)(2,1)S(1)}, u32[]{:S(2)}, u32[]{:S(2)}) %collective-permute-start.3) | collective-permute-done | bytes 557088 | tf_op jit(solution)/shard_map/ppermute | solution.py:30
  28.5 2.9 %collective-permute-start.8 = (bf16[272,1024]{1,0:T(8,128)(2,1)S(1)}, bf16[272,1024]{1,0:T(8,128)(2,1)S(1)}, u32[]{:S(2)}, u32[]{:S(2)}) collective-permute-start(bf16[272,1024]{1,0:T(8,128)(2,1)S(1)} %collective-permute-done.refs_1_), channel_id=1, source_target_pairs={{0,6},{2,0},{4,2},{6,4},{1,7},{3,1},{5,3},{7,5},{8,14},{10,8},{12,... | collective-permute-start | bytes 1671176 | tf_op jit(solution)/shard_map/ppermute | solution.py:294
  34.2 8.9 %h_dot.2 = (f32[8,1040,128]{2,1,0:T(8,128)}, f32[2,8,512]{2,1,0:T(8,128)}) custom-call(bf16[272,1024]{1,0:T(8,128)(2,1)} %slab_body.1.refs_0_, bf16[272,1024]{1,0:T(8,128)(2,1)} %copy-done.2, bf16[272,1024]{1,0:T(8,128)(2,1)} %copy-done.6, bf16[272,1024]{1,0:T(8,128)(2,1)} %copy-done.4, bf16[272,1024]{1,0:T(8,128)(2,1)} %copy-done.21, ...), custom_call_target="tpu_custom_call" | custom-call | flops 1048576 | bytes 1048576 | tf_op jit(solution)/shard_map/h_dot/pallas_call | solution.py:165
  45.7 3.8 %collective-permute-start.11 = (bf16[272,1024]{1,0:T(8,128)(2,1)S(1)}, bf16[272,1024]{1,0:T(8,128)(2,1)S(1)}, u32[]{:S(2)}, u32[]{:S(2)}) collective-permute-start(bf16[272,1024]{1,0:T(8,128)(2,1)S(1)} %collective-permute-done.8.refs_0_.refs_3_), channel_id=1, source_target_pairs={{0,6},{2,0},{4,2},{6,4},{1,7},{3,1},{5,3},{7,5},{8,14},{10,8},{12,... | collective-permute-start | bytes 1671176 | tf_op jit(solution)/shard_map/ppermute | solution.py:306
  49.5 4.2 %select_convert_fusion.1 = f16[8,1040,128]{2,1,0:T(8,128)(2,1)} fusion(f32[8,1040,128]{2,1,0:T(8,128)} %get-tuple-element.40, f32[]{:T(128)S(6)} %add.78, f32[]{:T(128)S(6)} %exp2.41, pred[1040]{0:T(1024)(128)(4,1)S(1)} %iota_compare_fusion.3), kind=kLoop, calls=%fused_computation.1 | loop fusion | flops 3194880 | bytes 6390808 | tf_op jit(solution)/shard_map/convert_element_type | solution.py:54
  53.7 4.5 %all-to-all-start = ((f16[8,1040,128]{2,1,0:T(8,128)(2,1)}), f16[8,1040,128]{2,1,0:T(8,128)(2,1)}, u32[]{:S(2)}, u32[]{:S(2)}) async-start(f16[8,1040,128]{2,1,0:T(8,128)(2,1)} %select_convert_fusion.1), calls=%async_computation | async-start | bytes 4259840 | tf_op jit(solution)/shard_map/all_to_all | solution.py:26
  64.3 8.9 %h_dot.3 = (f32[8,1040,128]{2,1,0:T(8,128)}, f32[2,8,512]{2,1,0:T(8,128)}) custom-call(bf16[272,1024]{1,0:T(8,128)(2,1)} %copy-done.8, bf16[272,1024]{1,0:T(8,128)(2,1)} %copy-done.12, bf16[272,1024]{1,0:T(8,128)(2,1)} %copy-done.10, bf16[272,1024]{1,0:T(8,128)(2,1)} %copy-done.14, bf16[272,1024]{1,0:T(8,128)(2,1)} %copy-done.24, ...), custom_call_target="tpu_custom_call" | custom-call | flops 1048576 | bytes 1048576 | tf_op jit(solution)/shard_map/h_dot/pallas_call | solution.py:165
  75.2 4.2 %select_convert_fusion = f16[8,1040,128]{2,1,0:T(8,128)(2,1)} fusion(f32[8,1040,128]{2,1,0:T(8,128)} %get-tuple-element.47, f32[]{:T(128)S(6)} %add.79, f32[]{:T(128)S(6)} %exp2.43, pred[1040]{0:T(1024)(128)(4,1)S(1)} %iota_compare_fusion.3), kind=kLoop, calls=%fused_computation | loop fusion | flops 3194880 | bytes 6390808 | tf_op jit(solution)/shard_map/convert_element_type | solution.py:54
  79.4 5.7 %all-to-all-done = f16[8,1040,128]{2,1,0:T(8,128)(2,1)} async-done(((f16[8,1040,128]{2,1,0:T(8,128)(2,1)}), f16[8,1040,128]{2,1,0:T(8,128)(2,1)}, u32[]{:S(2)}, u32[]{:S(2)}) %all-to-all-start) | async-done | bytes 2129952 | tf_op jit(solution)/shard_map/all_to_all | solution.py:26
  85.2 3.8 %all-to-all-start.1 = ((f16[8,1040,128]{2,1,0:T(8,128)(2,1)}), f16[8,1040,128]{2,1,0:T(8,128)(2,1)S(1)}, u32[]{:S(2)}, u32[]{:S(2)}) async-start(f16[8,1040,128]{2,1,0:T(8,128)(2,1)} %select_convert_fusion), calls=%async_computation.1 | async-start | bytes 4259840 | tf_op jit(solution)/shard_map/all_to_all | solution.py:26
  91.1 3.8 %turned_body.2.w_mine = bf16[1024,1024]{1,0:T(8,128)(2,1)} custom-call(s32[2]{0:T(128)} %get-tuple-element.95.corner, s32[8,16]{1,0:T(8,128)} %bitcast.37, bf16[2048,1024]{1,0:T(8,128)(2,1)} %src.7), custom_call_target="tpu_custom_call" | custom-call | tf_op jit(solution)/shard_map/turned_body/pallas_call | solution.py:102
  95.0 3.8 %turned_body.3.w_other = bf16[1024,1024]{1,0:T(8,128)(2,1)} custom-call(s32[2]{0:T(128)} %get-tuple-element.94.corner, s32[8,16]{1,0:T(8,128)} %bitcast.38, bf16[2048,1024]{1,0:T(8,128)(2,1)} %src.7), custom_call_target="tpu_custom_call" | custom-call | tf_op jit(solution)/shard_map/turned_body/pallas_call | solution.py:102
  98.8 3.8 %abs_reduce_fusion = bf16[]{:T(256)} fusion(bf16[2048,1024]{1,0:T(8,128)(2,1)} %src.7), kind=kLoop, calls=%fused_computation.3 | loop fusion | flops 4194303 | bytes 4194306 | tf_op jit(solution)/shard_map/reduce_max | solution.py:317
  104.7 2.1 multiply_reduce_fusion.1
  106.8 8.6 %all-to-all-done.1 = f16[8,1040,128]{2,1,0:T(8,128)(2,1)S(1)} async-done(((f16[8,1040,128]{2,1,0:T(8,128)(2,1)}), f16[8,1040,128]{2,1,0:T(8,128)(2,1)S(1)}, u32[]{:S(2)}, u32[]{:S(2)}) %all-to-all-start.1) | async-done | bytes 2129952 | tf_op jit(solution)/shard_map/all_to_all | solution.py:26
  115.3 1.7 broadcast_in_dim.51
  119.7 4.3 %all-to-all-start.2 = ((bf16[8,1024,128]{2,1,0:T(8,128)(2,1)}), bf16[8,1024,128]{2,1,0:T(8,128)(2,1)}, u32[]{:S(2)}, u32[]{:S(2)}) async-start(bf16[8,1024,128]{2,1,0:T(8,128)(2,1)} %broadcast_in_dim.90), calls=%async_computation.2 | async-start | bytes 4194304 | tf_op jit(solution)/shard_map/all_to_all | solution.py:26
  126.7 5.1 %collective-permute-done.17 = f32[8,128]{1,0:T(8,128)S(1)} collective-permute-done((f32[8,128]{1,0:T(8,128)S(1)}, f32[8,128]{1,0:T(8,128)S(1)}, u32[]{:S(2)}, u32[]{:S(2)}) %collective-permute-start.17) | collective-permute-done | bytes 4128 | tf_op jit(solution)/shard_map/ppermute | solution.py:328
  131.8 4.8 %collective-permute-done.18 = f32[8,128]{1,0:T(8,128)S(1)} collective-permute-done((f32[8,128]{1,0:T(8,128)S(1)}, f32[8,128]{1,0:T(8,128)S(1)}, u32[]{:S(2)}, u32[]{:S(2)}) %collective-permute-start.18) | collective-permute-done | bytes 4128 | tf_op jit(solution)/shard_map/ppermute | solution.py:329
  136.6 2.0 collective-permute-start.19
  138.6 9.2 %collective-permute-done.19 = f32[8,128]{1,0:T(8,128)S(1)} collective-permute-done((f32[8,128]{1,0:T(8,128)S(1)}, f32[8,128]{1,0:T(8,128)S(1)}, u32[]{:S(2)}, u32[]{:S(2)}) %collective-permute-start.19) | collective-permute-done | bytes 4128 | tf_op jit(solution)/shard_map/ppermute | solution.py:30
  149.7 4.2 %all-to-all-start.3 = ((bf16[8,1024,128]{2,1,0:T(8,128)(2,1)}), bf16[8,1024,128]{2,1,0:T(8,128)(2,1)S(1)}, u32[]{:S(2)}, u32[]{:S(2)}) async-start(bf16[8,1024,128]{2,1,0:T(8,128)(2,1)} %broadcast_in_dim.51), calls=%async_computation.3 | async-start | bytes 4194304 | tf_op jit(solution)/shard_map/all_to_all | solution.py:26
  154.2 8.9 %p_dot.2 = f32[1024,1024]{1,0:T(8,128)} custom-call(bf16[8,1024,128]{2,1,0:T(8,128)(2,1)} %all-to-all-done.2.mine, bf16[8,1024,128]{2,1,0:T(8,128)(2,1)} %collective-permute-done.20.other, bf16[1024,1024]{1,0:T(8,128)(2,1)} %turned_body.2.w_mine, bf16[1024,1024]{1,0:T(8,128)(2,1)} %turned_body.3.w_other), custom_call_target="tpu_custom_call" | custom-call | flops 1048576 | bytes 1048576 | tf_op jit(solution)/shard_map/p_dot/pallas_call | solution.py:186
  163.1 2.9 %fusion.13 = (f16[256,1024]{1,0:T(8,128)(2,1)}, f16[256,1024]{1,0:T(8,128)(2,1)}) fusion(f32[1024,1024]{1,0:T(8,128)} %p_dot.2, f32[]{:T(128)S(6)} %exp2.49), kind=kLoop, calls=%fused_computation.32 | loop fusion | flops 1048576 | bytes 3145732 | tf_op jit(solution)/shard_map/convert_element_type | solution.py:339
  166.3 1.7 collective-permute-start.22
  168.0 13.5 %all-to-all-done.3.mine = bf16[8,1024,128]{2,1,0:T(8,128)(2,1)S(1)} async-done(((bf16[8,1024,128]{2,1,0:T(8,128)(2,1)}), bf16[8,1024,128]{2,1,0:T(8,128)(2,1)S(1)}, u32[]{:S(2)}, u32[]{:S(2)}) %all-to-all-start.3) | async-done | bytes 2097184 | tf_op jit(solution)/shard_map/all_to_all | solution.py:26
  182.8 2.9 %fusion.8 = (f16[256,1024]{1,0:T(8,128)(2,1)}, f16[256,1024]{1,0:T(8,128)(2,1)}) fusion(f32[1024,1024]{1,0:T(8,128)} %p_dot.2, f32[]{:T(128)S(6)} %exp2.49, f16[256,1024]{1,0:T(8,128)(2,1)S(1)} %collective-permute-done.22), kind=kLoop, calls=%fused_computation.22 | loop fusion | flops 1572864 | bytes 3670020 | tf_op jit(solution)/shard_map/convert_element_type | solution.py:343
  185.7 2.5 collective-permute-start.24
  188.2 1.9 collective-permute-start.25
  190.1 8.9 %p_dot.3 = f32[1024,1024]{1,0:T(8,128)} custom-call(bf16[8,1024,128]{2,1,0:T(8,128)(2,1)} %copy-done.16, bf16[8,1024,128]{2,1,0:T(8,128)(2,1)} %collective-permute-done.23.other, bf16[1024,1024]{1,0:T(8,128)(2,1)} %turned_body.2.w_mine, bf16[1024,1024]{1,0:T(8,128)(2,1)} %turned_body.3.w_other), custom_call_target="tpu_custom_call" | custom-call | flops 1048576 | bytes 1048576 | tf_op jit(solution)/shard_map/p_dot/pallas_call | solution.py:186
  199.1 4.4 %fusion.10 = (f16[256,1024]{1,0:T(8,128)(2,1)}, f16[256,1024]{1,0:T(8,128)(2,1)}, f16[256,1024]{1,0:T(8,128)(2,1)}, f32[256,1024]{1,0:T(8,128)}) fusion(f32[1024,1024]{1,0:T(8,128)} %p_dot.3, f16[256,1024]{1,0:T(8,128)(2,1)} %collective-permute-done.21, f32[]{:T(128)S(6)} %exp2.49), kind=kLoop, calls=%fused_computation.25 | loop fusion | flops 2359296 | bytes 7340036 | tf_op jit(solution)/shard_map/convert_element_type | solution.py:348
  203.5 2.8 %collective-permute-start.26 = (f16[256,1024]{1,0:T(8,128)(2,1)}, f16[256,1024]{1,0:T(8,128)(2,1)}, u32[]{:S(2)}, u32[]{:S(2)}) collective-permute-start(f16[256,1024]{1,0:T(8,128)(2,1)} %get-tuple-element.64), channel_id=1, source_target_pairs={{0,1},{1,0},{2,3},{3,2},{4,5},{5,4},{6,7},{7,6},{8,9},{9,8},{10,11... | collective-permute-start | bytes 1572872 | tf_op jit(solution)/shard_map/ppermute | solution.py:43
  206.3 3.1 %collective-permute-start.28 = (f16[256,1024]{1,0:T(8,128)(2,1)}, f16[256,1024]{1,0:T(8,128)(2,1)}, u32[]{:S(2)}, u32[]{:S(2)}) collective-permute-start(f16[256,1024]{1,0:T(8,128)(2,1)} %get-tuple-element.66), channel_id=1, source_target_pairs={{0,6},{1,7},{2,0},{3,1},{4,2},{5,3},{6,4},{7,5},{8,14},{9,15},{10,... | collective-permute-start | bytes 1572872 | tf_op jit(solution)/shard_map/ppermute | solution.py:43
  211.3 2.2 collective-permute-done.25
  213.5 1.8 convert_add_fusion
  215.2 8.8 %collective-permute-done.26 = f16[256,1024]{1,0:T(8,128)(2,1)} collective-permute-done((f16[256,1024]{1,0:T(8,128)(2,1)}, f16[256,1024]{1,0:T(8,128)(2,1)}, u32[]{:S(2)}, u32[]{:S(2)}) %collective-permute-start.26) | collective-permute-done | bytes 524320 | tf_op jit(solution)/shard_map/ppermute | solution.py:43
  224.3 2.7 %multiply_convert_fusion.blocks = bf16[256,1024]{1,0:T(8,128)(2,1)} fusion(f32[256,1024]{1,0:T(8,128)S(1)} %bitcast.33, f16[256,1024]{1,0:T(8,128)(2,1)} %collective-permute-done.28, f16[256,1024]{1,0:T(8,128)(2,1)} %collective-permute-done.27, f32[256,1024]{1,0:T(8,128)S(1)} %convert_add_fusion, f16[256,1024]{1,0:T(8,128)(2,1)} %collective-permute-done.26, ...), kind=kLoop, calls=%fused_computation.35 | loop fusion | flops 2359296 | bytes 4194308 | tf_op jit(solution)/shard_map/convert_element_type | solution.py:355
  227.0 2.3 pick.1
  229.3 6.4 %all-to-all-start.4 = ((bf16[32,128,128]{2,1,0:T(8,128)(2,1)}), bf16[32,128,128]{2,1,0:T(8,128)(2,1)}, u32[]{:S(2)}, u32[]{:S(2)}) async-start(bf16[32,128,128]{2,1,0:T(8,128)(2,1)} %pick.1), calls=%async_computation.4 | async-start | bytes 2097152 | tf_op jit(solution)/shard_map/all_to_all | solution.py:26
  241.5 11.8 %all-to-all-done.4 = bf16[32,128,128]{2,1,0:T(8,128)(2,1)} async-done(((bf16[32,128,128]{2,1,0:T(8,128)(2,1)}), bf16[32,128,128]{2,1,0:T(8,128)(2,1)}, u32[]{:S(2)}, u32[]{:S(2)}) %all-to-all-start.4) | async-done | bytes 1048608 | tf_op jit(solution)/shard_map/all_to_all | solution.py:26
  253.3 2.1 fusion.3
  (147 shorter events, 33.3 us)
Async XLA Ops:
  3.3 15.9 %collective-permute-start = (bf16[272,1024]{1,0:T(8,128)(2,1)}, bf16[272,1024]{1,0:T(8,128)(2,1)S(1)}, u32[]{:S(2)}, u32[]{:S(2)}) collective-permute-start(bf16[272,1024]{1,0:T(8,128)(2,1)} %slab_body.1.refs_0_), channel_id=1, source_target_pairs={{0,1},{1,0},{2,3},{3,2},{4,5},{5,4},{6,7},{7,6},{8,9},{9,8},{10,11... | collective-permute-start | bytes 1671176 | tf_op jit(solution)/shard_map/ppermute | solution.py:30
  6.4 16.6 %collective-permute-start.1 = (bf16[272,1024]{1,0:T(8,128)(2,1)}, bf16[272,1024]{1,0:T(8,128)(2,1)S(1)}, u32[]{:S(2)}, u32[]{:S(2)}) collective-permute-start(bf16[272,1024]{1,0:T(8,128)(2,1)} %slab_body.1.refs_0_), channel_id=1, source_target_pairs={{0,2},{2,4},{4,6},{6,0},{1,3},{3,5},{5,7},{7,1},{8,10},{10,12},{12... | collective-permute-start | bytes 1671176 | tf_op jit(solution)/shard_map/ppermute | solution.py:288
  8.3 14.7 %collective-permute-start.2 = (bf16[272,1024]{1,0:T(8,128)(2,1)}, bf16[272,1024]{1,0:T(8,128)(2,1)S(1)}, u32[]{:S(2)}, u32[]{:S(2)}) collective-permute-start(bf16[272,1024]{1,0:T(8,128)(2,1)} %slab_body.1.refs_0_), channel_id=1, source_target_pairs={{0,6},{2,0},{4,2},{6,4},{1,7},{3,1},{5,3},{7,5},{8,14},{10,8},{12,... | collective-permute-start | bytes 1671176 | tf_op jit(solution)/shard_map/ppermute | solution.py:289
  19.2 13.6 %copy-start.2 = (bf16[272,1024]{1,0:T(8,128)(2,1)}, bf16[272,1024]{1,0:T(8,128)(2,1)S(1)}, u32[]{:S(2)}) copy-start(bf16[272,1024]{1,0:T(8,128)(2,1)S(1)} %collective-permute-done.refs_1_) | copy-start | bytes 1671172
  23.0 9.8 %copy-start.4 = (bf16[272,1024]{1,0:T(8,128)(2,1)}, bf16[272,1024]{1,0:T(8,128)(2,1)S(1)}, u32[]{:S(2)}) copy-start(bf16[272,1024]{1,0:T(8,128)(2,1)S(1)} %collective-permute-done.1.refs_3_.refs_6_) | copy-start | bytes 1671172
  23.0 9.8 %copy-start.6 = (bf16[272,1024]{1,0:T(8,128)(2,1)}, bf16[272,1024]{1,0:T(8,128)(2,1)S(1)}, u32[]{:S(2)}) copy-start(bf16[272,1024]{1,0:T(8,128)(2,1)S(1)} %collective-permute-done.2.refs_2_) | copy-start | bytes 1671172
  23.0 9.8 %collective-permute-start.7 = (bf16[1024,1024]{1,0:T(8,128)(2,1)}, bf16[1024,1024]{1,0:T(8,128)(2,1)S(1)}, u32[]{:S(2)}, u32[]{:S(2)}) collective-permute-start(bf16[1024,1024]{1,0:T(8,128)(2,1)} %mask_body.3), channel_id=1, source_target_pairs={{0,8},{8,0},{1,9},{9,1},{2,10},{10,2},{3,11},{11,3},{4,12},{12,4},... | collective-permute-start | bytes 6291464 | tf_op jit(solution)/shard_map/ppermute | solution.py:30
  23.1 5.4 %collective-permute-start.3 = (bf16[272,1024]{1,0:T(8,128)(2,1)S(1)}, bf16[272,1024]{1,0:T(8,128)(2,1)S(1)}, u32[]{:S(2)}, u32[]{:S(2)}) collective-permute-start(bf16[272,1024]{1,0:T(8,128)(2,1)S(1)} %copy-done), channel_id=1, source_target_pairs={{0,8},{8,0},{1,9},{9,1},{2,10},{10,2},{3,11},{11,3},{4,12},{12,4},... | collective-permute-start | bytes 1671176 | tf_op jit(solution)/shard_map/ppermute | solution.py:30
  23.6 7.7 %collective-permute-start.4 = (bf16[272,1024]{1,0:T(8,128)(2,1)S(1)}, bf16[272,1024]{1,0:T(8,128)(2,1)}, u32[]{:S(2)}, u32[]{:S(2)}) collective-permute-start(bf16[272,1024]{1,0:T(8,128)(2,1)S(1)} %collective-permute-done.refs_1_), channel_id=1, source_target_pairs={{0,8},{8,0},{1,9},{9,1},{2,10},{10,2},{3,11},{11,3},{4,12},{12,4},... | collective-permute-start | bytes 1671176 | tf_op jit(solution)/shard_map/ppermute | solution.py:30
  23.7 7.6 %collective-permute-start.6 = (bf16[272,1024]{1,0:T(8,128)(2,1)S(1)}, bf16[272,1024]{1,0:T(8,128)(2,1)}, u32[]{:S(2)}, u32[]{:S(2)}) collective-permute-start(bf16[272,1024]{1,0:T(8,128)(2,1)S(1)} %collective-permute-done.1.refs_3_.refs_6_), channel_id=1, source_target_pairs={{0,8},{8,0},{1,9},{9,1},{2,10},{10,2},{3,11},{11,3},{4,12},{12,4},... | collective-permute-start | bytes 1671176 | tf_op jit(solution)/shard_map/ppermute | solution.py:30
  24.1 7.9 %collective-permute-start.5 = (bf16[272,1024]{1,0:T(8,128)(2,1)S(1)}, bf16[272,1024]{1,0:T(8,128)(2,1)S(1)}, u32[]{:S(2)}, u32[]{:S(2)}) collective-permute-start(bf16[272,1024]{1,0:T(8,128)(2,1)S(1)} %collective-permute-done.2.refs_2_), channel_id=1, source_target_pairs={{0,8},{8,0},{1,9},{9,1},{2,10},{10,2},{3,11},{11,3},{4,12},{12,4},... | collective-permute-start | bytes 1671176 | tf_op jit(solution)/shard_map/ppermute | solution.py:30
  28.5 15.3 %collective-permute-start.8 = (bf16[272,1024]{1,0:T(8,128)(2,1)S(1)}, bf16[272,1024]{1,0:T(8,128)(2,1)S(1)}, u32[]{:S(2)}, u32[]{:S(2)}) collective-permute-start(bf16[272,1024]{1,0:T(8,128)(2,1)S(1)} %collective-permute-done.refs_1_), channel_id=1, source_target_pairs={{0,6},{2,0},{4,2},{6,4},{1,7},{3,1},{5,3},{7,5},{8,14},{10,8},{12,... | collective-permute-start | bytes 1671176 | tf_op jit(solution)/shard_map/ppermute | solution.py:294
  31.3 22.4 %collective-permute-start.9 = (bf16[272,1024]{1,0:T(8,128)(2,1)S(1)}, bf16[272,1024]{1,0:T(8,128)(2,1)S(1)}, u32[]{:S(2)}, u32[]{:S(2)}) collective-permute-start(bf16[272,1024]{1,0:T(8,128)(2,1)S(1)} %collective-permute-done.1.refs_3_.refs_6_), channel_id=1, source_target_pairs={{0,2},{2,4},{4,6},{6,0},{1,3},{3,5},{5,7},{7,1},{8,10},{10,12},{12... | collective-permute-start | bytes 1671176 | tf_op jit(solution)/shard_map/ppermute | solution.py:295
  31.3 27.7 %collective-permute-start.10 = (bf16[272,1024]{1,0:T(8,128)(2,1)S(1)}, bf16[272,1024]{1,0:T(8,128)(2,1)S(1)}, u32[]{:S(2)}, u32[]{:S(2)}) collective-permute-start(bf16[272,1024]{1,0:T(8,128)(2,1)S(1)} %collective-permute-done.refs_1_), channel_id=1, source_target_pairs={{0,2},{2,4},{4,6},{6,0},{1,3},{3,5},{5,7},{7,1},{8,10},{10,12},{12... | collective-permute-start | bytes 1671176 | tf_op jit(solution)/shard_map/ppermute | solution.py:296
  43.7 15.4 %copy-start.8 = (bf16[272,1024]{1,0:T(8,128)(2,1)}, bf16[272,1024]{1,0:T(8,128)(2,1)S(1)}, u32[]{:S(2)}) copy-start(bf16[272,1024]{1,0:T(8,128)(2,1)S(1)} %collective-permute-done.8.refs_0_.refs_3_) | copy-start | bytes 1671172
  45.7 15.4 %collective-permute-start.11 = (bf16[272,1024]{1,0:T(8,128)(2,1)S(1)}, bf16[272,1024]{1,0:T(8,128)(2,1)S(1)}, u32[]{:S(2)}, u32[]{:S(2)}) collective-permute-start(bf16[272,1024]{1,0:T(8,128)(2,1)S(1)} %collective-permute-done.8.refs_0_.refs_3_), channel_id=1, source_target_pairs={{0,6},{2,0},{4,2},{6,4},{1,7},{3,1},{5,3},{7,5},{8,14},{10,8},{12,... | collective-permute-start | bytes 1671176 | tf_op jit(solution)/shard_map/ppermute | solution.py:306
  53.7 31.5 %all-to-all-start = ((f16[8,1040,128]{2,1,0:T(8,128)(2,1)}), f16[8,1040,128]{2,1,0:T(8,128)(2,1)}, u32[]{:S(2)}, u32[]{:S(2)}) async-start(f16[8,1040,128]{2,1,0:T(8,128)(2,1)} %select_convert_fusion.1), calls=%async_computation | async-start | bytes 4259840 | tf_op jit(solution)/shard_map/all_to_all | solution.py:26
  59.1 2.0 collective-permute-start.13
  59.1 2.7 %collective-permute-start.12 = (bf16[272,1024]{1,0:T(8,128)(2,1)S(1)}, bf16[272,1024]{1,0:T(8,128)(2,1)S(1)}, u32[]{:S(2)}, u32[]{:S(2)}) collective-permute-start(bf16[272,1024]{1,0:T(8,128)(2,1)S(1)} %collective-permute-done.8.refs_0_.refs_3_), channel_id=1, source_target_pairs={{0,8},{8,0},{1,9},{9,1},{2,10},{10,2},{3,11},{11,3},{4,12},{12,4},... | collective-permute-start | bytes 1671176 | tf_op jit(solution)/shard_map/ppermute | solution.py:30
  59.6 3.0 %collective-permute-start.14 = (bf16[272,1024]{1,0:T(8,128)(2,1)S(1)}, bf16[272,1024]{1,0:T(8,128)(2,1)S(1)}, u32[]{:S(2)}, u32[]{:S(2)}) collective-permute-start(bf16[272,1024]{1,0:T(8,128)(2,1)S(1)} %collective-permute-done.9.refs_2_.refs_4_), channel_id=1, source_target_pairs={{0,8},{8,0},{1,9},{9,1},{2,10},{10,2},{3,11},{11,3},{4,12},{12,4},... | collective-permute-start | bytes 1671176 | tf_op jit(solution)/shard_map/ppermute | solution.py:30
  61.1 2.3 collective-permute-start.15
  79.4 9.5 %copy-start.27 = (s32[2,8]{1,0:T(2,128)S(1)}, s32[2,8]{1,0:T(2,128)}, u32[]{:S(2)}) copy-start(s32[2,8]{1,0:T(2,128)} %param.12) | copy-start | bytes 196
  85.2 30.2 %all-to-all-start.1 = ((f16[8,1040,128]{2,1,0:T(8,128)(2,1)}), f16[8,1040,128]{2,1,0:T(8,128)(2,1)S(1)}, u32[]{:S(2)}, u32[]{:S(2)}) async-start(f16[8,1040,128]{2,1,0:T(8,128)(2,1)} %select_convert_fusion), calls=%async_computation.1 | async-start | bytes 4259840 | tf_op jit(solution)/shard_map/all_to_all | solution.py:26
  119.7 30.0 %all-to-all-start.2 = ((bf16[8,1024,128]{2,1,0:T(8,128)(2,1)}), bf16[8,1024,128]{2,1,0:T(8,128)(2,1)}, u32[]{:S(2)}, u32[]{:S(2)}) async-start(bf16[8,1024,128]{2,1,0:T(8,128)(2,1)} %broadcast_in_dim.90), calls=%async_computation.2 | async-start | bytes 4194304 | tf_op jit(solution)/shard_map/all_to_all | solution.py:26
  125.4 1.2 collective-permute-start.16
  126.7 5.1 %collective-permute-start.17 = (f32[8,128]{1,0:T(8,128)S(1)}, f32[8,128]{1,0:T(8,128)S(1)}, u32[]{:S(2)}, u32[]{:S(2)}) collective-permute-start(f32[8,128]{1,0:T(8,128)S(1)} %broadcast_maximum_fusion), channel_id=1, source_target_pairs={{0,4},{2,6},{4,0},{6,2},{1,5},{3,7},{5,1},{7,3},{8,12},{10,14},{12... | collective-permute-start | bytes 12296 | tf_op jit(solution)/shard_map/ppermute | solution.py:328
  131.8 4.8 %collective-permute-start.18 = (f32[8,128]{1,0:T(8,128)S(1)}, f32[8,128]{1,0:T(8,128)S(1)}, u32[]{:S(2)}, u32[]{:S(2)}) collective-permute-start(f32[8,128]{1,0:T(8,128)S(1)} %fusion.22), channel_id=1, source_target_pairs={{0,2},{2,4},{4,6},{6,0},{1,3},{3,5},{5,7},{7,1},{8,10},{10,12},{12... | collective-permute-start | bytes 12296 | tf_op jit(solution)/shard_map/ppermute | solution.py:329
  136.6 11.2 %collective-permute-start.19 = (f32[8,128]{1,0:T(8,128)S(1)}, f32[8,128]{1,0:T(8,128)S(1)}, u32[]{:S(2)}, u32[]{:S(2)}) collective-permute-start(f32[8,128]{1,0:T(8,128)S(1)} %max.33), channel_id=1, source_target_pairs={{0,1},{1,0},{2,3},{3,2},{4,5},{5,4},{6,7},{7,6},{8,9},{9,8},{10,11... | collective-permute-start | bytes 12296 | tf_op jit(solution)/shard_map/ppermute | solution.py:30
  149.7 4.5 %collective-permute-start.20 = (bf16[8,1024,128]{2,1,0:T(8,128)(2,1)}, bf16[8,1024,128]{2,1,0:T(8,128)(2,1)}, u32[]{:S(2)}, u32[]{:S(2)}) collective-permute-start(bf16[8,1024,128]{2,1,0:T(8,128)(2,1)} %all-to-all-done.2.mine), channel_id=1, source_target_pairs={{0,8},{8,0},{1,9},{9,1},{2,10},{10,2},{3,11},{11,3},{4,12},{12,4},... | collective-permute-start | bytes 6291464 | tf_op jit(solution)/shard_map/ppermute | solution.py:30
  149.7 31.9 %all-to-all-start.3 = ((bf16[8,1024,128]{2,1,0:T(8,128)(2,1)}), bf16[8,1024,128]{2,1,0:T(8,128)(2,1)S(1)}, u32[]{:S(2)}, u32[]{:S(2)}) async-start(bf16[8,1024,128]{2,1,0:T(8,128)(2,1)} %broadcast_in_dim.51), calls=%async_computation.3 | async-start | bytes 4194304 | tf_op jit(solution)/shard_map/all_to_all | solution.py:26
  163.1 18.6 %copy-start.1 = (bf16[272,1024]{1,0:T(8,128)(2,1)S(1)}, bf16[272,1024]{1,0:T(8,128)(2,1)}, u32[]{:S(2)}) copy-start(bf16[272,1024]{1,0:T(8,128)(2,1)} %slab_body.1.refs_0_) | copy-start | bytes 1671172
  163.1 18.6 %copy-start.28 = (s32[1,1,16,1]{2,3,1,0:T(1,128)S(1)}, s32[1,1,16,1]{2,3,1,0:T(1,128)}, u32[]{:S(2)}) copy-start(s32[1,1,16,1]{2,3,1,0:T(1,128)} %param.13) | copy-start | bytes 196
  166.0 15.6 %collective-permute-start.21 = (f16[256,1024]{1,0:T(8,128)(2,1)}, f16[256,1024]{1,0:T(8,128)(2,1)}, u32[]{:S(2)}, u32[]{:S(2)}) collective-permute-start(f16[256,1024]{1,0:T(8,128)(2,1)} %get-tuple-element.91), channel_id=1, source_target_pairs={{0,6},{2,0},{4,2},{6,4},{1,7},{3,1},{5,3},{7,5},{8,14},{10,8},{12,... | collective-permute-start | bytes 1572872 | tf_op jit(solution)/shard_map/ppermute | solution.py:338
  166.3 15.3 %collective-permute-start.22 = (f16[256,1024]{1,0:T(8,128)(2,1)}, f16[256,1024]{1,0:T(8,128)(2,1)S(1)}, u32[]{:S(2)}, u32[]{:S(2)}) collective-permute-start(f16[256,1024]{1,0:T(8,128)(2,1)} %get-tuple-element.90), channel_id=1, source_target_pairs={{0,2},{2,4},{4,6},{6,0},{1,3},{3,5},{5,7},{7,1},{8,10},{10,12},{12... | collective-permute-start | bytes 1572872 | tf_op jit(solution)/shard_map/ppermute | solution.py:338
  181.6 8.6 %collective-permute-start.23 = (bf16[8,1024,128]{2,1,0:T(8,128)(2,1)S(1)}, bf16[8,1024,128]{2,1,0:T(8,128)(2,1)}, u32[]{:S(2)}, u32[]{:S(2)}) collective-permute-start(bf16[8,1024,128]{2,1,0:T(8,128)(2,1)S(1)} %all-to-all-done.3.mine), channel_id=1, source_target_pairs={{0,8},{8,0},{1,9},{9,1},{2,10},{10,2},{3,11},{11,3},{4,12},{12,4},... | collective-permute-start | bytes 6291464 | tf_op jit(solution)/shard_map/ppermute | solution.py:30
  185.7 25.6 %collective-permute-start.24 = (f16[256,1024]{1,0:T(8,128)(2,1)}, f16[256,1024]{1,0:T(8,128)(2,1)}, u32[]{:S(2)}, u32[]{:S(2)}) collective-permute-start(f16[256,1024]{1,0:T(8,128)(2,1)} %get-tuple-element.84), channel_id=1, source_target_pairs={{0,7},{1,6},{2,1},{3,0},{4,3},{5,2},{6,5},{7,4},{8,15},{9,14},{10,... | collective-permute-start | bytes 1572872 | tf_op jit(solution)/shard_map/ppermute | solution.py:43
  188.2 25.3 %collective-permute-start.25 = (f16[256,1024]{1,0:T(8,128)(2,1)}, f16[256,1024]{1,0:T(8,128)(2,1)}, u32[]{:S(2)}, u32[]{:S(2)}) collective-permute-start(f16[256,1024]{1,0:T(8,128)(2,1)} %get-tuple-element.85), channel_id=1, source_target_pairs={{0,3},{1,2},{2,5},{3,4},{4,7},{5,6},{6,1},{7,0},{8,11},{9,10},{10,... | collective-permute-start | bytes 1572872 | tf_op jit(solution)/shard_map/ppermute | solution.py:43
  199.0 10.4 %copy-start.3 = (bf16[272,1024]{1,0:T(8,128)(2,1)S(1)}, bf16[272,1024]{1,0:T(8,128)(2,1)}, u32[]{:S(2)}) copy-start(bf16[272,1024]{1,0:T(8,128)(2,1)} %copy-done.2) | copy-start | bytes 1671172
  199.0 10.4 %copy-start.5 = (bf16[272,1024]{1,0:T(8,128)(2,1)S(1)}, bf16[272,1024]{1,0:T(8,128)(2,1)}, u32[]{:S(2)}) copy-start(bf16[272,1024]{1,0:T(8,128)(2,1)} %copy-done.4) | copy-start | bytes 1671172
  199.0 10.5 %copy-start.7 = (bf16[272,1024]{1,0:T(8,128)(2,1)S(1)}, bf16[272,1024]{1,0:T(8,128)(2,1)}, u32[]{:S(2)}) copy-start(bf16[272,1024]{1,0:T(8,128)(2,1)} %copy-done.6) | copy-start | bytes 1671172
  199.0 11.2 %copy-start.9 = (bf16[272,1024]{1,0:T(8,128)(2,1)S(1)}, bf16[272,1024]{1,0:T(8,128)(2,1)}, u32[]{:S(2)}) copy-start(bf16[272,1024]{1,0:T(8,128)(2,1)} %copy-done.8) | copy-start | bytes 1671172
  199.1 11.1 %copy-start.11 = (bf16[272,1024]{1,0:T(8,128)(2,1)S(1)}, bf16[272,1024]{1,0:T(8,128)(2,1)}, u32[]{:S(2)}) copy-start(bf16[272,1024]{1,0:T(8,128)(2,1)} %copy-done.10) | copy-start | bytes 1671172
  203.5 20.6 %collective-permute-start.26 = (f16[256,1024]{1,0:T(8,128)(2,1)}, f16[256,1024]{1,0:T(8,128)(2,1)}, u32[]{:S(2)}, u32[]{:S(2)}) collective-permute-start(f16[256,1024]{1,0:T(8,128)(2,1)} %get-tuple-element.64), channel_id=1, source_target_pairs={{0,1},{1,0},{2,3},{3,2},{4,5},{5,4},{6,7},{7,6},{8,9},{9,8},{10,11... | collective-permute-start | bytes 1572872 | tf_op jit(solution)/shard_map/ppermute | solution.py:43
  206.2 18.1 %collective-permute-start.27 = (f16[256,1024]{1,0:T(8,128)(2,1)}, f16[256,1024]{1,0:T(8,128)(2,1)}, u32[]{:S(2)}, u32[]{:S(2)}) collective-permute-start(f16[256,1024]{1,0:T(8,128)(2,1)} %get-tuple-element.65), channel_id=1, source_target_pairs={{0,2},{1,3},{2,4},{3,5},{4,6},{5,7},{6,0},{7,1},{8,10},{9,11},{10,... | collective-permute-start | bytes 1572872 | tf_op jit(solution)/shard_map/ppermute | solution.py:43
  206.3 17.9 %collective-permute-start.28 = (f16[256,1024]{1,0:T(8,128)(2,1)}, f16[256,1024]{1,0:T(8,128)(2,1)}, u32[]{:S(2)}, u32[]{:S(2)}) collective-permute-start(f16[256,1024]{1,0:T(8,128)(2,1)} %get-tuple-element.66), channel_id=1, source_target_pairs={{0,6},{1,7},{2,0},{3,1},{4,2},{5,3},{6,4},{7,5},{8,14},{9,15},{10,... | collective-permute-start | bytes 1572872 | tf_op jit(solution)/shard_map/ppermute | solution.py:43
  211.3 13.0 %copy-start.18 = (f32[32,8,8,128]{3,1,2,0:T(8,128)S(1)}, f32[32,8,8,128]{3,1,2,0:T(8,128)}, u32[]{:S(2)}) copy-start(f32[32,8,8,128]{3,1,2,0:T(8,128)} %copy.19) | copy-start | bytes 3145732
  229.3 24.0 %all-to-all-start.4 = ((bf16[32,128,128]{2,1,0:T(8,128)(2,1)}), bf16[32,128,128]{2,1,0:T(8,128)(2,1)}, u32[]{:S(2)}, u32[]{:S(2)}) async-start(bf16[32,128,128]{2,1,0:T(8,128)(2,1)} %pick.1), calls=%async_computation.4 | async-start | bytes 2097152 | tf_op jit(solution)/shard_map/all_to_all | solution.py:26
  240.6 12.6 %copy-start.20 = (bf16[1,1,3,32,128,128]{5,4,3,2,1,0:T(8,128)(2,1)S(1)}, bf16[1,1,3,32,128,128]{5,4,3,2,1,0:T(8,128)(2,1)}, u32[]{:S(2)}) copy-start(bf16[1,1,3,32,128,128]{5,4,3,2,1,0:T(8,128)(2,1)} %param.14) | copy-start | bytes 9437188
  (15 other events, 45.5 us)
